TPU v7x, 512 devices: a whole 4x8x8 slice. The times are simulated.
512 devices in a mesh: state: 8 (over y), mode: 64 (over z, x, core).
Axes of the slice: x: 4, y: 8, z: 8, core: 2. Of those that a mesh axis runs over, the one named last changes fastest.
Arguments:
- coeffs: float32 [8, 512, 4096], P('state', 'mode'), may hold values from -0.375 to 0.375
- diag_h2: float32 [8, 32, 4096], P('state'), may hold values from -0.75 to 0.75
- diag_h3: float32 [8, 32, 4096], P('state'), may hold values from -0.75 to 0.75
- diag_v1: float32 [8, 32, 512], P('state', None, 'mode'), may hold values from -1.5 to 1.5
- coup_h2: float32 [32, 4096], replicated, may hold values from -0.75 to 0.75
- coup_h3: float32 [32, 4096], replicated, may hold values from -0.75 to 0.75
- coup_v1: float32 [32, 512], P(None, 'mode'), may hold values from -1.5 to 1.5
- pairs: int32 [128, 3], replicated, may hold values from 0 to 31, as said below
Outputs:
- action: float32 [8, 512, 4096], P('state', 'mode')
- diag_field: float32 [8, 64, 2048], P('state', 'mode')
- pair_field: float32 [8, 64, 3072], P('state', 'mode')
Inputs may be any that keep to these rules, and one draw needn't show every extreme that they name: `pairs`: each row is (target state, source state, coupling term); the source differs from the target; every state is the target of at most 48 rows, and one state of exactly 48.
All inputs are finite; a program needn't handle non-finite values.
Results may differ from a plain program's by a relative error of at most 0.0001.
Values sent between devices are 32-bit elements; how exact they have to be, the bound alone decides.
No kernel may reach another device: no remote copies, remote signals or barrier semaphores. Data moves between devices by JAX's collectives and lax.ppermute only.
A program may use at most 64 MiB of HBM per device.

v0:
```python
import jax
import jax.numpy as jnp
from jax import lax
from jax.experimental import pallas as pl
from jax.experimental.pallas import tpu as pltpu
from jax.sharding import Mesh, PartitionSpec as P

N = 64
G = 8
TERMS = 32
STATES = 8
SLOTS = 48
F32 = jnp.float32
BF16 = jnp.bfloat16
NT = (((1,), (1,)), ((), ()))
VMEM = pl.BlockSpec(memory_space=pltpu.VMEM)
SMEM = pl.BlockSpec(memory_space=pltpu.SMEM)


def dot(left, right):
    return jnp.dot(left, right, preferred_element_type=F32)


def dot_nt(left, right):
    return lax.dot_general(left, right, NT, preferred_element_type=F32)


def split(value):
    high = value.astype(BF16)
    low = (value - high.astype(F32)).astype(BF16)
    return high, low


def split_lanes(value):
    return jnp.concatenate(split(value), axis=1)


def half_blocks(operator):
    left = lax.broadcasted_iota(jnp.int32, operator.shape, 1) < N
    high = operator.astype(BF16).astype(F32)
    low = operator - high
    zero = jnp.zeros_like(operator)
    return [
        jnp.where(left, high, zero).astype(BF16),
        jnp.where(left, zero, high).astype(BF16),
        jnp.where(left, low, zero).astype(BF16),
        jnp.where(left, zero, low).astype(BF16),
    ]


def tile_nt(operator):
    h0, h1, l0, l1 = half_blocks(operator)
    zero = jnp.zeros((2 * N, 2 * N), BF16)
    high = jnp.concatenate([h0, h1], axis=0)
    low = jnp.concatenate([l0, l1], axis=0)
    return jnp.concatenate(
        [jnp.concatenate([high, low], axis=0), jnp.concatenate([high, zero], axis=0)], axis=1
    )


def tile_nn(operator):
    h0, h1, l0, l1 = half_blocks(operator)
    zero = jnp.zeros((2 * N, 2 * N), BF16)
    high = jnp.concatenate([h0, h1], axis=0)
    low = jnp.concatenate([l0, l1], axis=0)
    return jnp.concatenate(
        [jnp.concatenate([high, low], axis=1), jnp.concatenate([high, zero], axis=1)], axis=0
    )


def put_term(product, weight, index, high_ref, low_ref):
    value = product[:, : 2 * N] + product[:, 2 * N :]
    rows = pl.ds(pl.multiple_of(index * N, N), N)
    for pair in range(G // 2):
        part = value[pair * N : (pair + 1) * N] * weight[pair : pair + 1]
        high, low = split(part)
        high_ref[rows, pair * 2 * N : (pair + 1) * 2 * N] = high
        low_ref[rows, pair * 2 * N : (pair + 1) * 2 * N] = low


def act_on(left_ref, high_ref, low_ref):
    high, low = split(left_ref[...])
    both = dot(jnp.concatenate([high, low], axis=0), high_ref[...])
    return both[:N] + both[N:] + dot(high, low_ref[...])


def own_kernel(a_ref, ap_ref, h3_ref, h2_ref, v_ref, c3_ref, cv_ref,
               act_ref, mine_ref, other_ref, zh_ref, zl_ref, wh_ref, wl_ref):
    left = split_lanes(a_ref[...])

    def own_term(t, carry):
        put_term(dot_nt(left, tile_nt(h3_ref[t])), v_ref[t], t, wh_ref, wl_ref)
        return carry

    lax.fori_loop(0, TERMS, own_term, 0)
    act_ref[...] = act_on(h2_ref, wh_ref, wl_ref)

    wide = jnp.concatenate([ap_ref[p * N : (p + 1) * N, :] for p in range(G // 2)], axis=1)
    high, low = split(wide)
    rows_both = jnp.concatenate([high, low], axis=0)
    for j in range(TERMS // 4):
        part = slice(j * 4 * N, (j + 1) * 4 * N)
        both = dot_nt(rows_both, wh_ref[part, :])
        field = both[:N] + both[N:] + dot_nt(high, wl_ref[part, :])
        for half in range(2):
            lanes = slice(half * 2 * N, (half + 1) * 2 * N)
            where_to = pl.ds(2 * j + half, N // 2, stride=TERMS // 2)
            mine_ref[where_to, :] = field[: N // 2, lanes]
            other_ref[where_to, :] = field[N // 2 :, lanes]

    left_p = split_lanes(ap_ref[...])

    def coupling_term(k, carry):
        put_term(dot(left_p, tile_nn(c3_ref[k])), cv_ref[k], k, zh_ref, zl_ref)
        return carry

    lax.fori_loop(0, TERMS, coupling_term, 0)


def field_kernel(source_ref, term_ref, valid_ref, all_ref, zh_ref, zl_ref,
                 mine_ref, other_ref, gh_ref, gl_ref, f_ref):
    for q in range(STATES):
        for pair in range(G // 2):
            high, low = split(all_ref[q, pair * N : (pair + 1) * N, :])
            lanes = slice(pair * 2 * N, (pair + 1) * 2 * N)
            gh_ref[q * N : (q + 1) * N, lanes] = high
            gl_ref[q * N : (q + 1) * N, lanes] = low

    def block(j, carry):
        rows = pl.ds(pl.multiple_of(j * 4 * N, 4 * N), 4 * N)
        zh = zh_ref[rows, :]
        left = jnp.concatenate([zh, zl_ref[rows, :], zh], axis=1)
        for half in range(2):
            here = slice(half * 4 * N, (half + 1) * 4 * N)
            gh = gh_ref[here, :]
            right = jnp.concatenate([gh, gh, gl_ref[here, :]], axis=1)
            product = dot_nt(left, right)
            f_ref[2 * half, rows, :] = product[:, : 2 * N]
            f_ref[2 * half + 1, rows, :] = product[:, 2 * N :]
        return carry

    lax.fori_loop(0, TERMS // 4, block, 0)
    is_left = lax.broadcasted_iota(jnp.int32, (N, 2 * N), 1) < N

    def pick(slot):
        source = source_ref[slot]
        rows = pl.ds(pl.multiple_of(term_ref[slot] * N, N), N)
        return f_ref[source // 2, rows, :], lax.rem(source, 2)

    def slot_pair(i, carry):
        first, odd_first = pick(2 * i)
        second, odd_second = pick(2 * i + 1)
        first = jnp.where(odd_first == 1, pltpu.roll(first, N, 1), first)
        second = jnp.where(odd_second == 0, pltpu.roll(second, N, 1), second)
        first = jnp.where(valid_ref[2 * i] == 1, first, 0.0)
        second = jnp.where(valid_ref[2 * i + 1] == 1, second, 0.0)
        field = jnp.where(is_left, first, second)
        where_to = pl.ds(i, N // 2, stride=SLOTS // 2)
        mine_ref[where_to, :] = field[: N // 2]
        other_ref[where_to, :] = field[N // 2 :]
        return carry

    lax.fori_loop(0, SLOTS // 2, slot_pair, 0)


def pair_kernel(count_ref, all_ref, c3_ref, c2_ref, cv_ref, act_ref, out_ref, wh_ref, wl_ref):
    def coupling_term(k, carry):
        total = all_ref[0] * count_ref[k, 0]
        for q in range(1, STATES):
            total = total + all_ref[q] * count_ref[k, q]
        put_term(dot_nt(split_lanes(total), tile_nt(c3_ref[k])), cv_ref[k], k, wh_ref, wl_ref)
        return carry

    lax.fori_loop(0, TERMS, coupling_term, 0)
    out_ref[...] = act_ref[...] + act_on(c2_ref, wh_ref, wl_ref)


def cost(flops, nbytes):
    return pl.CostEstimate(flops=flops, bytes_accessed=nbytes, transcendentals=0)


def own_part(a2, a2p, h3, h2, v, c3, cv):
    return pl.pallas_call(
        own_kernel,
        out_shape=(
            jax.ShapeDtypeStruct((N, G * N), F32),
            jax.ShapeDtypeStruct((N // 2 * TERMS // 2, 2 * N), F32),
            jax.ShapeDtypeStruct((N // 2 * TERMS // 2, 2 * N), F32),
            jax.ShapeDtypeStruct((TERMS * N, G * N), BF16),
            jax.ShapeDtypeStruct((TERMS * N, G * N), BF16),
        ),
        in_specs=[VMEM] * 7,
        out_specs=[VMEM] * 5,
        scratch_shapes=[pltpu.VMEM((TERMS * N, G * N), BF16)] * 2,
        compiler_params=pltpu.CompilerParams(vmem_limit_bytes=28 << 20),
        cost_estimate=cost(3_000_000_000, 8 << 20),
        name="own_part",
    )(a2, a2p, h3, h2, v, c3, cv)


def pair_fields(source, term, valid, everyone, zh, zl):
    rows = N // 2 * SLOTS // 2
    return pl.pallas_call(
        field_kernel,
        out_shape=(
            jax.ShapeDtypeStruct((rows, 2 * N), F32),
            jax.ShapeDtypeStruct((rows, 2 * N), F32),
        ),
        in_specs=[SMEM] * 3 + [VMEM] * 3,
        out_specs=[VMEM] * 2,
        scratch_shapes=[
            pltpu.VMEM((STATES * N, G * N), BF16),
            pltpu.VMEM((STATES * N, G * N), BF16),
            pltpu.VMEM((STATES // 2, TERMS * N, 2 * N), F32),
        ],
        compiler_params=pltpu.CompilerParams(vmem_limit_bytes=28 << 20),
        cost_estimate=cost(3_000_000_000, 6 << 20),
        name="pair_fields",
    )(source, term, valid, everyone, zh, zl)


def pair_action(count, everyone, c3, c2, cv, act):
    return pl.pallas_call(
        pair_kernel,
        out_shape=jax.ShapeDtypeStruct((N, G * N), F32),
        in_specs=[SMEM] + [VMEM] * 5,
        out_specs=VMEM,
        scratch_shapes=[pltpu.VMEM((TERMS * N, G * N), BF16)] * 2,
        compiler_params=pltpu.CompilerParams(vmem_limit_bytes=28 << 20),
        cost_estimate=cost(3_000_000_000, 4 << 20),
        name="pair_action",
    )(count, everyone, c3, c2, cv, act)


def twice(flat):
    matrices = flat.reshape(TERMS, N, N)
    return jnp.concatenate([matrices, matrices], axis=2)


def rows_by_term(flat):
    return flat.reshape(TERMS, N, N).transpose(1, 0, 2).reshape(N, TERMS * N)


def lane_weights(v):
    return jnp.repeat(v, N, axis=1).reshape(TERMS, G // 2, 2 * N)


def arrange(coeffs, core):
    tensor = coeffs.reshape(G // 2, 2, N, N)
    plain = tensor.transpose(0, 2, 1, 3).reshape(G // 2 * N, 2 * N)
    rows = plain.reshape(G // 2, N // 2, 2, 2 * N)
    even, odd = rows[:, :, 0], rows[:, :, 1]
    first = jnp.where(core == 0, even, odd)
    second = jnp.where(core == 0, odd, even)
    return plain, jnp.concatenate([first, second], axis=1).reshape(G // 2 * N, 2 * N)


def read_list(pairs, myself):
    is_mine = pairs[:, 0] == myself
    rank = jnp.cumsum(is_mine.astype(jnp.int32)) - 1
    slots = jnp.arange(SLOTS, dtype=jnp.int32)
    picked = (rank[None, :] == slots[:, None]) & is_mine[None, :]
    source = jnp.sum(jnp.where(picked, pairs[None, :, 1], 0), axis=1)
    term = jnp.sum(jnp.where(picked, pairs[None, :, 2], 0), axis=1)
    valid = jnp.sum(picked.astype(jnp.int32), axis=1)
    by_term = (pairs[None, :, 2] == jnp.arange(TERMS, dtype=jnp.int32)[:, None]) & is_mine[None, :]
    by_source = pairs[None, :, 1] == jnp.arange(STATES, dtype=jnp.int32)[:, None]
    count = jnp.sum((by_term[:, None, :] & by_source[None, :, :]).astype(F32), axis=2)
    return source, term, valid, count


def per_device(coeffs, diag_h2, diag_h3, diag_v1, coup_h2, coup_h3, coup_v1, pairs):
    core = lax.axis_index("core")
    plain, mine_first = arrange(coeffs[0], core)
    everyone = lax.all_to_all(
        jnp.broadcast_to(plain[None], (STATES,) + plain.shape), "state", 0, 0, tiled=True
    )
    source, term, valid, count = read_list(pairs, lax.axis_index("state"))
    c3 = twice(coup_h3)
    cv = lane_weights(coup_v1)
    act, diag_mine, diag_other, zh, zl = own_part(
        plain, mine_first, twice(diag_h3[0]), rows_by_term(diag_h2[0]),
        lane_weights(diag_v1[0]), c3, cv,
    )
    swap = [(0, 1), (1, 0)]
    diag_sum = diag_mine + lax.ppermute(diag_other, "core", swap)
    pair_mine, pair_other = pair_fields(source, term, valid, everyone, zh, zl)
    pair_sum = pair_mine + lax.ppermute(pair_other, "core", swap)
    sums = jnp.concatenate(
        [diag_sum.reshape(N // 2, TERMS // 2, 2 * N), pair_sum.reshape(N // 2, SLOTS // 2, 2 * N)],
        axis=1,
    )
    parts = lax.all_to_all(sums, ("z", "x"), 0, 0, tiled=True)
    act = pair_action(count, everyone, c3, rows_by_term(coup_h2), cv, act)
    action = act.reshape(N, G, N).transpose(1, 0, 2).reshape(1, G, N * N)
    row = jnp.sum(parts, axis=0)
    diag_row = row[: TERMS // 2].reshape(1, 1, TERMS * N)
    pair_row = row[TERMS // 2 :].reshape(1, 1, SLOTS * N)
    return action, diag_row, pair_row


def solution(mesh):
    devices = mesh.devices
    fine = Mesh(devices.reshape(8, 8, 4, 2), ("state", "z", "x", "core"))
    mode = ("z", "x", "core")
    placed = (
        P("state", mode, None),
        P("state", None, None),
        P("state", None, None),
        P("state", None, mode),
        P(),
        P(),
        P(None, mode),
        P(),
    )
    out = P("state", mode, None)
    return jax.shard_map(
        per_device, mesh=fine, in_specs=placed, out_specs=(out, out, out), check_vma=False
    )
```

profile of v0, /device:TPU:8, one launch (start us, length us, event | category | flops | bytes accessed | tf_op | source)
XLA Modules:
  0.0 93.7 jit_solution(2687106712285885723)
XLA Ops:
  0.6 1.0 %reshape_squeeze.9 = f32[4,2,64,64]{3,2,1,0:T(8,128)S(1)} reshape(f32[1,8,4096]{2,1,0:T(8,128)} %param.8) | data formatting | bytes 262144 | tf_op jit(solution)/shard_map/reshape;squeeze | solution.py:249
  2.0 1.0 %broadcast_in_dim.40 = f32[8,256,128]{2,1,0:T(8,128)} broadcast(f32[256,128]{1,0:T(8,128)S(1)} %broadcast_in_dim.39.a_ref), dimensions={1,2} | broadcast | bytes 1179648 | tf_op jit(solution)/shard_map/broadcast_in_dim | solution.py:276
  3.1 9.4 %all-to-all-start = ((f32[8,256,128]{2,1,0:T(8,128)}), f32[8,256,128]{2,1,0:T(8,128)S(1)}, u32[]{:S(2)}, u32[]{:S(2)}) async-start(f32[8,256,128]{2,1,0:T(8,128)} %broadcast_in_dim.40), calls=%async_computation | async-start | bytes 2097152 | tf_op jit(solution)/shard_map/all_to_all | solution.py:275
  12.8 1.4 %reshape.130 = f32[32,64,64]{2,1,0:T(8,128)} reshape(f32[32,4096]{1,0:T(8,128)S(1)} %copy-done.5) | data formatting | bytes 1048576 | tf_op jit(solution)/shard_map/reshape | solution.py:236
  14.4 1.5 %reshape_squeeze.11 = f32[32,64,64]{2,1,0:T(8,128)S(1)} reshape(f32[1,32,4096]{2,1,0:T(8,128)} %param.9) | data formatting | bytes 1048576 | tf_op jit(solution)/shard_map/reshape;squeeze | solution.py:241
  16.9 2.5 %reshape_squeeze.10 = f32[32,64,64]{2,1,0:T(8,128)} reshape(f32[1,32,4096]{2,1,0:T(8,128)} %param.10) | data formatting | bytes 1048576 | tf_op jit(solution)/shard_map/reshape;squeeze | solution.py:236
  20.4 1.9 %pad_maximum_fusion.c3_ref = f32[32,64,128]{2,1,0:T(8,128)S(1)} fusion(f32[32,64,64]{2,1,0:T(8,128)} %reshape.130), kind=kLoop, calls=%fused_computation | loop fusion | flops 262144 | bytes 1572864 | tf_op jit(solution)/shard_map/concatenate | solution.py:237
  22.7 16.0 %own_part.1 = (f32[64,512]{1,0:T(8,128)S(1)}, f32[512,128]{1,0:T(8,128)S(1)}, f32[512,128]{1,0:T(8,128)S(1)}, bf16[2048,512]{1,0:T(8,128)(2,1)S(1)}, bf16[2048,512]{1,0:T(8,128)(2,1)S(1)}) custom-call(f32[256,128]{1,0:T(8,128)S(1)} %broadcast_in_dim.39.a_ref, f32[256,128]{1,0:T(8,128)S(1)} %bitcast.29, f32[32,64,128]{2,1,0:T(8,128)S(1)} %pad_maximum_fusion.1.h3_ref, ...), custom_call_target="tpu_custom_call" | custom-call | flops 3000000000 | bytes 8388608 | tf_op jit(solution)/shard_map/own_part/pallas_call | solution.py:183
  38.8 1.3 %copy-done = bf16[2048,512]{1,0:T(8,128)(2,1)} copy-done((bf16[2048,512]{1,0:T(8,128)(2,1)}, bf16[2048,512]{1,0:T(8,128)(2,1)S(1)}, u32[]{:S(2)}) %copy-start) | copy-done | bytes 2097176
  40.1 1.3 %copy-done.2 = bf16[2048,512]{1,0:T(8,128)(2,1)} copy-done((bf16[2048,512]{1,0:T(8,128)(2,1)}, bf16[2048,512]{1,0:T(8,128)(2,1)S(1)}, u32[]{:S(2)}) %copy-start.2) | copy-done | bytes 2097176
  41.4 1.6 %copy-done.1 = bf16[2048,512]{1,0:T(8,128)(2,1)S(1)} copy-done((bf16[2048,512]{1,0:T(8,128)(2,1)S(1)}, bf16[2048,512]{1,0:T(8,128)(2,1)}, u32[]{:S(2)}) %copy-start.1) | copy-done | bytes 2097176
  43.0 1.6 %copy-done.3 = bf16[2048,512]{1,0:T(8,128)(2,1)S(1)} copy-done((bf16[2048,512]{1,0:T(8,128)(2,1)S(1)}, bf16[2048,512]{1,0:T(8,128)(2,1)}, u32[]{:S(2)}) %copy-start.3) | copy-done | bytes 2097176
  44.6 7.7 %pair_fields.1 = (f32[768,128]{1,0:T(8,128)S(1)}, f32[768,128]{1,0:T(8,128)S(1)}) custom-call(s32[48]{0:T(128)S(1)} %get-tuple-element.19.source_ref, s32[48]{0:T(128)S(1)} %get-tuple-element.18.term_ref, s32[48]{0:T(128)S(1)} %get-tuple-element.17.valid_ref, f32[8,256,128]{2,1,0:T(8,128)S(1)} %all-to-all-done.all_ref, bf16[2048,512]{1,0:T(8,128)(2,1)S(1)} %copy-done.1, ...), custom_call_target="tpu_custom_call" | custom-call | flops 3000000000 | bytes 6291456 | tf_op jit(solution)/shard_map/pair_fields/pallas_call | solution.py:203
  52.3 1.9 %collective-permute-start.1 = (f32[768,128]{1,0:T(8,128)S(1)}, f32[768,128]{1,0:T(8,128)S(1)}, u32[]{:S(2)}, u32[]{:S(2)}) collective-permute-start(f32[768,128]{1,0:T(8,128)S(1)} %get-tuple-element.16), channel_id=1, source_target_pairs={{0,1},{1,0},{2,3},{3,2},{4,5},{5,4},{6,7},{7,6},{8,9},{9,8},{10,11... | collective-permute-start | bytes 1179656 | tf_op jit(solution)/shard_map/ppermute | solution.py:288
  54.2 2.4 %collective-permute-start = (f32[512,128]{1,0:T(8,128)S(1)}, f32[512,128]{1,0:T(8,128)S(1)}, u32[]{:S(2)}, u32[]{:S(2)}) collective-permute-start(f32[512,128]{1,0:T(8,128)S(1)} %get-tuple-element.12), channel_id=1, source_target_pairs={{0,1},{1,0},{2,3},{3,2},{4,5},{5,4},{6,7},{7,6},{8,9},{9,8},{10,11... | collective-permute-start | bytes 786440 | tf_op jit(solution)/shard_map/ppermute | solution.py:286
  56.7 1.1 %collective-permute-done = f32[512,128]{1,0:T(8,128)S(1)} collective-permute-done((f32[512,128]{1,0:T(8,128)S(1)}, f32[512,128]{1,0:T(8,128)S(1)}, u32[]{:S(2)}, u32[]{:S(2)}) %collective-permute-start) | collective-permute-done | bytes 262176 | tf_op jit(solution)/shard_map/ppermute | solution.py:286
  57.9 0.9 pad_maximum_fusion.2
  58.8 11.6 %all-to-all-start.1 = ((f32[32,40,128]{2,1,0:T(8,128)}), f32[32,40,128]{2,1,0:T(8,128)}, u32[]{:S(2)}, u32[]{:S(2)}) async-start(f32[32,40,128]{2,1,0:T(8,128)} %pad_maximum_fusion.2), calls=%async_computation.1 | async-start | bytes 1310720 | tf_op jit(solution)/shard_map/all_to_all | solution.py:293
  70.4 1.4 %reshape.131 = f32[32,64,64]{2,1,0:T(8,128)} reshape(f32[32,4096]{1,0:T(8,128)S(1)} %copy-done.6) | data formatting | bytes 1048576 | tf_op jit(solution)/shard_map/reshape | solution.py:241
  71.8 2.9 %copy.45 = f32[32,64,64]{2,0,1:T(8,128)} copy(f32[32,64,64]{2,1,0:T(8,128)} %reshape.131) | data formatting | bytes 1048576 | tf_op jit(solution)/shard_map/reshape | solution.py:241
  74.7 1.6 %reshape.132.c2_ref = f32[64,2048]{1,0:T(8,128)S(1)} reshape(f32[64,32,64]{2,1,0:T(8,128)} %bitcast.31) | data formatting | bytes 1048576 | tf_op jit(solution)/shard_map/reshape | solution.py:241
  76.4 9.2 %pair_action.1 = f32[64,512]{1,0:T(8,128)S(1)} custom-call(f32[32,8]{1,0:T(8,128)S(1)} %convert_reduce_fusion.count_ref, f32[8,256,128]{2,1,0:T(8,128)S(1)} %all-to-all-done.all_ref, f32[32,64,128]{2,1,0:T(8,128)S(1)} %pad_maximum_fusion.c3_ref, f32[64,2048]{1,0:T(8,128)S(1)} %reshape.132.c2_ref, f32[32,4,128]{2,1,0:T(4,128)S(1)} %reshape_reshape.9.cv_ref, ...), custom_call_target="tpu_custom_call" | custom-call | flops 3000000000 | bytes 4194304 | tf_op jit(solution)/shard_map/pair_action/pallas_call | solution.py:223
  86.5 4.8 %all-to-all-done.1 = f32[32,40,128]{2,1,0:T(8,128)} async-done(((f32[32,40,128]{2,1,0:T(8,128)}), f32[32,40,128]{2,1,0:T(8,128)}, u32[]{:S(2)}, u32[]{:S(2)}) %all-to-all-start.1) | async-done | bytes 655392 | tf_op jit(solution)/shard_map/all_to_all | solution.py:293
  91.3 1.1 %reduce_sum.49 = f32[40,128]{1,0:T(8,128)S(1)} reduce(f32[32,40,128]{2,1,0:T(8,128)} %all-to-all-done.1, f32[]{:T(128)} %constant.16.clone.1), dimensions={0}, to_apply=%region_5.6 | reduce | flops 158720 | bytes 675844 | tf_op jit(solution)/shard_map/reduce_sum | solution.py:296
  (57 shorter events, 5.6 us)
Async XLA Ops:
  1.9 10.9 %copy-start.5 = (f32[32,4096]{1,0:T(8,128)S(1)}, f32[32,4096]{1,0:T(8,128)}, u32[]{:S(2)}) copy-start(f32[32,4096]{1,0:T(8,128)} %param.13) | copy-start | bytes 1572868
  3.1 11.1 %copy-start.9 = (f32[32,8]{0,1:T(8,128)S(1)}, f32[32,8]{0,1:T(8,128)}, u32[]{:S(2)}) copy-start(f32[32,8]{0,1:T(8,128)} %param.14) | copy-start | bytes 3076
  3.1 38.3 %all-to-all-start = ((f32[8,256,128]{2,1,0:T(8,128)}), f32[8,256,128]{2,1,0:T(8,128)S(1)}, u32[]{:S(2)}, u32[]{:S(2)}) async-start(f32[8,256,128]{2,1,0:T(8,128)} %broadcast_in_dim.40), calls=%async_computation | async-start | bytes 2097152 | tf_op jit(solution)/shard_map/all_to_all | solution.py:275
  16.5 2.9 %copy-start.10 = (f32[1,32,8]{1,2,0:T(8,128)S(1)}, f32[1,32,8]{1,2,0:T(8,128)}, u32[]{:S(2)}) copy-start(f32[1,32,8]{1,2,0:T(8,128)} %param.11) | copy-start | bytes 3076
  16.5 3.1 %copy-start.13 = (s32[128,3]{0,1:T(4,128)S(1)}, s32[128,3]{0,1:T(4,128)}, u32[]{:S(2)}) copy-start(s32[128,3]{0,1:T(4,128)} %param.15) | copy-start | bytes 4612
  20.0 2.4 %copy-start.4 = (f32[32,64,64]{2,1,0:T(8,128)S(1)}, f32[32,64,64]{2,1,0:T(8,128)}, u32[]{:S(2)}) copy-start(f32[32,64,64]{2,1,0:T(8,128)} %reshape_squeeze.10) | copy-start | bytes 1572868
  20.1 2.6 %copy-start.7 = (s32[128]{0:T(128)}, s32[128]{0:T(128)S(1)}, u32[]{:S(2)}) copy-start(s32[128]{0:T(128)S(1)} %get-tuple-element.25) | copy-start | bytes 1540
  20.1 2.6 %copy-start.11 = (s32[128]{0:T(128)}, s32[128]{0:T(128)S(1)}, u32[]{:S(2)}) copy-start(s32[128]{0:T(128)S(1)} %get-tuple-element.26) | copy-start | bytes 1540
  38.7 1.3 %copy-start = (bf16[2048,512]{1,0:T(8,128)(2,1)}, bf16[2048,512]{1,0:T(8,128)(2,1)S(1)}, u32[]{:S(2)}) copy-start(bf16[2048,512]{1,0:T(8,128)(2,1)S(1)} %get-tuple-element.13.zh_ref) | copy-start | bytes 6291460
  40.1 1.3 %copy-start.2 = (bf16[2048,512]{1,0:T(8,128)(2,1)}, bf16[2048,512]{1,0:T(8,128)(2,1)S(1)}, u32[]{:S(2)}) copy-start(bf16[2048,512]{1,0:T(8,128)(2,1)S(1)} %get-tuple-element.14.zl_ref) | copy-start | bytes 6291460
  41.4 1.6 %copy-start.1 = (bf16[2048,512]{1,0:T(8,128)(2,1)S(1)}, bf16[2048,512]{1,0:T(8,128)(2,1)}, u32[]{:S(2)}) copy-start(bf16[2048,512]{1,0:T(8,128)(2,1)} %copy-done) | copy-start | bytes 6291460
  43.0 1.6 %copy-start.3 = (bf16[2048,512]{1,0:T(8,128)(2,1)S(1)}, bf16[2048,512]{1,0:T(8,128)(2,1)}, u32[]{:S(2)}) copy-start(bf16[2048,512]{1,0:T(8,128)(2,1)} %copy-done.2) | copy-start | bytes 6291460
  52.3 5.5 %collective-permute-start.1 = (f32[768,128]{1,0:T(8,128)S(1)}, f32[768,128]{1,0:T(8,128)S(1)}, u32[]{:S(2)}, u32[]{:S(2)}) collective-permute-start(f32[768,128]{1,0:T(8,128)S(1)} %get-tuple-element.16), channel_id=1, source_target_pairs={{0,1},{1,0},{2,3},{3,2},{4,5},{5,4},{6,7},{7,6},{8,9},{9,8},{10,11... | collective-permute-start | bytes 1179656 | tf_op jit(solution)/shard_map/ppermute | solution.py:288
  54.2 3.6 %collective-permute-start = (f32[512,128]{1,0:T(8,128)S(1)}, f32[512,128]{1,0:T(8,128)S(1)}, u32[]{:S(2)}, u32[]{:S(2)}) collective-permute-start(f32[512,128]{1,0:T(8,128)S(1)} %get-tuple-element.12), channel_id=1, source_target_pairs={{0,1},{1,0},{2,3},{3,2},{4,5},{5,4},{6,7},{7,6},{8,9},{9,8},{10,11... | collective-permute-start | bytes 786440 | tf_op jit(solution)/shard_map/ppermute | solution.py:286
  57.8 12.6 %copy-start.6 = (f32[32,4096]{1,0:T(8,128)S(1)}, f32[32,4096]{1,0:T(8,128)}, u32[]{:S(2)}) copy-start(f32[32,4096]{1,0:T(8,128)} %param.12) | copy-start | bytes 1572868
  58.8 32.5 %all-to-all-start.1 = ((f32[32,40,128]{2,1,0:T(8,128)}), f32[32,40,128]{2,1,0:T(8,128)}, u32[]{:S(2)}, u32[]{:S(2)}) async-start(f32[32,40,128]{2,1,0:T(8,128)} %pad_maximum_fusion.2), calls=%async_computation.1 | async-start | bytes 1310720 | tf_op jit(solution)/shard_map/all_to_all | solution.py:293
  71.8 4.5 %copy-start.12 = (s32[128]{0:T(128)S(1)}, s32[128]{0:T(128)}, u32[]{:S(2)}) copy-start(s32[128]{0:T(128)} %copy-done.11) | copy-start | bytes 1540
  71.8 4.5 %copy-start.8 = (s32[128]{0:T(128)S(1)}, s32[128]{0:T(128)}, u32[]{:S(2)}) copy-start(s32[128]{0:T(128)} %copy-done.7) | copy-start | bytes 1540
where the time goes:
time: 94.3 us; the launch traced here: 93.7 us
  Pallas kernels  32.9 us (35%)
  starting transfers between devices  25.3 us (27%)
  local copies, waits for them, and re-layouts  23.5 us (25%)
  waiting for transfers between devices  5.94 us (6%)
  other arithmetic  5.04 us (5%)
  between operations  0.96 us (1%)
    pallas_call x1, Pallas kernels, own_part(): pl.pallas_call(own_kernel, out_shape=(jax.ShapeDtypeStruct((N, G * N), F3...  16 us
    all_to_all x1, starting transfers between devices, per_device(): parts = lax.all_to_all(sums, ('z', 'x'), 0, 0, tiled=True)  11.6 us
    all_to_all x1, starting transfers between devices, per_device(): lax.all_to_all(jnp.broadcast_to(plain[None], (STATES,) + plain.shape), 's...  9.38 us
    pallas_call x1, Pallas kernels, pair_action(): pl.pallas_call(pair_kernel, out_shape=jax.ShapeDtypeStruct((N, G * N), F3...  9.17 us
    pallas_call x1, Pallas kernels, pair_fields(): pl.pallas_call(field_kernel, out_shape=(jax.ShapeDtypeStruct((rows, 2 * N...  7.74 us
    reshape x4, local copies, waits for them, and re-layouts, rows_by_term(): return flat.reshape(TERMS, N, N).transpose(1, 0, 2).reshape(N, TERMS * N)  6.22 us
    unnamed x29, local copies, waits for them, and re-layouts  5.94 us
    all_to_all x1, waiting for transfers between devices, per_device(): parts = lax.all_to_all(sums, ('z', 'x'), 0, 0, tiled=True)  4.79 us
  transfers between devices with their start and end apart: 4, of which 2 were waited for; matrix products, arithmetic and copies ran while one was open for 18% of the time, Pallas kernels for 27%

commit v1 on v0

v1 whole, which is shorter than its diff:
```python
import jax
import jax.numpy as jnp
from jax import lax
from jax.experimental import pallas as pl
from jax.experimental.pallas import tpu as pltpu
from jax.sharding import Mesh, PartitionSpec as P

N = 64
G = 8
PAIRS = G // 2
LANES = 2 * N
TERMS = 32
STATES = 8
SLOTS = 48
OWN_TILES = TERMS // 2
ALL_TILES = (TERMS + SLOTS) // 2
UNROLL = 4
CHUNKS = TERMS // 4
F32 = jnp.float32
BF16 = jnp.bfloat16
NT = (((1,), (1,)), ((), ()))
VMEM = pl.BlockSpec(memory_space=pltpu.VMEM)
SMEM = pl.BlockSpec(memory_space=pltpu.SMEM)
HBM = pl.BlockSpec(memory_space=pltpu.HBM)


def dot(left, right):
    return jnp.dot(left, right, preferred_element_type=F32)


def dot_nt(left, right):
    return lax.dot_general(left, right, NT, preferred_element_type=F32)


def is_left(rows):
    return lax.broadcasted_iota(jnp.int32, (rows, LANES), 1) < N


def split(value):
    high = value.astype(BF16)
    low = (value - high.astype(F32)).astype(BF16)
    return high, low


def split_lanes(value):
    return jnp.concatenate(split(value), axis=1)


def half_blocks(operator):
    left = is_left(N)
    high = operator.astype(BF16).astype(F32)
    low = operator - high
    zero = jnp.zeros_like(operator)
    return [
        jnp.where(left, high, zero).astype(BF16),
        jnp.where(left, zero, high).astype(BF16),
        jnp.where(left, low, zero).astype(BF16),
        jnp.where(left, zero, low).astype(BF16),
    ]


def tile_nt(operator):
    h0, h1, l0, l1 = half_blocks(operator)
    zero = jnp.zeros((LANES, LANES), BF16)
    high = jnp.concatenate([h0, h1], axis=0)
    low = jnp.concatenate([l0, l1], axis=0)
    return jnp.concatenate(
        [jnp.concatenate([high, low], axis=0), jnp.concatenate([high, zero], axis=0)], axis=1
    )


def tile_nn(operator):
    h0, h1, l0, l1 = half_blocks(operator)
    zero = jnp.zeros((LANES, LANES), BF16)
    high = jnp.concatenate([h0, h1], axis=0)
    low = jnp.concatenate([l0, l1], axis=0)
    return jnp.concatenate(
        [jnp.concatenate([high, low], axis=1), jnp.concatenate([high, zero], axis=1)], axis=0
    )


def spread(raw_ref, out_ref):
    left = is_left(N // 2)
    for t in range(TERMS):
        start = (t // 8) * (8 * N // 2) + t % 8
        value = raw_ref[pl.ds(start, N // 2, stride=8), :]
        turned = pltpu.roll(value, N, 1)
        out_ref[t, pl.ds(0, N // 2, stride=2), :] = jnp.where(left, value, turned)
        out_ref[t, pl.ds(1, N // 2, stride=2), :] = jnp.where(left, turned, value)


def put_term(product, weights, index, high_ref, low_ref):
    value = product[:, :LANES] + product[:, LANES:]
    rows = pl.ds(pl.multiple_of(index * N, N), N)
    left = is_left(1)
    for pair in range(PAIRS):
        weight = jnp.where(left, weights[2 * pair], weights[2 * pair + 1])
        high, low = split(value[pair * N : (pair + 1) * N] * weight)
        high_ref[rows, pair * LANES : (pair + 1) * LANES] = high
        low_ref[rows, pair * LANES : (pair + 1) * LANES] = low


def put_left(operators, index, left_ref):
    high, low = split(jnp.where(is_left(N), operators[0], operators[1]))
    columns = pl.ds(pl.multiple_of(index * LANES, LANES), LANES)
    left_ref[:N, columns] = high
    left_ref[N:, columns] = low


def act_on(left_ref, high_ref, low_ref):
    both = dot(left_ref[...], high_ref[...])
    return both[:N] + both[N:] + dot(left_ref[:N], low_ref[...])


def arrange_kernel(core_ref, raw_ref, out_ref, plain_ref, mine_ref):
    left = is_left(N // 2)
    is_first = core_ref[0] == 0
    for pair in range(PAIRS):
        one = raw_ref[pl.ds(2 * pair, N // 2, stride=G), :]
        two = raw_ref[pl.ds(2 * pair + 1, N // 2, stride=G), :]
        even = jnp.where(left, one, pltpu.roll(two, N, 1))
        odd = jnp.where(left, pltpu.roll(one, N, 1), two)
        plain_ref[pl.ds(pair * N, N // 2, stride=2), :] = even
        plain_ref[pl.ds(pair * N + 1, N // 2, stride=2), :] = odd
        mine_ref[pair * N : pair * N + N // 2, :] = jnp.where(is_first, even, odd)
        mine_ref[pair * N + N // 2 : (pair + 1) * N, :] = jnp.where(is_first, odd, even)
    for q in range(STATES):
        out_ref[q] = plain_ref[...]


def own_kernel(v_ref, cv_ref, a_ref, ap_ref, h3_ref, h2_ref, c3_ref,
               act_ref, field_ref, zh_hbm, zl_hbm,
               ops_ref, left_ref, wh_ref, wl_ref, zh_ref, zl_ref, sems):
    def chunk_copies(j):
        rows = pl.ds(pl.multiple_of(j * UNROLL * N, UNROLL * N), UNROLL * N)
        return [
            pltpu.make_async_copy(zh_ref.at[rows, :], zh_hbm.at[rows, :], sems.at[0, j]),
            pltpu.make_async_copy(zl_ref.at[rows, :], zl_hbm.at[rows, :], sems.at[1, j]),
        ]

    left_p = split_lanes(ap_ref[...])
    spread(c3_ref, ops_ref)

    def coupling_terms(j, carry):
        for u in range(UNROLL):
            k = j * UNROLL + u
            product = dot(left_p, tile_nn(ops_ref[k]))
            put_term(product, [cv_ref[k, g] for g in range(G)], k, zh_ref, zl_ref)

        @pl.when(j > 0)
        def _():
            for copy in chunk_copies(j - 1):
                copy.start()

        return carry

    lax.fori_loop(0, CHUNKS, coupling_terms, 0)

    spread(h2_ref, ops_ref)
    for i in range(OWN_TILES):
        put_left((ops_ref[2 * i], ops_ref[2 * i + 1]), i, left_ref)
    for copy in chunk_copies(CHUNKS - 1):
        copy.start()
    spread(h3_ref, ops_ref)
    left = split_lanes(a_ref[...])

    def own_terms(j, carry):
        for u in range(UNROLL):
            t = j * UNROLL + u
            product = dot_nt(left, tile_nt(ops_ref[t]))
            put_term(product, [v_ref[t, g] for g in range(G)], t, wh_ref, wl_ref)
        return carry

    lax.fori_loop(0, CHUNKS, own_terms, 0)
    act_ref[...] = act_on(left_ref, wh_ref, wl_ref)

    wide = jnp.concatenate([ap_ref[p * N : (p + 1) * N, :] for p in range(PAIRS)], axis=1)
    high, low = split(wide)
    rows_both = jnp.concatenate([high, low], axis=0)
    for j in range(CHUNKS):
        part = slice(j * UNROLL * N, (j + 1) * UNROLL * N)
        both = dot_nt(rows_both, wh_ref[part, :])
        field_ref[:, part] = both[:N] + both[N:] + dot_nt(high, wl_ref[part, :])

    for j in range(CHUNKS):
        for copy in chunk_copies(j):
            copy.wait()


def field_kernel(source_ref, term_ref, valid_ref, all_ref, own_ref, zh_hbm, zl_hbm,
                 mine_ref, other_ref, gh_ref, gl_ref, zh_ref, zl_ref, f_ref, sems):
    def chunk_copies(j):
        rows = pl.ds(pl.multiple_of(j * UNROLL * N, UNROLL * N), UNROLL * N)
        return [
            pltpu.make_async_copy(zh_hbm.at[rows, :], zh_ref.at[rows, :], sems.at[0, j]),
            pltpu.make_async_copy(zl_hbm.at[rows, :], zl_ref.at[rows, :], sems.at[1, j]),
        ]

    for j in range(CHUNKS):
        for copy in chunk_copies(j):
            copy.start()
    for q in range(STATES):
        for pair in range(PAIRS):
            high, low = split(all_ref[q, pair * N : (pair + 1) * N, :])
            lanes = slice(pair * LANES, (pair + 1) * LANES)
            gh_ref[q * N : (q + 1) * N, lanes] = high
            gl_ref[q * N : (q + 1) * N, lanes] = low
    for i in range(OWN_TILES):
        where_to = pl.ds(i, N // 2, stride=ALL_TILES)
        lanes = slice(i * LANES, (i + 1) * LANES)
        mine_ref[where_to, :] = own_ref[: N // 2, lanes]
        other_ref[where_to, :] = own_ref[N // 2 :, lanes]

    def block(j, carry):
        for copy in chunk_copies(j):
            copy.wait()
        rows = pl.ds(pl.multiple_of(j * UNROLL * N, UNROLL * N), UNROLL * N)
        zh = zh_ref[rows, :]
        left = jnp.concatenate([zh, zl_ref[rows, :], zh], axis=1)
        for half in range(2):
            here = slice(half * 4 * N, (half + 1) * 4 * N)
            gh = gh_ref[here, :]
            right = jnp.concatenate([gh, gh, gl_ref[here, :]], axis=1)
            product = dot_nt(left, right)
            f_ref[2 * half, rows, :] = product[:, :LANES]
            f_ref[2 * half + 1, rows, :] = product[:, LANES:]
        return carry

    lax.fori_loop(0, CHUNKS, block, 0)
    left_lanes = is_left(N)

    def pick(slot):
        source = source_ref[slot]
        rows = pl.ds(pl.multiple_of(term_ref[slot] * N, N), N)
        return f_ref[source // 2, rows, :], lax.rem(source, 2)

    def slot_pair(i):
        first, odd_first = pick(2 * i)
        second, odd_second = pick(2 * i + 1)
        first = jnp.where(odd_first == 1, pltpu.roll(first, N, 1), first)
        second = jnp.where(odd_second == 0, pltpu.roll(second, N, 1), second)
        first = jnp.where(valid_ref[2 * i] == 1, first, 0.0)
        second = jnp.where(valid_ref[2 * i + 1] == 1, second, 0.0)
        field = jnp.where(left_lanes, first, second)
        where_to = pl.ds(OWN_TILES + i, N // 2, stride=ALL_TILES)
        mine_ref[where_to, :] = field[: N // 2]
        other_ref[where_to, :] = field[N // 2 :]

    def slot_pairs(i, carry):
        for u in range(4):
            slot_pair(4 * i + u)
        return carry

    lax.fori_loop(0, SLOTS // 8, slot_pairs, 0)


def pair_kernel(source_ref, term_ref, valid_ref, cv_ref, all_ref, c3_ref, c2_ref, act_ref,
                out_ref, left_all_ref, ops_ref, left_ref, wh_ref, wl_ref, sum_ref):
    for q in range(STATES):
        left_all_ref[q] = split_lanes(all_ref[q])
    spread(c2_ref, ops_ref)

    def left_tiles(i, carry):
        for u in range(2):
            tile = 2 * i + u
            first, second = term_ref[2 * tile], term_ref[2 * tile + 1]
            put_left((ops_ref[first], ops_ref[second]), tile, left_ref)
        return carry

    lax.fori_loop(0, SLOTS // 4, left_tiles, 0)
    spread(c3_ref, ops_ref)

    def slot_terms(j, carry):
        for u in range(UNROLL):
            slot = j * UNROLL + u
            k = term_ref[slot]
            product = dot_nt(left_all_ref[source_ref[slot]], tile_nt(ops_ref[k]))
            is_valid = valid_ref[slot] == 1
            weights = [jnp.where(is_valid, cv_ref[k, g], 0.0) for g in range(G)]
            put_term(product, weights, slot, wh_ref, wl_ref)
        return carry

    lax.fori_loop(0, SLOTS // UNROLL, slot_terms, 0)
    action = act_ref[...] + act_on(left_ref, wh_ref, wl_ref)
    left = is_left(N // 2)
    for pair in range(PAIRS):
        sum_ref[pair * N : (pair + 1) * N, :] = action[:, pair * LANES : (pair + 1) * LANES]
        even = sum_ref[pl.ds(pair * N, N // 2, stride=2), :]
        odd = sum_ref[pl.ds(pair * N + 1, N // 2, stride=2), :]
        one = jnp.where(left, even, pltpu.roll(odd, N, 1))
        two = jnp.where(left, pltpu.roll(even, N, 1), odd)
        out_ref[pl.ds(2 * pair, N // 2, stride=G), :] = one
        out_ref[pl.ds(2 * pair + 1, N // 2, stride=G), :] = two


def total_kernel(parts_ref, own_ref, pair_ref):
    total = parts_ref[0]
    for i in range(1, N // 2):
        total = total + parts_ref[i]
    own_ref[...] = total[:OWN_TILES]
    pair_ref[...] = total[OWN_TILES:]


def shape(*dims, dtype=F32):
    return jax.ShapeDtypeStruct(dims, dtype)


def cost(flops, nbytes):
    return pl.CostEstimate(flops=flops, bytes_accessed=nbytes, transcendentals=0)


def params(mib):
    return pltpu.CompilerParams(vmem_limit_bytes=mib << 20)


OWN_GRANT = 52
FIELD_GRANT = 50


def arrange(core, raw):
    return pl.pallas_call(
        arrange_kernel,
        out_shape=(shape(STATES, PAIRS * N, LANES), shape(PAIRS * N, LANES), shape(PAIRS * N, LANES)),
        in_specs=[SMEM, VMEM],
        out_specs=[pl.BlockSpec(), VMEM, VMEM],
        compiler_params=params(8),
        name="arrange",
    )(core, raw)


def own_part(v, cv, a2, a2p, h3, h2, c3):
    big = pltpu.VMEM((TERMS * N, G * N), BF16)
    return pl.pallas_call(
        own_kernel,
        out_shape=(
            shape(N, G * N),
            shape(N, TERMS * N),
            shape(TERMS * N, G * N, dtype=BF16),
            shape(TERMS * N, G * N, dtype=BF16),
        ),
        in_specs=[SMEM] * 2 + [VMEM] * 5,
        out_specs=[VMEM] * 2 + [HBM] * 2,
        scratch_shapes=[
            pltpu.VMEM((TERMS, N, LANES), F32),
            pltpu.VMEM((LANES, TERMS * N), BF16),
            big, big, big, big,
            pltpu.SemaphoreType.DMA((2, CHUNKS)),
        ],
        compiler_params=params(OWN_GRANT),
        cost_estimate=cost(3_000_000_000, 8 << 20),
        name="own_part",
    )(v, cv, a2, a2p, h3, h2, c3)


def both_fields(source, term, valid, everyone, own, zh, zl):
    big = pltpu.VMEM((TERMS * N, G * N), BF16)
    rows = N // 2 * ALL_TILES
    return pl.pallas_call(
        field_kernel,
        out_shape=(shape(rows, LANES), shape(rows, LANES)),
        in_specs=[SMEM] * 3 + [VMEM] * 2 + [HBM] * 2,
        out_specs=[VMEM] * 2,
        scratch_shapes=[
            pltpu.VMEM((STATES * N, G * N), BF16),
            pltpu.VMEM((STATES * N, G * N), BF16),
            big, big,
            pltpu.VMEM((STATES // 2, TERMS * N, LANES), F32),
            pltpu.SemaphoreType.DMA((2, CHUNKS)),
        ],
        compiler_params=params(FIELD_GRANT),
        cost_estimate=cost(3_000_000_000, 6 << 20),
        name="both_fields",
    )(source, term, valid, everyone, own, zh, zl)


def pair_action(source, term, valid, cv, everyone, c3, c2, act):
    return pl.pallas_call(
        pair_kernel,
        out_shape=shape(PAIRS * N, LANES),
        in_specs=[SMEM] * 4 + [VMEM] * 4,
        out_specs=pl.BlockSpec(),
        scratch_shapes=[
            pltpu.VMEM((STATES, PAIRS * N, 2 * LANES), BF16),
            pltpu.VMEM((TERMS, N, LANES), F32),
            pltpu.VMEM((LANES, SLOTS * N), BF16),
            pltpu.VMEM((SLOTS * N, G * N), BF16),
            pltpu.VMEM((SLOTS * N, G * N), BF16),
            pltpu.VMEM((PAIRS * N, LANES), F32),
        ],
        compiler_params=params(24),
        cost_estimate=cost(3_000_000_000, 4 << 20),
        name="pair_action",
    )(source, term, valid, cv, everyone, c3, c2, act)


def total(parts):
    return pl.pallas_call(
        total_kernel,
        out_shape=(shape(OWN_TILES, LANES), shape(SLOTS // 2, LANES)),
        in_specs=[pl.BlockSpec()],
        out_specs=(pl.BlockSpec(), pl.BlockSpec()),
        compiler_params=params(8),
        name="total",
    )(parts)


def tile_rows(flat):
    blocks = flat.shape[0] // 8
    tiles = flat.reshape(blocks, 8, N // 2, LANES)
    return tiles.transpose(0, 2, 1, 3).reshape(blocks * 8 * N // 2, LANES)


def read_list(pairs, myself):
    is_mine = pairs[:, 0] == myself
    rank = jnp.cumsum(is_mine.astype(jnp.int32)) - 1
    slots = jnp.arange(SLOTS, dtype=jnp.int32)
    picked = (rank[None, :] == slots[:, None]) & is_mine[None, :]
    source = jnp.sum(jnp.where(picked, pairs[None, :, 1], 0), axis=1)
    term = jnp.sum(jnp.where(picked, pairs[None, :, 2], 0), axis=1)
    valid = jnp.sum(picked.astype(jnp.int32), axis=1)
    return source, term, valid


def per_device(coeffs, diag_h2, diag_h3, diag_v1, coup_h2, coup_h3, coup_v1, pairs):
    core = lax.axis_index("core").astype(jnp.int32)[None]
    to_all, plain, mine_first = arrange(core, tile_rows(coeffs[0]))
    everyone = lax.all_to_all(to_all, "state", 0, 0, tiled=True)
    listed = read_list(pairs, lax.axis_index("state"))
    c3 = tile_rows(coup_h3)
    act, own, zh, zl = own_part(
        diag_v1[0], coup_v1, plain, mine_first, tile_rows(diag_h3[0]), tile_rows(diag_h2[0]), c3
    )
    mine, other = both_fields(*listed, everyone, own, zh, zl)
    sums = mine + lax.ppermute(other, "core", [(0, 1), (1, 0)])
    parts = lax.all_to_all(
        sums.reshape(N // 2, ALL_TILES, LANES), ("z", "x"), 0, 0, tiled=True
    )
    out = pair_action(*listed, coup_v1, everyone, c3, tile_rows(coup_h2), act)
    action = out.reshape(N // 2, G, LANES).transpose(1, 0, 2).reshape(1, G, N * N)
    own_row, pair_row = total(parts)
    return action, own_row.reshape(1, 1, TERMS * N), pair_row.reshape(1, 1, SLOTS * N)


def solution(mesh):
    fine = Mesh(mesh.devices.reshape(8, 8, 4, 2), ("state", "z", "x", "core"))
    mode = ("z", "x", "core")
    placed = (
        P("state", mode, None),
        P("state", None, None),
        P("state", None, None),
        P("state", None, mode),
        P(),
        P(),
        P(None, mode),
        P(),
    )
    out = P("state", mode, None)
    return jax.shard_map(
        per_device, mesh=fine, in_specs=placed, out_specs=(out, out, out), check_vma=False
    )
```

time: 94.3 us -> 85.5 us (0.907)
  the two profiles are of different devices: /device:TPU:8 before, /device:TPU:1 now
where the time goes in v1:
time: 85.5 us; the launch traced here: 84.5 us
  waiting for transfers between devices  29.8 us (35%)
  Pallas kernels  26.5 us (31%)
  starting transfers between devices  25 us (29%)
  other arithmetic  1.34 us (2%)
  local copies, waits for them, and re-layouts  1.21 us (1%)
    all_to_all x1, waiting for transfers between devices, per_device(): everyone = lax.all_to_all(to_all, 'state', 0, 0, tiled=True)  17.1 us
    all_to_all x1, starting transfers between devices, per_device(): lax.all_to_all(sums.reshape(N // 2, ALL_TILES, LANES), ('z', 'x'), 0, 0,...  12.9 us
    all_to_all x1, waiting for transfers between devices, per_device(): lax.all_to_all(sums.reshape(N // 2, ALL_TILES, LANES), ('z', 'x'), 0, 0,...  11 us
    pallas_call x1, Pallas kernels, own_part(): pl.pallas_call(own_kernel, out_shape=(shape(N, G * N), shape(N, TERMS * N...  9.48 us
    pallas_call x1, Pallas kernels, pair_action(): pl.pallas_call(pair_kernel, out_shape=shape(PAIRS * N, LANES), in_specs=[...  7.76 us
    all_to_all x1, starting transfers between devices, per_device(): everyone = lax.all_to_all(to_all, 'state', 0, 0, tiled=True)  7.64 us
    pallas_call x1, Pallas kernels, both_fields(): pl.pallas_call(field_kernel, out_shape=(shape(rows, LANES), shape(rows, L...  7.43 us
    ppermute x1, starting transfers between devices, per_device(): sums = mine + lax.ppermute(other, 'core', [(0, 1), (1, 0)])  4.44 us
  transfers between devices with their start and end apart: 3, of which 3 were waited for; matrix products, arithmetic and copies ran while one was open for 1% of the time, Pallas kernels for 20%

profile of v1, /device:TPU:1, one launch (start us, length us, event | category | flops | bytes accessed | tf_op | source)
XLA Modules:
  0.0 84.5 jit_solution(2988720114493769567)
XLA Ops:
  0.6 0.0 copy-start.5
  0.7 0.0 copy-start
  0.7 0.9 %copy-done = f32[1,8,4096]{2,1,0:T(8,128)S(1)} copy-done((f32[1,8,4096]{2,1,0:T(8,128)S(1)}, f32[1,8,4096]{2,1,0:T(8,128)}, u32[]{:S(2)}) %copy-start) | copy-done | bytes 131096
  1.6 1.1 %arrange.1 = (f32[8,256,128]{2,1,0:T(8,128)}, f32[256,128]{1,0:T(8,128)S(1)}, f32[256,128]{1,0:T(8,128)S(1)}) custom-call(s32[1]{0:T(128)} %bitcast.3.core_ref, f32[256,128]{1,0:T(8,128)S(1)} %bitcast.41), custom_call_target="tpu_custom_call" | custom-call | tf_op jit(solution)/shard_map/arrange/pallas_call | solution.py:321
  2.7 7.6 %all-to-all-start = ((f32[8,256,128]{2,1,0:T(8,128)}), f32[8,256,128]{2,1,0:T(8,128)S(1)}, u32[]{:S(2)}, u32[]{:S(2)}) async-start(f32[8,256,128]{2,1,0:T(8,128)} %get-tuple-element.14), calls=%async_computation | async-start | bytes 2097152 | tf_op jit(solution)/shard_map/all_to_all | solution.py:427
  10.4 0.0 copy-done.5
  10.4 0.1 copy.22.cv_ref
  10.4 0.1 copy.20
  10.5 0.1 copy.19
  10.6 0.2 reduce-window.8
  10.8 0.1 add_reduce_fusion
  10.9 0.2 convert_reduce_fusion
  11.1 9.5 %own_part.1 = (f32[64,512]{1,0:T(8,128)S(1)}, f32[64,2048]{1,0:T(8,128)S(1)}, bf16[2048,512]{1,0:T(8,128)(2,1)}, bf16[2048,512]{1,0:T(8,128)(2,1)}) custom-call(f32[32,8]{1,0:T(8,128)S(1)} %bitcast.42, f32[32,8]{1,0:T(8,128)S(1)} %copy.22.cv_ref, f32[256,128]{1,0:T(8,128)S(1)} %get-tuple-element.15.a_ref, f32[256,128]{1,0:T(8,128)S(1)} %get-tuple-element.16.ap_ref, ...), custom_call_target="tpu_custom_call" | custom-call | flops 3000000000 | bytes 8388608 | tf_op jit(solution)/shard_map/own_part/pallas_call | solution.py:333
  20.6 17.1 %all-to-all-done.all_ref = f32[8,256,128]{2,1,0:T(8,128)S(1)} async-done(((f32[8,256,128]{2,1,0:T(8,128)}), f32[8,256,128]{2,1,0:T(8,128)S(1)}, u32[]{:S(2)}, u32[]{:S(2)}) %all-to-all-start) | async-done | bytes 1048608 | tf_op jit(solution)/shard_map/all_to_all | solution.py:427
  37.6 7.4 %both_fields.1 = (f32[1280,128]{1,0:T(8,128)S(1)}, f32[1280,128]{1,0:T(8,128)S(1)}) custom-call(s32[48]{0:T(128)S(1)} %get-tuple-element.27.source_ref, s32[48]{0:T(128)S(1)} %get-tuple-element.26.term_ref, s32[48]{0:T(128)S(1)} %get-tuple-element.25.valid_ref, f32[8,256,128]{2,1,0:T(8,128)S(1)} %all-to-all-done.all_ref, ...), custom_call_target="tpu_custom_call" | custom-call | flops 3000000000 | bytes 6291456 | tf_op jit(solution)/shard_map/both_fields/pallas_call | solution.py:358
  45.1 0.0 copy-start.3
  45.1 0.0 copy-start.4
  45.1 4.4 %collective-permute-start = (f32[1280,128]{1,0:T(8,128)S(1)}, f32[1280,128]{1,0:T(8,128)S(1)}, u32[]{:S(2)}, u32[]{:S(2)}) collective-permute-start(f32[1280,128]{1,0:T(8,128)S(1)} %get-tuple-element.22), channel_id=1, source_target_pairs={{0,1},{1,0},{2,3},{3,2},{4,5},{5,4},{6,7},{7,6},{8,9},{9,8},{10,11... | collective-permute-start | bytes 1966088 | tf_op jit(solution)/shard_map/ppermute | solution.py:434
  49.6 1.7 %collective-permute-done = f32[1280,128]{1,0:T(8,128)S(1)} collective-permute-done((f32[1280,128]{1,0:T(8,128)S(1)}, f32[1280,128]{1,0:T(8,128)S(1)}, u32[]{:S(2)}, u32[]{:S(2)}) %collective-permute-start) | collective-permute-done | bytes 655392 | tf_op jit(solution)/shard_map/ppermute | solution.py:434
  51.3 0.9 %add.9 = f32[1280,128]{1,0:T(8,128)} add(f32[1280,128]{1,0:T(8,128)S(1)} %get-tuple-element.21, f32[1280,128]{1,0:T(8,128)S(1)} %collective-permute-done) | non-fusion elementwise | flops 163840 | bytes 1966080 | tf_op jit(solution)/shard_map/add | solution.py:434
  52.2 12.9 %all-to-all-start.1 = ((f32[32,40,128]{2,1,0:T(8,128)}), f32[32,40,128]{2,1,0:T(8,128)S(1)}, u32[]{:S(2)}, u32[]{:S(2)}) async-start(f32[32,40,128]{2,1,0:T(8,128)} %bitcast.48), calls=%async_computation.1 | async-start | bytes 1310720 | tf_op jit(solution)/shard_map/all_to_all | solution.py:435
  65.1 7.8 %pair_action.1 = f32[256,128]{1,0:T(8,128)} custom-call(s32[48]{0:T(128)S(1)} %get-tuple-element.27.source_ref, s32[48]{0:T(128)S(1)} %get-tuple-element.26.term_ref, s32[48]{0:T(128)S(1)} %get-tuple-element.25.valid_ref, f32[32,8]{1,0:T(8,128)S(1)} %copy.22.cv_ref, f32[8,256,128]{2,1,0:T(8,128)S(1)} %all-to-all-done.all_ref, f32[1024,128]{1,0:T(8,128)S(1)} %bitcast.46, ...), custom_call_target="tpu_custom_call" | custom-call | flops 3000000000 | bytes 4194304 | tf_op jit(solution)/shard_map/pair_action/pallas_call | solution.py:377
  72.8 11.0 %all-to-all-done.1.parts_ref = f32[32,40,128]{2,1,0:T(8,128)S(1)} async-done(((f32[32,40,128]{2,1,0:T(8,128)}), f32[32,40,128]{2,1,0:T(8,128)S(1)}, u32[]{:S(2)}, u32[]{:S(2)}) %all-to-all-start.1) | async-done | bytes 655392 | tf_op jit(solution)/shard_map/all_to_all | solution.py:435
  83.8 0.7 total.1
  (12 shorter events, 0.0 us)
Async XLA Ops:
  0.6 9.7 %copy-start.5 = (f32[32,8]{0,1:T(8,128)S(1)}, f32[32,8]{0,1:T(8,128)}, u32[]{:S(2)}) copy-start(f32[32,8]{0,1:T(8,128)} %param.14) | copy-start | bytes 3076
  0.6 9.8 %copy-start.6 = (f32[1,32,8]{1,2,0:T(8,128)S(1)}, f32[1,32,8]{1,2,0:T(8,128)}, u32[]{:S(2)}) copy-start(f32[1,32,8]{1,2,0:T(8,128)} %param.11) | copy-start | bytes 3076
  0.7 0.9 %copy-start = (f32[1,8,4096]{2,1,0:T(8,128)S(1)}, f32[1,8,4096]{2,1,0:T(8,128)}, u32[]{:S(2)}) copy-start(f32[1,8,4096]{2,1,0:T(8,128)} %param.8) | copy-start | bytes 393220
  1.6 9.0 %copy-start.7 = (s32[128,3]{0,1:T(4,128)S(1)}, s32[128,3]{0,1:T(4,128)}, u32[]{:S(2)}) copy-start(s32[128,3]{0,1:T(4,128)} %param.15) | copy-start | bytes 4612
  1.6 9.5 %copy-start.1 = (f32[1,32,4096]{2,1,0:T(8,128)S(1)}, f32[1,32,4096]{2,1,0:T(8,128)}, u32[]{:S(2)}) copy-start(f32[1,32,4096]{2,1,0:T(8,128)} %param.10) | copy-start | bytes 1572868
  1.6 9.5 %copy-start.2 = (f32[1,32,4096]{2,1,0:T(8,128)S(1)}, f32[1,32,4096]{2,1,0:T(8,128)}, u32[]{:S(2)}) copy-start(f32[1,32,4096]{2,1,0:T(8,128)} %param.9) | copy-start | bytes 1572868
  2.7 34.9 %all-to-all-start = ((f32[8,256,128]{2,1,0:T(8,128)}), f32[8,256,128]{2,1,0:T(8,128)S(1)}, u32[]{:S(2)}, u32[]{:S(2)}) async-start(f32[8,256,128]{2,1,0:T(8,128)} %get-tuple-element.14), calls=%async_computation | async-start | bytes 2097152 | tf_op jit(solution)/shard_map/all_to_all | solution.py:427
  45.1 20.0 %copy-start.3 = (f32[32,4096]{1,0:T(8,128)S(1)}, f32[32,4096]{1,0:T(8,128)}, u32[]{:S(2)}) copy-start(f32[32,4096]{1,0:T(8,128)} %param.13) | copy-start | bytes 1572868
  45.1 20.0 %copy-start.4 = (f32[32,4096]{1,0:T(8,128)S(1)}, f32[32,4096]{1,0:T(8,128)}, u32[]{:S(2)}) copy-start(f32[32,4096]{1,0:T(8,128)} %param.12) | copy-start | bytes 1572868
  45.1 6.2 %collective-permute-start = (f32[1280,128]{1,0:T(8,128)S(1)}, f32[1280,128]{1,0:T(8,128)S(1)}, u32[]{:S(2)}, u32[]{:S(2)}) collective-permute-start(f32[1280,128]{1,0:T(8,128)S(1)} %get-tuple-element.22), channel_id=1, source_target_pairs={{0,1},{1,0},{2,3},{3,2},{4,5},{5,4},{6,7},{7,6},{8,9},{9,8},{10,11... | collective-permute-start | bytes 1966088 | tf_op jit(solution)/shard_map/ppermute | solution.py:434
  52.2 31.7 %all-to-all-start.1 = ((f32[32,40,128]{2,1,0:T(8,128)}), f32[32,40,128]{2,1,0:T(8,128)S(1)}, u32[]{:S(2)}, u32[]{:S(2)}) async-start(f32[32,40,128]{2,1,0:T(8,128)} %bitcast.48), calls=%async_computation.1 | async-start | bytes 1310720 | tf_op jit(solution)/shard_map/all_to_all | solution.py:435

commit v2 on v1

--- a/solution.py
+++ b/solution.py
@@ -13,7 +13,10 @@
 STATES = 8
 SLOTS = 48
 OWN_TILES = TERMS // 2
-ALL_TILES = (TERMS + SLOTS) // 2
+PAIR_TILES = SLOTS // 2
+X_CHIPS = 4
+LAST_TILES = OWN_TILES // X_CHIPS
+ALL_TILES = PAIR_TILES + LAST_TILES
 UNROLL = 4
 CHUNKS = TERMS // 4
 F32 = jnp.float32
@@ -129,7 +132,7 @@
 
 
 def own_kernel(v_ref, cv_ref, a_ref, ap_ref, h3_ref, h2_ref, c3_ref,
-               act_ref, field_ref, zh_hbm, zl_hbm,
+               act_ref, mine_ref, other_ref, zh_hbm, zl_hbm,
                ops_ref, left_ref, wh_ref, wl_ref, zh_ref, zl_ref, sems):
     def chunk_copies(j):
         rows = pl.ds(pl.multiple_of(j * UNROLL * N, UNROLL * N), UNROLL * N)
@@ -180,14 +183,19 @@
     for j in range(CHUNKS):
         part = slice(j * UNROLL * N, (j + 1) * UNROLL * N)
         both = dot_nt(rows_both, wh_ref[part, :])
-        field_ref[:, part] = both[:N] + both[N:] + dot_nt(high, wl_ref[part, :])
+        field = both[:N] + both[N:] + dot_nt(high, wl_ref[part, :])
+        for half in range(2):
+            lanes = slice(half * LANES, (half + 1) * LANES)
+            rows = slice((2 * j + half) * N // 2, (2 * j + half + 1) * N // 2)
+            mine_ref[rows, :] = field[: N // 2, lanes]
+            other_ref[rows, :] = field[N // 2 :, lanes]
 
     for j in range(CHUNKS):
         for copy in chunk_copies(j):
             copy.wait()
 
 
-def field_kernel(source_ref, term_ref, valid_ref, all_ref, own_ref, zh_hbm, zl_hbm,
+def field_kernel(source_ref, term_ref, valid_ref, all_ref, zh_hbm, zl_hbm,
                  mine_ref, other_ref, gh_ref, gl_ref, zh_ref, zl_ref, f_ref, sems):
     def chunk_copies(j):
         rows = pl.ds(pl.multiple_of(j * UNROLL * N, UNROLL * N), UNROLL * N)
@@ -205,16 +213,10 @@
             lanes = slice(pair * LANES, (pair + 1) * LANES)
             gh_ref[q * N : (q + 1) * N, lanes] = high
             gl_ref[q * N : (q + 1) * N, lanes] = low
-    for i in range(OWN_TILES):
-        where_to = pl.ds(i, N // 2, stride=ALL_TILES)
-        lanes = slice(i * LANES, (i + 1) * LANES)
-        mine_ref[where_to, :] = own_ref[: N // 2, lanes]
-        other_ref[where_to, :] = own_ref[N // 2 :, lanes]
-
     def block(j, carry):
-        for copy in chunk_copies(j):
+        for copy in chunk_copies(2 * j) + chunk_copies(2 * j + 1):
             copy.wait()
-        rows = pl.ds(pl.multiple_of(j * UNROLL * N, UNROLL * N), UNROLL * N)
+        rows = pl.ds(pl.multiple_of(j * 2 * UNROLL * N, 2 * UNROLL * N), 2 * UNROLL * N)
         zh = zh_ref[rows, :]
         left = jnp.concatenate([zh, zl_ref[rows, :], zh], axis=1)
         for half in range(2):
@@ -226,7 +228,7 @@
             f_ref[2 * half + 1, rows, :] = product[:, LANES:]
         return carry
 
-    lax.fori_loop(0, CHUNKS, block, 0)
+    lax.fori_loop(0, CHUNKS // 2, block, 0)
     left_lanes = is_left(N)
 
     def pick(slot):
@@ -242,16 +244,16 @@
         first = jnp.where(valid_ref[2 * i] == 1, first, 0.0)
         second = jnp.where(valid_ref[2 * i + 1] == 1, second, 0.0)
         field = jnp.where(left_lanes, first, second)
-        where_to = pl.ds(OWN_TILES + i, N // 2, stride=ALL_TILES)
+        where_to = pl.ds(i, N // 2, stride=PAIR_TILES)
         mine_ref[where_to, :] = field[: N // 2]
         other_ref[where_to, :] = field[N // 2 :]
 
     def slot_pairs(i, carry):
-        for u in range(4):
-            slot_pair(4 * i + u)
+        for u in range(8):
+            slot_pair(8 * i + u)
         return carry
 
-    lax.fori_loop(0, SLOTS // 8, slot_pairs, 0)
+    lax.fori_loop(0, PAIR_TILES // 8, slot_pairs, 0)
 
 
 def pair_kernel(source_ref, term_ref, valid_ref, cv_ref, all_ref, c3_ref, c2_ref, act_ref,
@@ -293,12 +295,27 @@
         out_ref[pl.ds(2 * pair + 1, N // 2, stride=G), :] = two
 
 
+def merge_kernel(mine_ref, theirs_ref, own_ref, out_ref):
+    for a in range(N // 2):
+        here = slice(a * PAIR_TILES, (a + 1) * PAIR_TILES)
+        out_ref[a * ALL_TILES : a * ALL_TILES + PAIR_TILES, :] = mine_ref[here, :] + theirs_ref[here, :]
+    for r in range(LAST_TILES):
+        out_ref[pl.ds(PAIR_TILES + r, N // 2, stride=ALL_TILES), :] = own_ref[r]
+
+
 def total_kernel(parts_ref, own_ref, pair_ref):
-    total = parts_ref[0]
+    def part(i, first, count):
+        return parts_ref[i * ALL_TILES + first : i * ALL_TILES + first + count, :]
+
+    total = part(0, 0, PAIR_TILES)
     for i in range(1, N // 2):
-        total = total + parts_ref[i]
-    own_ref[...] = total[:OWN_TILES]
-    pair_ref[...] = total[OWN_TILES:]
+        total = total + part(i, 0, PAIR_TILES)
+    pair_ref[...] = total
+    for x in range(X_CHIPS):
+        total = part(x, PAIR_TILES, LAST_TILES)
+        for z in range(1, N // 2 // X_CHIPS):
+            total = total + part(z * X_CHIPS + x, PAIR_TILES, LAST_TILES)
+        own_ref[x * LAST_TILES : (x + 1) * LAST_TILES, :] = total
 
 
 def shape(*dims, dtype=F32):
@@ -314,7 +331,7 @@
 
 
 OWN_GRANT = 52
-FIELD_GRANT = 50
+FIELD_GRANT = 52
 
 
 def arrange(core, raw):
@@ -334,12 +351,13 @@
         own_kernel,
         out_shape=(
             shape(N, G * N),
-            shape(N, TERMS * N),
+            shape(N // 2 * OWN_TILES, LANES),
+            shape(N // 2 * OWN_TILES, LANES),
             shape(TERMS * N, G * N, dtype=BF16),
             shape(TERMS * N, G * N, dtype=BF16),
         ),
         in_specs=[SMEM] * 2 + [VMEM] * 5,
-        out_specs=[VMEM] * 2 + [HBM] * 2,
+        out_specs=[VMEM] * 3 + [HBM] * 2,
         scratch_shapes=[
             pltpu.VMEM((TERMS, N, LANES), F32),
             pltpu.VMEM((LANES, TERMS * N), BF16),
@@ -352,13 +370,13 @@
     )(v, cv, a2, a2p, h3, h2, c3)
 
 
-def both_fields(source, term, valid, everyone, own, zh, zl):
+def pair_fields(source, term, valid, everyone, zh, zl):
     big = pltpu.VMEM((TERMS * N, G * N), BF16)
-    rows = N // 2 * ALL_TILES
+    rows = N // 2 * PAIR_TILES
     return pl.pallas_call(
         field_kernel,
         out_shape=(shape(rows, LANES), shape(rows, LANES)),
-        in_specs=[SMEM] * 3 + [VMEM] * 2 + [HBM] * 2,
+        in_specs=[SMEM] * 3 + [VMEM] + [HBM] * 2,
         out_specs=[VMEM] * 2,
         scratch_shapes=[
             pltpu.VMEM((STATES * N, G * N), BF16),
@@ -369,8 +387,8 @@
         ],
         compiler_params=params(FIELD_GRANT),
         cost_estimate=cost(3_000_000_000, 6 << 20),
-        name="both_fields",
-    )(source, term, valid, everyone, own, zh, zl)
+        name="pair_fields",
+    )(source, term, valid, everyone, zh, zl)
 
 
 def pair_action(source, term, valid, cv, everyone, c3, c2, act):
@@ -393,10 +411,21 @@
     )(source, term, valid, cv, everyone, c3, c2, act)
 
 
+def merge(mine, theirs, own):
+    return pl.pallas_call(
+        merge_kernel,
+        out_shape=shape(N // 2 * ALL_TILES, LANES),
+        in_specs=[VMEM] * 3,
+        out_specs=pl.BlockSpec(),
+        compiler_params=params(8),
+        name="merge",
+    )(mine, theirs, own)
+
+
 def total(parts):
     return pl.pallas_call(
         total_kernel,
-        out_shape=(shape(OWN_TILES, LANES), shape(SLOTS // 2, LANES)),
+        out_shape=(shape(OWN_TILES, LANES), shape(PAIR_TILES, LANES)),
         in_specs=[pl.BlockSpec()],
         out_specs=(pl.BlockSpec(), pl.BlockSpec()),
         compiler_params=params(8),
@@ -421,23 +450,41 @@
     return source, term, valid
 
 
+def other_core(value):
+    return lax.ppermute(value, "core", [(0, 1), (1, 0)])
+
+
+def reduce_own(mine, other):
+    x = lax.axis_index("x")
+    tiles = (mine + other_core(other)).reshape(2, 2, LAST_TILES, N // 2, LANES)
+    for axis, bit in ((1, 1), (0, 2)):
+        mine_here = (x // bit) % 2
+        keep = lax.dynamic_index_in_dim(tiles, mine_here, axis, False)
+        send = lax.dynamic_index_in_dim(tiles, 1 - mine_here, axis, False)
+        tiles = keep + lax.ppermute(send, "x", [(i, i ^ bit) for i in range(X_CHIPS)])
+    return tiles
+
+
 def per_device(coeffs, diag_h2, diag_h3, diag_v1, coup_h2, coup_h3, coup_v1, pairs):
     core = lax.axis_index("core").astype(jnp.int32)[None]
     to_all, plain, mine_first = arrange(core, tile_rows(coeffs[0]))
     everyone = lax.all_to_all(to_all, "state", 0, 0, tiled=True)
     listed = read_list(pairs, lax.axis_index("state"))
     c3 = tile_rows(coup_h3)
-    act, own, zh, zl = own_part(
+    act, own_mine, own_other, zh, zl = own_part(
         diag_v1[0], coup_v1, plain, mine_first, tile_rows(diag_h3[0]), tile_rows(diag_h2[0]), c3
     )
-    mine, other = both_fields(*listed, everyone, own, zh, zl)
-    sums = mine + lax.ppermute(other, "core", [(0, 1), (1, 0)])
+    everyone, own_columns = lax.optimization_barrier(
+        (everyone, reduce_own(own_mine, own_other))
+    )
+    pair_mine, pair_other = pair_fields(*listed, everyone, zh, zl)
+    sums = merge(pair_mine, other_core(pair_other), own_columns)
     parts = lax.all_to_all(
-        sums.reshape(N // 2, ALL_TILES, LANES), ("z", "x"), 0, 0, tiled=True
+        sums.reshape(N // 2, 1, ALL_TILES * LANES), ("z", "x"), 0, 0, tiled=True
     )
     out = pair_action(*listed, coup_v1, everyone, c3, tile_rows(coup_h2), act)
     action = out.reshape(N // 2, G, LANES).transpose(1, 0, 2).reshape(1, G, N * N)
-    own_row, pair_row = total(parts)
+    own_row, pair_row = total(parts.reshape(N // 2 * ALL_TILES, LANES))
     return action, own_row.reshape(1, 1, TERMS * N), pair_row.reshape(1, 1, SLOTS * N)
 
 

time: 85.5 us -> 80.8 us (0.945)
  waiting for transfers between devices: 29.8 us -> 18.1 us
  starting transfers between devices: 25 us -> 32.7 us
    all_to_all x1, waiting for transfers between devices: 17.1 us -> 0.01 us  [per_device(): everyone = lax.all_to_all(to_all, 'state', 0, 0, tiled=True)]
    ppermute x1 -> x4, starting transfers between devices: 4.44 us -> 13.6 us  [the longest x2 8.8 us: other_core(): return lax.ppermute(value, 'core', [(0, 1), (1, 0)])]
    ppermute x1 -> x4, waiting for transfers between devices: 1.7 us -> 10.4 us  [the longest x2 8.01 us: reduce_own(): lax.ppermute(send, 'x', [(i, i ^ bit) for i in range(X_CHIPS)])]
    all_to_all x1, waiting for transfers between devices: 11 us -> 7.7 us  [per_device(): lax.all_to_all(sums.reshape(N // 2, 1, ALL_TILES * LANES), ('z', 'x'), 0,...]
    all_to_all x1, starting transfers between devices: 12.9 us -> 11.5 us  [per_device(): lax.all_to_all(sums.reshape(N // 2, 1, ALL_TILES * LANES), ('z', 'x'), 0,...]
    pallas_call x3 -> x4, Pallas kernels: 17.6 us -> 17.5 us  [the longest x1 9.47 us: own_part(): pl.pallas_call(own_kernel, out_shape=(shape(N, G * N), shape(N // 2 * OWN...]
  transfers between devices with their start and end apart: 3 -> 6, of which waited for: 3 -> 5; matrix products, arithmetic and copies ran while one was open for 1% -> 1% of each run, Pallas kernels for 20% -> 22%
where the time goes in v2:
time: 80.8 us; the launch traced here: 79.9 us
  starting transfers between devices  32.7 us (40%)
  Pallas kernels  26.4 us (33%)
  waiting for transfers between devices  18.1 us (22%)
  local copies, waits for them, and re-layouts  1.24 us (2%)
  between operations  0.89 us (1%)
    all_to_all x1, starting transfers between devices, per_device(): lax.all_to_all(sums.reshape(N // 2, 1, ALL_TILES * LANES), ('z', 'x'), 0,...  11.5 us
    pallas_call x1, Pallas kernels, own_part(): pl.pallas_call(own_kernel, out_shape=(shape(N, G * N), shape(N // 2 * OWN...  9.47 us
    ppermute x2, starting transfers between devices, other_core(): return lax.ppermute(value, 'core', [(0, 1), (1, 0)])  8.8 us
    ppermute x2, waiting for transfers between devices, reduce_own(): lax.ppermute(send, 'x', [(i, i ^ bit) for i in range(X_CHIPS)])  8.01 us
    pallas_call x1, Pallas kernels, pair_action(): pl.pallas_call(pair_kernel, out_shape=shape(PAIRS * N, LANES), in_specs=[...  7.77 us
    all_to_all x1, waiting for transfers between devices, per_device(): lax.all_to_all(sums.reshape(N // 2, 1, ALL_TILES * LANES), ('z', 'x'), 0,...  7.7 us
    all_to_all x1, starting transfers between devices, per_device(): everyone = lax.all_to_all(to_all, 'state', 0, 0, tiled=True)  7.64 us
    pallas_call x1, Pallas kernels, pair_fields(): pl.pallas_call(field_kernel, out_shape=(shape(rows, LANES), shape(rows, L...  6.59 us
  transfers between devices with their start and end apart: 6, of which 5 were waited for; matrix products, arithmetic and copies ran while one was open for 1% of the time, Pallas kernels for 22%

profile of v2, /device:TPU:1, one launch (start us, length us, event | category | flops | bytes accessed | tf_op | source)
XLA Modules:
  0.0 79.9 jit_solution(4918332745335322906)
XLA Ops:
  0.7 0.9 %copy-done = f32[1,8,4096]{2,1,0:T(8,128)S(1)} copy-done((f32[1,8,4096]{2,1,0:T(8,128)S(1)}, f32[1,8,4096]{2,1,0:T(8,128)}, u32[]{:S(2)}) %copy-start) | copy-done | bytes 131096
  1.6 1.1 %arrange.1 = (f32[8,256,128]{2,1,0:T(8,128)}, f32[256,128]{1,0:T(8,128)S(1)}, f32[256,128]{1,0:T(8,128)S(1)}) custom-call(s32[1]{0:T(128)} %bitcast.3.core_ref, f32[256,128]{1,0:T(8,128)S(1)} %bitcast.52), custom_call_target="tpu_custom_call" | custom-call | tf_op jit(solution)/shard_map/arrange/pallas_call | solution.py:338
  2.7 7.6 %all-to-all-start = ((f32[8,256,128]{2,1,0:T(8,128)}), f32[8,256,128]{2,1,0:T(8,128)S(1)}, u32[]{:S(2)}, u32[]{:S(2)}) async-start(f32[8,256,128]{2,1,0:T(8,128)} %get-tuple-element.17), calls=%async_computation | async-start | bytes 2097152 | tf_op jit(solution)/shard_map/all_to_all | solution.py:471
  10.3 0.1 copy.27.cv_ref
  10.4 0.1 copy.25
  10.5 9.5 %own_part.1 = (f32[64,512]{1,0:T(8,128)S(1)}, f32[512,128]{1,0:T(8,128)S(1)}, f32[512,128]{1,0:T(8,128)S(1)}, bf16[2048,512]{1,0:T(8,128)(2,1)}, bf16[2048,512]{1,0:T(8,128)(2,1)}) custom-call(f32[32,8]{1,0:T(8,128)S(1)} %bitcast.53, f32[32,8]{1,0:T(8,128)S(1)} %copy.27.cv_ref, f32[256,128]{1,0:T(8,128)S(1)} %get-tuple-element.18.a_ref, ...), custom_call_target="tpu_custom_call" | custom-call | flops 3000000000 | bytes 8388608 | tf_op jit(solution)/shard_map/own_part/pallas_call | solution.py:350
  20.0 4.7 %collective-permute-start = (f32[512,128]{1,0:T(8,128)S(1)}, f32[512,128]{1,0:T(8,128)S(1)}, u32[]{:S(2)}, u32[]{:S(2)}) collective-permute-start(f32[512,128]{1,0:T(8,128)S(1)} %get-tuple-element.21), channel_id=1, source_target_pairs={{0,1},{1,0},{2,3},{3,2},{4,5},{5,4},{6,7},{7,6},{8,9},{9,8},{10,11... | collective-permute-start | bytes 786440 | tf_op jit(solution)/shard_map/ppermute | solution.py:454
  24.7 1.1 %collective-permute-done = f32[512,128]{1,0:T(8,128)S(1)} collective-permute-done((f32[512,128]{1,0:T(8,128)S(1)}, f32[512,128]{1,0:T(8,128)S(1)}, u32[]{:S(2)}, u32[]{:S(2)}) %collective-permute-start) | collective-permute-done | bytes 262176 | tf_op jit(solution)/shard_map/ppermute | solution.py:454
  25.9 1.9 %collective-permute-start.1 = (f32[2,4,32,128]{3,2,1,0:T(8,128)S(1)}, f32[2,4,32,128]{3,2,1,0:T(8,128)S(1)}, u32[]{:S(2)}, u32[]{:S(2)}) collective-permute-start(f32[2,4,32,128]{3,2,1,0:T(8,128)S(1)} %dynamic-slice_bitcast_fusion), channel_id=1, source_target_pairs={{0,2},{2,0},{4,6},{6,4},{1,3},{3,1},{5,7},{7,5},{8,10},{10,8},{12,... | collective-permute-start | bytes 393224 | tf_op jit(solution)/shard_map/ppermute | solution.py:464
  27.9 0.1 copy.24
  28.0 0.2 reduce-window.8
  28.2 0.1 add_reduce_fusion
  28.3 4.2 %collective-permute-done.1 = f32[2,4,32,128]{3,2,1,0:T(8,128)S(1)} collective-permute-done((f32[2,4,32,128]{3,2,1,0:T(8,128)S(1)}, f32[2,4,32,128]{3,2,1,0:T(8,128)S(1)}, u32[]{:S(2)}, u32[]{:S(2)}) %collective-permute-start.1) | collective-permute-done | bytes 131104 | tf_op jit(solution)/shard_map/ppermute | solution.py:464
  32.5 2.8 %collective-permute-start.2 = (f32[4,32,128]{2,1,0:T(8,128)S(1)}, f32[4,32,128]{2,1,0:T(8,128)S(1)}, u32[]{:S(2)}, u32[]{:S(2)}) collective-permute-start(f32[4,32,128]{2,1,0:T(8,128)S(1)} %dynamic-slice_bitcast_fusion.1), channel_id=1, source_target_pairs={{0,4},{2,6},{4,0},{6,2},{1,5},{3,7},{5,1},{7,3},{8,12},{10,14},{12... | collective-permute-start | bytes 196616 | tf_op jit(solution)/shard_map/ppermute | solution.py:464
  35.3 0.1 convert_reduce_fusion
  35.5 3.8 %collective-permute-done.2 = f32[4,32,128]{2,1,0:T(8,128)S(1)} collective-permute-done((f32[4,32,128]{2,1,0:T(8,128)S(1)}, f32[4,32,128]{2,1,0:T(8,128)S(1)}, u32[]{:S(2)}, u32[]{:S(2)}) %collective-permute-start.2) | collective-permute-done | bytes 65568 | tf_op jit(solution)/shard_map/ppermute | solution.py:464
  39.3 6.6 %pair_fields.1 = (f32[768,128]{1,0:T(8,128)S(1)}, f32[768,128]{1,0:T(8,128)S(1)}) custom-call(s32[48]{0:T(128)S(1)} %get-tuple-element.33.source_ref, s32[48]{0:T(128)S(1)} %get-tuple-element.32.term_ref, s32[48]{0:T(128)S(1)} %get-tuple-element.31.valid_ref, f32[8,256,128]{2,1,0:T(8,128)S(1)} %all-to-all-done.all_ref, ...), custom_call_target="tpu_custom_call" | custom-call | flops 3000000000 | bytes 6291456 | tf_op jit(solution)/shard_map/pair_fields/pallas_call | solution.py:376
  46.0 4.1 %collective-permute-start.3 = (f32[768,128]{1,0:T(8,128)S(1)}, f32[768,128]{1,0:T(8,128)S(1)}, u32[]{:S(2)}, u32[]{:S(2)}) collective-permute-start(f32[768,128]{1,0:T(8,128)S(1)} %get-tuple-element.27), channel_id=1, source_target_pairs={{0,1},{1,0},{2,3},{3,2},{4,5},{5,4},{6,7},{7,6},{8,9},{9,8},{10,11... | collective-permute-start | bytes 1179656 | tf_op jit(solution)/shard_map/ppermute | solution.py:454
  50.1 1.3 %collective-permute-done.3.theirs_ref = f32[768,128]{1,0:T(8,128)S(1)} collective-permute-done((f32[768,128]{1,0:T(8,128)S(1)}, f32[768,128]{1,0:T(8,128)S(1)}, u32[]{:S(2)}, u32[]{:S(2)}) %collective-permute-start.3) | collective-permute-done | bytes 393248 | tf_op jit(solution)/shard_map/ppermute | solution.py:454
  51.4 0.8 %merge.1 = f32[896,128]{1,0:T(8,128)} custom-call(f32[768,128]{1,0:T(8,128)S(1)} %get-tuple-element.26.mine_ref, f32[768,128]{1,0:T(8,128)S(1)} %collective-permute-done.3.theirs_ref, f32[4,32,128]{2,1,0:T(8,128)S(1)} %bitcast_add_fusion.1.own_ref), custom_call_target="tpu_custom_call" | custom-call | tf_op jit(solution)/shard_map/merge/pallas_call | solution.py:415
  52.2 11.5 %all-to-all-start.1 = ((f32[32,1,3584]{2,1,0:T(1,128)}), f32[32,1,3584]{2,1,0:T(1,128)S(1)}, u32[]{:S(2)}, u32[]{:S(2)}) async-start(f32[32,1,3584]{2,1,0:T(1,128)} %bitcast.28), calls=%async_computation.1 | async-start | bytes 917504 | tf_op jit(solution)/shard_map/all_to_all | solution.py:482
  63.8 7.8 %pair_action.1 = f32[256,128]{1,0:T(8,128)} custom-call(s32[48]{0:T(128)S(1)} %get-tuple-element.33.source_ref, s32[48]{0:T(128)S(1)} %get-tuple-element.32.term_ref, s32[48]{0:T(128)S(1)} %get-tuple-element.31.valid_ref, f32[32,8]{1,0:T(8,128)S(1)} %copy.27.cv_ref, f32[8,256,128]{2,1,0:T(8,128)S(1)} %all-to-all-done.all_ref, f32[1024,128]{1,0:T(8,128)S(1)} %bitcast.57, ...), custom_call_target="tpu_custom_call" | custom-call | flops 3000000000 | bytes 4194304 | tf_op jit(solution)/shard_map/pair_action/pallas_call | solution.py:395
  71.5 7.7 %all-to-all-done.1 = f32[32,1,3584]{2,1,0:T(1,128)S(1)} async-done(((f32[32,1,3584]{2,1,0:T(1,128)}), f32[32,1,3584]{2,1,0:T(1,128)S(1)}, u32[]{:S(2)}, u32[]{:S(2)}) %all-to-all-start.1) | async-done | bytes 458784 | tf_op jit(solution)/shard_map/all_to_all | solution.py:482
  79.2 0.6 total.1
  (23 shorter events, 0.1 us)
Async XLA Ops:
  0.6 9.7 %copy-start.5 = (f32[32,8]{0,1:T(8,128)S(1)}, f32[32,8]{0,1:T(8,128)}, u32[]{:S(2)}) copy-start(f32[32,8]{0,1:T(8,128)} %param.14) | copy-start | bytes 3076
  0.6 9.8 %copy-start.6 = (f32[1,32,8]{1,2,0:T(8,128)S(1)}, f32[1,32,8]{1,2,0:T(8,128)}, u32[]{:S(2)}) copy-start(f32[1,32,8]{1,2,0:T(8,128)} %param.11) | copy-start | bytes 3076
  0.7 0.9 %copy-start = (f32[1,8,4096]{2,1,0:T(8,128)S(1)}, f32[1,8,4096]{2,1,0:T(8,128)}, u32[]{:S(2)}) copy-start(f32[1,8,4096]{2,1,0:T(8,128)} %param.8) | copy-start | bytes 393220
  1.6 8.9 %copy-start.1 = (f32[1,32,4096]{2,1,0:T(8,128)S(1)}, f32[1,32,4096]{2,1,0:T(8,128)}, u32[]{:S(2)}) copy-start(f32[1,32,4096]{2,1,0:T(8,128)} %param.10) | copy-start | bytes 1572868
  1.6 8.9 %copy-start.2 = (f32[1,32,4096]{2,1,0:T(8,128)S(1)}, f32[1,32,4096]{2,1,0:T(8,128)}, u32[]{:S(2)}) copy-start(f32[1,32,4096]{2,1,0:T(8,128)} %param.9) | copy-start | bytes 1572868
  2.7 36.6 %all-to-all-start = ((f32[8,256,128]{2,1,0:T(8,128)}), f32[8,256,128]{2,1,0:T(8,128)S(1)}, u32[]{:S(2)}, u32[]{:S(2)}) async-start(f32[8,256,128]{2,1,0:T(8,128)} %get-tuple-element.17), calls=%async_computation | async-start | bytes 2097152 | tf_op jit(solution)/shard_map/all_to_all | solution.py:471
  10.5 14.2 %copy-start.7 = (s32[128,3]{0,1:T(4,128)S(1)}, s32[128,3]{0,1:T(4,128)}, u32[]{:S(2)}) copy-start(s32[128,3]{0,1:T(4,128)} %param.15) | copy-start | bytes 4612
  20.0 5.8 %collective-permute-start = (f32[512,128]{1,0:T(8,128)S(1)}, f32[512,128]{1,0:T(8,128)S(1)}, u32[]{:S(2)}, u32[]{:S(2)}) collective-permute-start(f32[512,128]{1,0:T(8,128)S(1)} %get-tuple-element.21), channel_id=1, source_target_pairs={{0,1},{1,0},{2,3},{3,2},{4,5},{5,4},{6,7},{7,6},{8,9},{9,8},{10,11... | collective-permute-start | bytes 786440 | tf_op jit(solution)/shard_map/ppermute | solution.py:454
  25.9 6.6 %collective-permute-start.1 = (f32[2,4,32,128]{3,2,1,0:T(8,128)S(1)}, f32[2,4,32,128]{3,2,1,0:T(8,128)S(1)}, u32[]{:S(2)}, u32[]{:S(2)}) collective-permute-start(f32[2,4,32,128]{3,2,1,0:T(8,128)S(1)} %dynamic-slice_bitcast_fusion), channel_id=1, source_target_pairs={{0,2},{2,0},{4,6},{6,4},{1,3},{3,1},{5,7},{7,5},{8,10},{10,8},{12,... | collective-permute-start | bytes 393224 | tf_op jit(solution)/shard_map/ppermute | solution.py:464
  32.5 6.8 %collective-permute-start.2 = (f32[4,32,128]{2,1,0:T(8,128)S(1)}, f32[4,32,128]{2,1,0:T(8,128)S(1)}, u32[]{:S(2)}, u32[]{:S(2)}) collective-permute-start(f32[4,32,128]{2,1,0:T(8,128)S(1)} %dynamic-slice_bitcast_fusion.1), channel_id=1, source_target_pairs={{0,4},{2,6},{4,0},{6,2},{1,5},{3,7},{5,1},{7,3},{8,12},{10,14},{12... | collective-permute-start | bytes 196616 | tf_op jit(solution)/shard_map/ppermute | solution.py:464
  45.9 17.8 %copy-start.3 = (f32[32,4096]{1,0:T(8,128)S(1)}, f32[32,4096]{1,0:T(8,128)}, u32[]{:S(2)}) copy-start(f32[32,4096]{1,0:T(8,128)} %param.13) | copy-start | bytes 1572868
  45.9 17.8 %copy-start.4 = (f32[32,4096]{1,0:T(8,128)S(1)}, f32[32,4096]{1,0:T(8,128)}, u32[]{:S(2)}) copy-start(f32[32,4096]{1,0:T(8,128)} %param.12) | copy-start | bytes 1572868
  46.0 5.5 %collective-permute-start.3 = (f32[768,128]{1,0:T(8,128)S(1)}, f32[768,128]{1,0:T(8,128)S(1)}, u32[]{:S(2)}, u32[]{:S(2)}) collective-permute-start(f32[768,128]{1,0:T(8,128)S(1)} %get-tuple-element.27), channel_id=1, source_target_pairs={{0,1},{1,0},{2,3},{3,2},{4,5},{5,4},{6,7},{7,6},{8,9},{9,8},{10,11... | collective-permute-start | bytes 1179656 | tf_op jit(solution)/shard_map/ppermute | solution.py:454
  52.2 27.0 %all-to-all-start.1 = ((f32[32,1,3584]{2,1,0:T(1,128)}), f32[32,1,3584]{2,1,0:T(1,128)S(1)}, u32[]{:S(2)}, u32[]{:S(2)}) async-start(f32[32,1,3584]{2,1,0:T(1,128)} %bitcast.28), calls=%async_computation.1 | async-start | bytes 917504 | tf_op jit(solution)/shard_map/all_to_all | solution.py:482

commit v3 on v2

--- a/solution.py
+++ b/solution.py
@@ -1,3 +1,5 @@
+import functools
+
 import jax
 import jax.numpy as jnp
 from jax import lax
@@ -14,9 +16,10 @@
 SLOTS = 48
 OWN_TILES = TERMS // 2
 PAIR_TILES = SLOTS // 2
+ALL_TILES = OWN_TILES + PAIR_TILES
 X_CHIPS = 4
-LAST_TILES = OWN_TILES // X_CHIPS
-ALL_TILES = PAIR_TILES + LAST_TILES
+Z_CHIPS = 8
+HALF_SLOTS = SLOTS // 2
 UNROLL = 4
 CHUNKS = TERMS // 4
 F32 = jnp.float32
@@ -125,8 +128,13 @@
         odd = jnp.where(left, pltpu.roll(one, N, 1), two)
         plain_ref[pl.ds(pair * N, N // 2, stride=2), :] = even
         plain_ref[pl.ds(pair * N + 1, N // 2, stride=2), :] = odd
-        mine_ref[pair * N : pair * N + N // 2, :] = jnp.where(is_first, even, odd)
-        mine_ref[pair * N + N // 2 : (pair + 1) * N, :] = jnp.where(is_first, odd, even)
+        for x in range(X_CHIPS):
+            first = plain_ref[pl.ds(pair * N + 2 * x, Z_CHIPS, stride=2 * X_CHIPS), :]
+            second = plain_ref[pl.ds(pair * N + 2 * x + 1, Z_CHIPS, stride=2 * X_CHIPS), :]
+            start = pair * N + x * Z_CHIPS
+            mine_ref[start : start + Z_CHIPS, :] = jnp.where(is_first, first, second)
+            start += N // 2
+            mine_ref[start : start + Z_CHIPS, :] = jnp.where(is_first, second, first)
     for q in range(STATES):
         out_ref[q] = plain_ref[...]
 
@@ -256,8 +264,8 @@
     lax.fori_loop(0, PAIR_TILES // 8, slot_pairs, 0)
 
 
-def pair_kernel(source_ref, term_ref, valid_ref, cv_ref, all_ref, c3_ref, c2_ref, act_ref,
-                out_ref, left_all_ref, ops_ref, left_ref, wh_ref, wl_ref, sum_ref):
+def pair_kernel(base, source_ref, term_ref, valid_ref, cv_ref, all_ref, c3_ref, c2_ref, act_ref,
+                out_ref, left_all_ref, ops_ref, left_ref, wh_ref, wl_ref, *sum_ref):
     for q in range(STATES):
         left_all_ref[q] = split_lanes(all_ref[q])
     spread(c2_ref, ops_ref)
@@ -265,25 +273,29 @@
     def left_tiles(i, carry):
         for u in range(2):
             tile = 2 * i + u
-            first, second = term_ref[2 * tile], term_ref[2 * tile + 1]
+            first, second = term_ref[base + 2 * tile], term_ref[base + 2 * tile + 1]
             put_left((ops_ref[first], ops_ref[second]), tile, left_ref)
         return carry
 
-    lax.fori_loop(0, SLOTS // 4, left_tiles, 0)
+    lax.fori_loop(0, HALF_SLOTS // 4, left_tiles, 0)
     spread(c3_ref, ops_ref)
 
     def slot_terms(j, carry):
         for u in range(UNROLL):
             slot = j * UNROLL + u
-            k = term_ref[slot]
-            product = dot_nt(left_all_ref[source_ref[slot]], tile_nt(ops_ref[k]))
-            is_valid = valid_ref[slot] == 1
+            k = term_ref[base + slot]
+            product = dot_nt(left_all_ref[source_ref[base + slot]], tile_nt(ops_ref[k]))
+            is_valid = valid_ref[base + slot] == 1
             weights = [jnp.where(is_valid, cv_ref[k, g], 0.0) for g in range(G)]
             put_term(product, weights, slot, wh_ref, wl_ref)
         return carry
 
-    lax.fori_loop(0, SLOTS // UNROLL, slot_terms, 0)
+    lax.fori_loop(0, HALF_SLOTS // UNROLL, slot_terms, 0)
     action = act_ref[...] + act_on(left_ref, wh_ref, wl_ref)
+    if base == 0:
+        out_ref[...] = action
+        return
+    (sum_ref,) = sum_ref
     left = is_left(N // 2)
     for pair in range(PAIRS):
         sum_ref[pair * N : (pair + 1) * N, :] = action[:, pair * LANES : (pair + 1) * LANES]
@@ -295,27 +307,22 @@
         out_ref[pl.ds(2 * pair + 1, N // 2, stride=G), :] = two
 
 
-def merge_kernel(mine_ref, theirs_ref, own_ref, out_ref):
-    for a in range(N // 2):
-        here = slice(a * PAIR_TILES, (a + 1) * PAIR_TILES)
-        out_ref[a * ALL_TILES : a * ALL_TILES + PAIR_TILES, :] = mine_ref[here, :] + theirs_ref[here, :]
-    for r in range(LAST_TILES):
-        out_ref[pl.ds(PAIR_TILES + r, N // 2, stride=ALL_TILES), :] = own_ref[r]
+def merge_kernel(parts_ref, own_ref, out_ref):
+    for z in range(Z_CHIPS):
+        total = parts_ref[0, z * PAIR_TILES : (z + 1) * PAIR_TILES, :]
+        for x in range(1, X_CHIPS):
+            total = total + parts_ref[x, z * PAIR_TILES : (z + 1) * PAIR_TILES, :]
+        out_ref[z * ALL_TILES : z * ALL_TILES + PAIR_TILES, :] = total
+    for i in range(OWN_TILES):
+        out_ref[pl.ds(PAIR_TILES + i, Z_CHIPS, stride=ALL_TILES), :] = own_ref[i]
 
 
 def total_kernel(parts_ref, own_ref, pair_ref):
-    def part(i, first, count):
-        return parts_ref[i * ALL_TILES + first : i * ALL_TILES + first + count, :]
-
-    total = part(0, 0, PAIR_TILES)
-    for i in range(1, N // 2):
-        total = total + part(i, 0, PAIR_TILES)
-    pair_ref[...] = total
-    for x in range(X_CHIPS):
-        total = part(x, PAIR_TILES, LAST_TILES)
-        for z in range(1, N // 2 // X_CHIPS):
-            total = total + part(z * X_CHIPS + x, PAIR_TILES, LAST_TILES)
-        own_ref[x * LAST_TILES : (x + 1) * LAST_TILES, :] = total
+    total = parts_ref[0]
+    for z in range(1, Z_CHIPS):
+        total = total + parts_ref[z]
+    pair_ref[...] = total[:PAIR_TILES]
+    own_ref[...] = total[PAIR_TILES:]
 
 
 def shape(*dims, dtype=F32):
@@ -391,35 +398,36 @@
     )(source, term, valid, everyone, zh, zl)
 
 
-def pair_action(source, term, valid, cv, everyone, c3, c2, act):
+def pair_action(base, source, term, valid, cv, everyone, c3, c2, act):
+    last = [pltpu.VMEM((PAIRS * N, LANES), F32)] if base else []
     return pl.pallas_call(
-        pair_kernel,
-        out_shape=shape(PAIRS * N, LANES),
+        functools.partial(pair_kernel, base),
+        out_shape=shape(PAIRS * N, LANES) if base else shape(N, G * N),
         in_specs=[SMEM] * 4 + [VMEM] * 4,
-        out_specs=pl.BlockSpec(),
+        out_specs=pl.BlockSpec() if base else VMEM,
         scratch_shapes=[
             pltpu.VMEM((STATES, PAIRS * N, 2 * LANES), BF16),
             pltpu.VMEM((TERMS, N, LANES), F32),
-            pltpu.VMEM((LANES, SLOTS * N), BF16),
-            pltpu.VMEM((SLOTS * N, G * N), BF16),
-            pltpu.VMEM((SLOTS * N, G * N), BF16),
-            pltpu.VMEM((PAIRS * N, LANES), F32),
-        ],
+            pltpu.VMEM((LANES, HALF_SLOTS * N), BF16),
+            pltpu.VMEM((HALF_SLOTS * N, G * N), BF16),
+            pltpu.VMEM((HALF_SLOTS * N, G * N), BF16),
+        ]
+        + last,
         compiler_params=params(24),
-        cost_estimate=cost(3_000_000_000, 4 << 20),
-        name="pair_action",
+        cost_estimate=cost(1_500_000_000, 4 << 20),
+        name="pair_action_last" if base else "pair_action_first",
     )(source, term, valid, cv, everyone, c3, c2, act)
 
 
-def merge(mine, theirs, own):
+def merge(parts, own):
     return pl.pallas_call(
         merge_kernel,
-        out_shape=shape(N // 2 * ALL_TILES, LANES),
-        in_specs=[VMEM] * 3,
+        out_shape=shape(Z_CHIPS * ALL_TILES, LANES),
+        in_specs=[VMEM] * 2,
         out_specs=pl.BlockSpec(),
         compiler_params=params(8),
         name="merge",
-    )(mine, theirs, own)
+    )(parts, own)
 
 
 def total(parts):
@@ -456,8 +464,8 @@
 
 def reduce_own(mine, other):
     x = lax.axis_index("x")
-    tiles = (mine + other_core(other)).reshape(2, 2, LAST_TILES, N // 2, LANES)
-    for axis, bit in ((1, 1), (0, 2)):
+    tiles = (mine + other_core(other)).reshape(OWN_TILES, 2, 2, Z_CHIPS, LANES)
+    for axis, bit in ((2, 1), (1, 2)):
         mine_here = (x // bit) % 2
         keep = lax.dynamic_index_in_dim(tiles, mine_here, axis, False)
         send = lax.dynamic_index_in_dim(tiles, 1 - mine_here, axis, False)
@@ -474,17 +482,21 @@
     act, own_mine, own_other, zh, zl = own_part(
         diag_v1[0], coup_v1, plain, mine_first, tile_rows(diag_h3[0]), tile_rows(diag_h2[0]), c3
     )
-    everyone, own_columns = lax.optimization_barrier(
+    everyone, own_rows = lax.optimization_barrier(
         (everyone, reduce_own(own_mine, own_other))
     )
     pair_mine, pair_other = pair_fields(*listed, everyone, zh, zl)
-    sums = merge(pair_mine, other_core(pair_other), own_columns)
+    sums = pair_mine + other_core(pair_other)
     parts = lax.all_to_all(
-        sums.reshape(N // 2, 1, ALL_TILES * LANES), ("z", "x"), 0, 0, tiled=True
-    )
-    out = pair_action(*listed, coup_v1, everyone, c3, tile_rows(coup_h2), act)
+        sums.reshape(X_CHIPS, Z_CHIPS * PAIR_TILES, LANES), "x", 0, 0, tiled=True
+    )
+    c2 = tile_rows(coup_h2)
+    act = pair_action(0, *listed, coup_v1, everyone, c3, c2, act)
+    act, sums = lax.optimization_barrier((act, merge(parts, own_rows)))
+    parts = lax.all_to_all(sums.reshape(Z_CHIPS, ALL_TILES, LANES), "z", 0, 0, tiled=True)
+    out = pair_action(HALF_SLOTS, *listed, coup_v1, everyone, c3, c2, act)
     action = out.reshape(N // 2, G, LANES).transpose(1, 0, 2).reshape(1, G, N * N)
-    own_row, pair_row = total(parts.reshape(N // 2 * ALL_TILES, LANES))
+    own_row, pair_row = total(parts)
     return action, own_row.reshape(1, 1, TERMS * N), pair_row.reshape(1, 1, SLOTS * N)
 
 

time: 80.8 us -> 83.8 us (1.037)
  the two profiles are of different devices: /device:TPU:1 before, /device:TPU:8 now
where the time goes in v3:
time: 83.8 us; the launch traced here: 83.3 us
  starting transfers between devices  30.9 us (37%)
  Pallas kernels  27.7 us (33%)
  waiting for transfers between devices  21.3 us (25%)
  other arithmetic  1.27 us (2%)
  local copies, waits for them, and re-layouts  1.26 us (2%)
  between operations  0.9 us (1%)
    pallas_call x1, Pallas kernels, own_part(): pl.pallas_call(own_kernel, out_shape=(shape(N, G * N), shape(N // 2 * OWN...  9.47 us
    ppermute x2, waiting for transfers between devices, reduce_own(): lax.ppermute(send, 'x', [(i, i ^ bit) for i in range(X_CHIPS)])  9.34 us
    all_to_all x1, starting transfers between devices, per_device(): everyone = lax.all_to_all(to_all, 'state', 0, 0, tiled=True)  9.25 us
    pallas_call x2, Pallas kernels, pair_action(): pl.pallas_call(functools.partial(pair_kernel, base), out_shape=shape(PAIR...  9.22 us
    all_to_all x1, starting transfers between devices, per_device(): lax.all_to_all(sums.reshape(Z_CHIPS, ALL_TILES, LANES), 'z', 0, 0, tiled=...  9.19 us
    pallas_call x1, Pallas kernels, pair_fields(): pl.pallas_call(field_kernel, out_shape=(shape(rows, LANES), shape(rows, L...  6.59 us
    ppermute x2, starting transfers between devices, reduce_own(): lax.ppermute(send, 'x', [(i, i ^ bit) for i in range(X_CHIPS)])  5.15 us
    all_to_all x1, waiting for transfers between devices, per_device(): lax.all_to_all(sums.reshape(Z_CHIPS, ALL_TILES, LANES), 'z', 0, 0, tiled=...  4.44 us
  transfers between devices with their start and end apart: 7, of which 6 were waited for; matrix products, arithmetic and copies ran while one was open for 1% of the time, Pallas kernels for 22%

profile of v3, /device:TPU:8, one launch (start us, length us, event | category | flops | bytes accessed | tf_op | source)
XLA Modules:
  0.0 83.3 jit_solution(9355481513993520228)
XLA Ops:
  0.7 0.9 %copy-done = f32[1,8,4096]{2,1,0:T(8,128)S(1)} copy-done((f32[1,8,4096]{2,1,0:T(8,128)S(1)}, f32[1,8,4096]{2,1,0:T(8,128)}, u32[]{:S(2)}) %copy-start) | copy-done | bytes 131096
  1.6 1.1 %arrange.1 = (f32[8,256,128]{2,1,0:T(8,128)}, f32[256,128]{1,0:T(8,128)S(1)}, f32[256,128]{1,0:T(8,128)S(1)}) custom-call(s32[1]{0:T(128)} %bitcast.3.core_ref, f32[256,128]{1,0:T(8,128)S(1)} %bitcast.52), custom_call_target="tpu_custom_call" | custom-call | tf_op jit(solution)/shard_map/arrange/pallas_call | solution.py:345
  2.7 9.3 %all-to-all-start = ((f32[8,256,128]{2,1,0:T(8,128)}), f32[8,256,128]{2,1,0:T(8,128)S(1)}, u32[]{:S(2)}, u32[]{:S(2)}) async-start(f32[8,256,128]{2,1,0:T(8,128)} %get-tuple-element.19), calls=%async_computation | async-start | bytes 2097152 | tf_op jit(solution)/shard_map/all_to_all | solution.py:479
  12.1 9.5 %own_part.1 = (f32[64,512]{1,0:T(8,128)S(1)}, f32[512,128]{1,0:T(8,128)S(1)}, f32[512,128]{1,0:T(8,128)S(1)}, bf16[2048,512]{1,0:T(8,128)(2,1)}, bf16[2048,512]{1,0:T(8,128)(2,1)}) custom-call(f32[32,8]{1,0:T(8,128)S(1)} %bitcast.53, f32[32,8]{1,0:T(8,128)S(1)} %copy.31.cv_ref, f32[256,128]{1,0:T(8,128)S(1)} %get-tuple-element.20.a_ref, ...), custom_call_target="tpu_custom_call" | custom-call | flops 3000000000 | bytes 8388608 | tf_op jit(solution)/shard_map/own_part/pallas_call | solution.py:357
  21.6 1.9 %collective-permute-start = (f32[512,128]{1,0:T(8,128)S(1)}, f32[512,128]{1,0:T(8,128)S(1)}, u32[]{:S(2)}, u32[]{:S(2)}) collective-permute-start(f32[512,128]{1,0:T(8,128)S(1)} %get-tuple-element.23), channel_id=1, source_target_pairs={{0,1},{1,0},{2,3},{3,2},{4,5},{5,4},{6,7},{7,6},{8,9},{9,8},{10,11... | collective-permute-start | bytes 786440 | tf_op jit(solution)/shard_map/ppermute | solution.py:462
  23.6 1.5 %collective-permute-done = f32[512,128]{1,0:T(8,128)S(1)} collective-permute-done((f32[512,128]{1,0:T(8,128)S(1)}, f32[512,128]{1,0:T(8,128)S(1)}, u32[]{:S(2)}, u32[]{:S(2)}) %collective-permute-start) | collective-permute-done | bytes 262176 | tf_op jit(solution)/shard_map/ppermute | solution.py:462
  25.1 1.9 %collective-permute-start.1 = (f32[16,2,8,128]{3,2,0,1:T(8,128)S(1)}, f32[16,2,8,128]{3,2,0,1:T(8,128)S(1)}, u32[]{:S(2)}, u32[]{:S(2)}) collective-permute-start(f32[16,2,8,128]{3,2,0,1:T(8,128)S(1)} %bitcast.62), channel_id=1, source_target_pairs={{0,2},{2,0},{4,6},{6,4},{1,3},{3,1},{5,7},{7,5},{8,10},{10,8},{12,... | collective-permute-start | bytes 393224 | tf_op jit(solution)/shard_map/ppermute | solution.py:472
  27.2 0.2 reduce-window.8
  27.5 5.1 %collective-permute-done.1 = f32[16,2,8,128]{3,2,0,1:T(8,128)S(1)} collective-permute-done((f32[16,2,8,128]{3,2,0,1:T(8,128)S(1)}, f32[16,2,8,128]{3,2,0,1:T(8,128)S(1)}, u32[]{:S(2)}, u32[]{:S(2)}) %collective-permute-start.1) | collective-permute-done | bytes 131104 | tf_op jit(solution)/shard_map/ppermute | solution.py:472
  32.6 3.2 %collective-permute-start.2 = (f32[16,8,128]{2,1,0:T(8,128)S(1)}, f32[16,8,128]{2,1,0:T(8,128)S(1)}, u32[]{:S(2)}, u32[]{:S(2)}) collective-permute-start(f32[16,8,128]{2,1,0:T(8,128)S(1)} %dynamic-slice_bitcast_fusion), channel_id=1, source_target_pairs={{0,4},{2,6},{4,0},{6,2},{1,5},{3,7},{5,1},{7,3},{8,12},{10,14},{12... | collective-permute-start | bytes 196616 | tf_op jit(solution)/shard_map/ppermute | solution.py:472
  35.8 0.1 convert_reduce_fusion
  36.0 4.3 %collective-permute-done.2 = f32[16,8,128]{2,1,0:T(8,128)S(1)} collective-permute-done((f32[16,8,128]{2,1,0:T(8,128)S(1)}, f32[16,8,128]{2,1,0:T(8,128)S(1)}, u32[]{:S(2)}, u32[]{:S(2)}) %collective-permute-start.2) | collective-permute-done | bytes 65568 | tf_op jit(solution)/shard_map/ppermute | solution.py:472
  40.3 6.6 %pair_fields.1 = (f32[768,128]{1,0:T(8,128)S(1)}, f32[768,128]{1,0:T(8,128)S(1)}) custom-call(s32[48]{0:T(128)S(1)} %get-tuple-element.37.source_ref, s32[48]{0:T(128)S(1)} %get-tuple-element.36.term_ref, s32[48]{0:T(128)S(1)} %get-tuple-element.35.valid_ref, f32[8,256,128]{2,1,0:T(8,128)S(1)} %all-to-all-done.all_ref, ...), custom_call_target="tpu_custom_call" | custom-call | flops 3000000000 | bytes 6291456 | tf_op jit(solution)/shard_map/pair_fields/pallas_call | solution.py:383
  46.9 1.9 %collective-permute-start.3 = (f32[768,128]{1,0:T(8,128)S(1)}, f32[768,128]{1,0:T(8,128)S(1)}, u32[]{:S(2)}, u32[]{:S(2)}) collective-permute-start(f32[768,128]{1,0:T(8,128)S(1)} %get-tuple-element.29), channel_id=1, source_target_pairs={{0,1},{1,0},{2,3},{3,2},{4,5},{5,4},{6,7},{7,6},{8,9},{9,8},{10,11... | collective-permute-start | bytes 1179656 | tf_op jit(solution)/shard_map/ppermute | solution.py:462
  48.8 1.7 %collective-permute-done.3 = f32[768,128]{1,0:T(8,128)S(1)} collective-permute-done((f32[768,128]{1,0:T(8,128)S(1)}, f32[768,128]{1,0:T(8,128)S(1)}, u32[]{:S(2)}, u32[]{:S(2)}) %collective-permute-start.3) | collective-permute-done | bytes 393248 | tf_op jit(solution)/shard_map/ppermute | solution.py:462
  50.5 0.8 add.52
  51.3 3.5 %all-to-all-start.1 = ((f32[4,192,128]{2,1,0:T(8,128)}), f32[4,192,128]{2,1,0:T(8,128)S(1)}, u32[]{:S(2)}, u32[]{:S(2)}) async-start(f32[4,192,128]{2,1,0:T(8,128)} %bitcast.29), calls=%async_computation.1 | async-start | bytes 786432 | tf_op jit(solution)/shard_map/all_to_all | solution.py:490
  54.8 4.2 %pair_action_first.1.act_ref = f32[64,512]{1,0:T(8,128)S(1)} custom-call(s32[48]{0:T(128)S(1)} %get-tuple-element.37.source_ref, s32[48]{0:T(128)S(1)} %get-tuple-element.36.term_ref, s32[48]{0:T(128)S(1)} %get-tuple-element.35.valid_ref, f32[32,8]{1,0:T(8,128)S(1)} %copy.31.cv_ref, f32[8,256,128]{2,1,0:T(8,128)S(1)} %all-to-all-done.all_ref, ...), custom_call_target="tpu_custom_call" | custom-call | flops 1500000000 | bytes 4194304 | tf_op jit(solution)/shard_map/pair_action_first/pallas_call | solution.py:403
  59.0 4.4 %all-to-all-done.1.parts_ref = f32[4,192,128]{2,1,0:T(8,128)S(1)} async-done(((f32[4,192,128]{2,1,0:T(8,128)}), f32[4,192,128]{2,1,0:T(8,128)S(1)}, u32[]{:S(2)}, u32[]{:S(2)}) %all-to-all-start.1) | async-done | bytes 393248 | tf_op jit(solution)/shard_map/all_to_all | solution.py:490
  63.4 0.7 merge.1
  64.1 9.2 %all-to-all-start.2 = ((f32[8,40,128]{2,1,0:T(8,128)}), f32[8,40,128]{2,1,0:T(8,128)S(1)}, u32[]{:S(2)}, u32[]{:S(2)}) async-start(f32[8,40,128]{2,1,0:T(8,128)} %bitcast.33), calls=%async_computation.2 | async-start | bytes 327680 | tf_op jit(solution)/shard_map/all_to_all | solution.py:496
  73.3 5.0 %pair_action_last.1 = f32[256,128]{1,0:T(8,128)} custom-call(s32[48]{0:T(128)S(1)} %get-tuple-element.37.source_ref, s32[48]{0:T(128)S(1)} %get-tuple-element.36.term_ref, s32[48]{0:T(128)S(1)} %get-tuple-element.35.valid_ref, f32[32,8]{1,0:T(8,128)S(1)} %copy.31.cv_ref, f32[8,256,128]{2,1,0:T(8,128)S(1)} %all-to-all-done.all_ref, f32[1024,128]{1,0:T(8,128)S(1)} %bitcast.58, ...), custom_call_target="tpu_custom_call" | custom-call | flops 1500000000 | bytes 4194304 | tf_op jit(solution)/shard_map/pair_action_last/pallas_call | solution.py:403
  78.3 4.4 %all-to-all-done.2.parts_ref = f32[8,40,128]{2,1,0:T(8,128)S(1)} async-done(((f32[8,40,128]{2,1,0:T(8,128)}), f32[8,40,128]{2,1,0:T(8,128)S(1)}, u32[]{:S(2)}, u32[]{:S(2)}) %all-to-all-start.2) | async-done | bytes 163872 | tf_op jit(solution)/shard_map/all_to_all | solution.py:496
  82.7 0.6 total.1
  (28 shorter events, 0.5 us)
Async XLA Ops:
  0.6 11.3 %copy-start.5 = (f32[32,8]{0,1:T(8,128)S(1)}, f32[32,8]{0,1:T(8,128)}, u32[]{:S(2)}) copy-start(f32[32,8]{0,1:T(8,128)} %param.14) | copy-start | bytes 3076
  0.6 11.4 %copy-start.6 = (f32[1,32,8]{1,2,0:T(8,128)S(1)}, f32[1,32,8]{1,2,0:T(8,128)}, u32[]{:S(2)}) copy-start(f32[1,32,8]{1,2,0:T(8,128)} %param.11) | copy-start | bytes 3076
  0.7 0.9 %copy-start = (f32[1,8,4096]{2,1,0:T(8,128)S(1)}, f32[1,8,4096]{2,1,0:T(8,128)}, u32[]{:S(2)}) copy-start(f32[1,8,4096]{2,1,0:T(8,128)} %param.8) | copy-start | bytes 393220
  1.6 10.6 %copy-start.1 = (f32[1,32,4096]{2,1,0:T(8,128)S(1)}, f32[1,32,4096]{2,1,0:T(8,128)}, u32[]{:S(2)}) copy-start(f32[1,32,4096]{2,1,0:T(8,128)} %param.10) | copy-start | bytes 1572868
  1.6 10.6 %copy-start.2 = (f32[1,32,4096]{2,1,0:T(8,128)S(1)}, f32[1,32,4096]{2,1,0:T(8,128)}, u32[]{:S(2)}) copy-start(f32[1,32,4096]{2,1,0:T(8,128)} %param.9) | copy-start | bytes 1572868
  2.7 37.6 %all-to-all-start = ((f32[8,256,128]{2,1,0:T(8,128)}), f32[8,256,128]{2,1,0:T(8,128)S(1)}, u32[]{:S(2)}, u32[]{:S(2)}) async-start(f32[8,256,128]{2,1,0:T(8,128)} %get-tuple-element.19), calls=%async_computation | async-start | bytes 2097152 | tf_op jit(solution)/shard_map/all_to_all | solution.py:479
  12.1 11.4 %copy-start.7 = (s32[128,3]{0,1:T(4,128)S(1)}, s32[128,3]{0,1:T(4,128)}, u32[]{:S(2)}) copy-start(s32[128,3]{0,1:T(4,128)} %param.15) | copy-start | bytes 4612
  21.6 3.4 %collective-permute-start = (f32[512,128]{1,0:T(8,128)S(1)}, f32[512,128]{1,0:T(8,128)S(1)}, u32[]{:S(2)}, u32[]{:S(2)}) collective-permute-start(f32[512,128]{1,0:T(8,128)S(1)} %get-tuple-element.23), channel_id=1, source_target_pairs={{0,1},{1,0},{2,3},{3,2},{4,5},{5,4},{6,7},{7,6},{8,9},{9,8},{10,11... | collective-permute-start | bytes 786440 | tf_op jit(solution)/shard_map/ppermute | solution.py:462
  25.1 7.4 %collective-permute-start.1 = (f32[16,2,8,128]{3,2,0,1:T(8,128)S(1)}, f32[16,2,8,128]{3,2,0,1:T(8,128)S(1)}, u32[]{:S(2)}, u32[]{:S(2)}) collective-permute-start(f32[16,2,8,128]{3,2,0,1:T(8,128)S(1)} %bitcast.62), channel_id=1, source_target_pairs={{0,2},{2,0},{4,6},{6,4},{1,3},{3,1},{5,7},{7,5},{8,10},{10,8},{12,... | collective-permute-start | bytes 393224 | tf_op jit(solution)/shard_map/ppermute | solution.py:472
  32.6 7.7 %collective-permute-start.2 = (f32[16,8,128]{2,1,0:T(8,128)S(1)}, f32[16,8,128]{2,1,0:T(8,128)S(1)}, u32[]{:S(2)}, u32[]{:S(2)}) collective-permute-start(f32[16,8,128]{2,1,0:T(8,128)S(1)} %dynamic-slice_bitcast_fusion), channel_id=1, source_target_pairs={{0,4},{2,6},{4,0},{6,2},{1,5},{3,7},{5,1},{7,3},{8,12},{10,14},{12... | collective-permute-start | bytes 196616 | tf_op jit(solution)/shard_map/ppermute | solution.py:472
  40.3 14.5 %copy-start.3 = (f32[32,4096]{1,0:T(8,128)S(1)}, f32[32,4096]{1,0:T(8,128)}, u32[]{:S(2)}) copy-start(f32[32,4096]{1,0:T(8,128)} %param.13) | copy-start | bytes 1572868
  40.3 14.5 %copy-start.4 = (f32[32,4096]{1,0:T(8,128)S(1)}, f32[32,4096]{1,0:T(8,128)}, u32[]{:S(2)}) copy-start(f32[32,4096]{1,0:T(8,128)} %param.12) | copy-start | bytes 1572868
  46.9 3.6 %collective-permute-start.3 = (f32[768,128]{1,0:T(8,128)S(1)}, f32[768,128]{1,0:T(8,128)S(1)}, u32[]{:S(2)}, u32[]{:S(2)}) collective-permute-start(f32[768,128]{1,0:T(8,128)S(1)} %get-tuple-element.29), channel_id=1, source_target_pairs={{0,1},{1,0},{2,3},{3,2},{4,5},{5,4},{6,7},{7,6},{8,9},{9,8},{10,11... | collective-permute-start | bytes 1179656 | tf_op jit(solution)/shard_map/ppermute | solution.py:462
  51.3 12.1 %all-to-all-start.1 = ((f32[4,192,128]{2,1,0:T(8,128)}), f32[4,192,128]{2,1,0:T(8,128)S(1)}, u32[]{:S(2)}, u32[]{:S(2)}) async-start(f32[4,192,128]{2,1,0:T(8,128)} %bitcast.29), calls=%async_computation.1 | async-start | bytes 786432 | tf_op jit(solution)/shard_map/all_to_all | solution.py:490
  64.1 18.6 %all-to-all-start.2 = ((f32[8,40,128]{2,1,0:T(8,128)}), f32[8,40,128]{2,1,0:T(8,128)S(1)}, u32[]{:S(2)}, u32[]{:S(2)}) async-start(f32[8,40,128]{2,1,0:T(8,128)} %bitcast.33), calls=%async_computation.2 | async-start | bytes 327680 | tf_op jit(solution)/shard_map/all_to_all | solution.py:496

commit v4 on v2

--- a/solution.py
+++ b/solution.py
@@ -131,39 +131,8 @@
         out_ref[q] = plain_ref[...]
 
 
-def own_kernel(v_ref, cv_ref, a_ref, ap_ref, h3_ref, h2_ref, c3_ref,
-               act_ref, mine_ref, other_ref, zh_hbm, zl_hbm,
-               ops_ref, left_ref, wh_ref, wl_ref, zh_ref, zl_ref, sems):
-    def chunk_copies(j):
-        rows = pl.ds(pl.multiple_of(j * UNROLL * N, UNROLL * N), UNROLL * N)
-        return [
-            pltpu.make_async_copy(zh_ref.at[rows, :], zh_hbm.at[rows, :], sems.at[0, j]),
-            pltpu.make_async_copy(zl_ref.at[rows, :], zl_hbm.at[rows, :], sems.at[1, j]),
-        ]
-
-    left_p = split_lanes(ap_ref[...])
-    spread(c3_ref, ops_ref)
-
-    def coupling_terms(j, carry):
-        for u in range(UNROLL):
-            k = j * UNROLL + u
-            product = dot(left_p, tile_nn(ops_ref[k]))
-            put_term(product, [cv_ref[k, g] for g in range(G)], k, zh_ref, zl_ref)
-
-        @pl.when(j > 0)
-        def _():
-            for copy in chunk_copies(j - 1):
-                copy.start()
-
-        return carry
-
-    lax.fori_loop(0, CHUNKS, coupling_terms, 0)
-
-    spread(h2_ref, ops_ref)
-    for i in range(OWN_TILES):
-        put_left((ops_ref[2 * i], ops_ref[2 * i + 1]), i, left_ref)
-    for copy in chunk_copies(CHUNKS - 1):
-        copy.start()
+def own_kernel(v_ref, a_ref, ap_ref, h3_ref, h2_ref,
+               act_ref, mine_ref, other_ref, ops_ref, left_ref, wh_ref, wl_ref):
     spread(h3_ref, ops_ref)
     left = split_lanes(a_ref[...])
 
@@ -175,8 +144,6 @@
         return carry
 
     lax.fori_loop(0, CHUNKS, own_terms, 0)
-    act_ref[...] = act_on(left_ref, wh_ref, wl_ref)
-
     wide = jnp.concatenate([ap_ref[p * N : (p + 1) * N, :] for p in range(PAIRS)], axis=1)
     high, low = split(wide)
     rows_both = jnp.concatenate([high, low], axis=0)
@@ -190,9 +157,44 @@
             mine_ref[rows, :] = field[: N // 2, lanes]
             other_ref[rows, :] = field[N // 2 :, lanes]
 
-    for j in range(CHUNKS):
+    spread(h2_ref, ops_ref)
+    for i in range(OWN_TILES):
+        put_left((ops_ref[2 * i], ops_ref[2 * i + 1]), i, left_ref)
+    act_ref[...] = act_on(left_ref, wh_ref, wl_ref)
+
+
+def turned_kernel(cv_ref, ap_ref, c3_ref, zh_hbm, zl_hbm, ops_ref, zh_ref, zl_ref, sems):
+    def chunk_copies(j):
+        rows = pl.ds(pl.multiple_of(j * UNROLL * N, UNROLL * N), UNROLL * N)
+        return [
+            pltpu.make_async_copy(zh_ref.at[rows, :], zh_hbm.at[rows, :], sems.at[0, j]),
+            pltpu.make_async_copy(zl_ref.at[rows, :], zl_hbm.at[rows, :], sems.at[1, j]),
+        ]
+
+    left_p = split_lanes(ap_ref[...])
+    spread(c3_ref, ops_ref)
+
+    def coupling_terms(j, carry):
+        for u in range(UNROLL):
+            k = j * UNROLL + u
+            product = dot(left_p, tile_nn(ops_ref[k]))
+            put_term(product, [cv_ref[k, g] for g in range(G)], k, zh_ref, zl_ref)
+
+        @pl.when(j > 0)
+        def _():
+            for copy in chunk_copies(j - 1):
+                copy.start()
+
+        return carry
+
+    lax.fori_loop(0, CHUNKS, coupling_terms, 0)
+    for j in range(CHUNKS - 1):
         for copy in chunk_copies(j):
             copy.wait()
+    for copy in chunk_copies(CHUNKS - 1):
+        copy.start()
+    for copy in chunk_copies(CHUNKS - 1):
+        copy.wait()
 
 
 def field_kernel(source_ref, term_ref, valid_ref, all_ref, zh_hbm, zl_hbm,
@@ -249,11 +251,11 @@
         other_ref[where_to, :] = field[N // 2 :]
 
     def slot_pairs(i, carry):
-        for u in range(8):
-            slot_pair(8 * i + u)
+        for u in range(PAIR_TILES // 2):
+            slot_pair(PAIR_TILES // 2 * i + u)
         return carry
 
-    lax.fori_loop(0, PAIR_TILES // 8, slot_pairs, 0)
+    lax.fori_loop(0, 2, slot_pairs, 0)
 
 
 def pair_kernel(source_ref, term_ref, valid_ref, cv_ref, all_ref, c3_ref, c2_ref, act_ref,
@@ -345,7 +347,7 @@
     )(core, raw)
 
 
-def own_part(v, cv, a2, a2p, h3, h2, c3):
+def own_part(v, a2, a2p, h3, h2):
     big = pltpu.VMEM((TERMS * N, G * N), BF16)
     return pl.pallas_call(
         own_kernel,
@@ -353,21 +355,39 @@
             shape(N, G * N),
             shape(N // 2 * OWN_TILES, LANES),
             shape(N // 2 * OWN_TILES, LANES),
+        ),
+        in_specs=[SMEM] + [VMEM] * 4,
+        out_specs=[VMEM] * 3,
+        scratch_shapes=[
+            pltpu.VMEM((TERMS, N, LANES), F32),
+            pltpu.VMEM((LANES, TERMS * N), BF16),
+            big, big,
+        ],
+        compiler_params=params(24),
+        cost_estimate=cost(2_000_000_000, 4 << 20),
+        name="own_part",
+    )(v, a2, a2p, h3, h2)
+
+
+def turned(cv, a2p, c3):
+    big = pltpu.VMEM((TERMS * N, G * N), BF16)
+    return pl.pallas_call(
+        turned_kernel,
+        out_shape=(
             shape(TERMS * N, G * N, dtype=BF16),
             shape(TERMS * N, G * N, dtype=BF16),
         ),
-        in_specs=[SMEM] * 2 + [VMEM] * 5,
-        out_specs=[VMEM] * 3 + [HBM] * 2,
+        in_specs=[SMEM] + [VMEM] * 2,
+        out_specs=[HBM] * 2,
         scratch_shapes=[
             pltpu.VMEM((TERMS, N, LANES), F32),
-            pltpu.VMEM((LANES, TERMS * N), BF16),
-            big, big, big, big,
+            big, big,
             pltpu.SemaphoreType.DMA((2, CHUNKS)),
         ],
         compiler_params=params(OWN_GRANT),
-        cost_estimate=cost(3_000_000_000, 8 << 20),
-        name="own_part",
-    )(v, cv, a2, a2p, h3, h2, c3)
+        cost_estimate=cost(1_000_000_000, 6 << 20),
+        name="turned",
+    )(cv, a2p, c3)
 
 
 def pair_fields(source, term, valid, everyone, zh, zl):
@@ -471,9 +491,10 @@
     everyone = lax.all_to_all(to_all, "state", 0, 0, tiled=True)
     listed = read_list(pairs, lax.axis_index("state"))
     c3 = tile_rows(coup_h3)
-    act, own_mine, own_other, zh, zl = own_part(
-        diag_v1[0], coup_v1, plain, mine_first, tile_rows(diag_h3[0]), tile_rows(diag_h2[0]), c3
-    )
+    act, own_mine, own_other = own_part(
+        diag_v1[0], plain, mine_first, tile_rows(diag_h3[0]), tile_rows(diag_h2[0])
+    )
+    zh, zl = turned(coup_v1, mine_first, c3)
     everyone, own_columns = lax.optimization_barrier(
         (everyone, reduce_own(own_mine, own_other))
     )

time: 80.8 us -> 80.2 us (level)
  waiting for transfers between devices: 18.1 us -> 14.1 us
  Pallas kernels: 26.4 us -> 28.3 us
  starting transfers between devices: 32.7 us -> 34.1 us
    pallas_call x0 -> x1, Pallas kernels: none -> 5.4 us  [turned(): pl.pallas_call(turned_kernel, out_shape=(shape(TERMS * N, G * N, dtype=BF...]
    ppermute x2, waiting for transfers between devices: 8.01 us -> 4.27 us  [reduce_own(): lax.ppermute(send, 'x', [(i, i ^ bit) for i in range(X_CHIPS)])]
    pallas_call x1, Pallas kernels: 9.47 us -> 6.04 us  [own_part(): pl.pallas_call(own_kernel, out_shape=(shape(N, G * N), shape(N // 2 * OWN...]
    all_to_all x1, starting transfers between devices: 11.5 us -> 12.9 us  [per_device(): lax.all_to_all(sums.reshape(N // 2, 1, ALL_TILES * LANES), ('z', 'x'), 0,...]
    unnamed x18 -> x22, local copies, waits for them, and re-layouts: 1.09 us -> 1.74 us
  transfers between devices with their start and end apart: 6 -> 6, of which waited for: 5 -> 4; matrix products, arithmetic and copies ran while one was open for 1% -> 1% of each run, Pallas kernels for 22% -> 24%
where the time goes in v4:
time: 80.2 us; the launch traced here: 79.8 us
  starting transfers between devices  34.1 us (43%)
  Pallas kernels  28.3 us (35%)
  waiting for transfers between devices  14.1 us (18%)
  local copies, waits for them, and re-layouts  1.89 us (2%)
  between operations  0.94 us (1%)
    all_to_all x1, starting transfers between devices, per_device(): lax.all_to_all(sums.reshape(N // 2, 1, ALL_TILES * LANES), ('z', 'x'), 0,...  12.9 us
    ppermute x2, starting transfers between devices, other_core(): return lax.ppermute(value, 'core', [(0, 1), (1, 0)])  8.77 us
    pallas_call x1, Pallas kernels, pair_action(): pl.pallas_call(pair_kernel, out_shape=shape(PAIRS * N, LANES), in_specs=[...  7.75 us
    all_to_all x1, waiting for transfers between devices, per_device(): lax.all_to_all(sums.reshape(N // 2, 1, ALL_TILES * LANES), ('z', 'x'), 0,...  7.72 us
    all_to_all x1, starting transfers between devices, per_device(): everyone = lax.all_to_all(to_all, 'state', 0, 0, tiled=True)  7.64 us
    pallas_call x1, Pallas kernels, pair_fields(): pl.pallas_call(field_kernel, out_shape=(shape(rows, LANES), shape(rows, L...  6.53 us
    pallas_call x1, Pallas kernels, own_part(): pl.pallas_call(own_kernel, out_shape=(shape(N, G * N), shape(N // 2 * OWN...  6.04 us
    pallas_call x1, Pallas kernels, turned(): pl.pallas_call(turned_kernel, out_shape=(shape(TERMS * N, G * N, dtype=BF...  5.4 us
  transfers between devices with their start and end apart: 6, of which 4 were waited for; matrix products, arithmetic and copies ran while one was open for 1% of the time, Pallas kernels for 24%

profile of v4, /device:TPU:1, one launch (start us, length us, event | category | flops | bytes accessed | tf_op | source)
XLA Modules:
  0.0 79.8 jit_solution(1960993230373092455)
XLA Ops:
  0.7 0.9 %copy-done = f32[1,8,4096]{2,1,0:T(8,128)S(1)} copy-done((f32[1,8,4096]{2,1,0:T(8,128)S(1)}, f32[1,8,4096]{2,1,0:T(8,128)}, u32[]{:S(2)}) %copy-start) | copy-done | bytes 131096
  1.6 1.1 %arrange.1 = (f32[8,256,128]{2,1,0:T(8,128)}, f32[256,128]{1,0:T(8,128)S(1)}, f32[256,128]{1,0:T(8,128)S(1)}) custom-call(s32[1]{0:T(128)} %bitcast.3.core_ref, f32[256,128]{1,0:T(8,128)S(1)} %bitcast.52), custom_call_target="tpu_custom_call" | custom-call | tf_op jit(solution)/shard_map/arrange/pallas_call | solution.py:340
  2.7 7.6 %all-to-all-start = ((f32[8,256,128]{2,1,0:T(8,128)}), f32[8,256,128]{2,1,0:T(8,128)S(1)}, u32[]{:S(2)}, u32[]{:S(2)}) async-start(f32[8,256,128]{2,1,0:T(8,128)} %get-tuple-element.17), calls=%async_computation | async-start | bytes 2097152 | tf_op jit(solution)/shard_map/all_to_all | solution.py:491
  10.3 0.1 copy.25
  10.5 6.0 %own_part.1 = (f32[64,512]{1,0:T(8,128)S(1)}, f32[512,128]{1,0:T(8,128)S(1)}, f32[512,128]{1,0:T(8,128)S(1)}) custom-call(f32[32,8]{1,0:T(8,128)S(1)} %bitcast.53, f32[256,128]{1,0:T(8,128)S(1)} %get-tuple-element.18.a_ref, f32[256,128]{1,0:T(8,128)S(1)} %get-tuple-element.19.ap_ref, f32[1024,128]{1,0:T(8,128)S(1)} %bitcast.54, f32[1024,128]{1,0:T(8,128)S(1)} %bitcast.55), custom_call_target="tpu_custom_call" | custom-call | flops 2000000000 | bytes 4194304 | tf_op jit(solution)/shard_map/own_part/pallas_call | solution.py:352
  16.5 0.6 copy-done.5
  17.2 4.7 %collective-permute-start = (f32[512,128]{1,0:T(8,128)S(1)}, f32[512,128]{1,0:T(8,128)S(1)}, u32[]{:S(2)}, u32[]{:S(2)}) collective-permute-start(f32[512,128]{1,0:T(8,128)S(1)} %get-tuple-element.21), channel_id=1, source_target_pairs={{0,1},{1,0},{2,3},{3,2},{4,5},{5,4},{6,7},{7,6},{8,9},{9,8},{10,11... | collective-permute-start | bytes 786440 | tf_op jit(solution)/shard_map/ppermute | solution.py:474
  21.9 0.1 copy.24
  22.0 0.2 reduce-window.8
  22.2 0.8 %collective-permute-done = f32[512,128]{1,0:T(8,128)S(1)} collective-permute-done((f32[512,128]{1,0:T(8,128)S(1)}, f32[512,128]{1,0:T(8,128)S(1)}, u32[]{:S(2)}, u32[]{:S(2)}) %collective-permute-start) | collective-permute-done | bytes 262176 | tf_op jit(solution)/shard_map/ppermute | solution.py:474
  23.0 1.9 %collective-permute-start.1 = (f32[2,4,32,128]{3,2,1,0:T(8,128)S(1)}, f32[2,4,32,128]{3,2,1,0:T(8,128)S(1)}, u32[]{:S(2)}, u32[]{:S(2)}) collective-permute-start(f32[2,4,32,128]{3,2,1,0:T(8,128)S(1)} %dynamic-slice_bitcast_fusion), channel_id=1, source_target_pairs={{0,2},{2,0},{4,6},{6,4},{1,3},{3,1},{5,7},{7,5},{8,10},{10,8},{12,... | collective-permute-start | bytes 393224 | tf_op jit(solution)/shard_map/ppermute | solution.py:484
  25.0 0.1 add_reduce_fusion
  25.2 0.1 convert_reduce_fusion
  25.3 4.3 %collective-permute-done.1 = f32[2,4,32,128]{3,2,1,0:T(8,128)S(1)} collective-permute-done((f32[2,4,32,128]{3,2,1,0:T(8,128)S(1)}, f32[2,4,32,128]{3,2,1,0:T(8,128)S(1)}, u32[]{:S(2)}, u32[]{:S(2)}) %collective-permute-start.1) | collective-permute-done | bytes 131104 | tf_op jit(solution)/shard_map/ppermute | solution.py:484
  29.7 2.8 %collective-permute-start.2 = (f32[4,32,128]{2,1,0:T(8,128)S(1)}, f32[4,32,128]{2,1,0:T(8,128)S(1)}, u32[]{:S(2)}, u32[]{:S(2)}) collective-permute-start(f32[4,32,128]{2,1,0:T(8,128)S(1)} %dynamic-slice_bitcast_fusion.1), channel_id=1, source_target_pairs={{0,4},{2,6},{4,0},{6,2},{1,5},{3,7},{5,1},{7,3},{8,12},{10,14},{12... | collective-permute-start | bytes 196616 | tf_op jit(solution)/shard_map/ppermute | solution.py:484
  32.5 5.4 %turned.1 = (bf16[2048,512]{1,0:T(8,128)(2,1)}, bf16[2048,512]{1,0:T(8,128)(2,1)}) custom-call(f32[32,8]{1,0:T(8,128)S(1)} %copy.26.cv_ref, f32[256,128]{1,0:T(8,128)S(1)} %get-tuple-element.19.ap_ref, f32[1024,128]{1,0:T(8,128)S(1)} %bitcast.56), custom_call_target="tpu_custom_call" | custom-call | flops 1000000000 | bytes 6291456 | tf_op jit(solution)/shard_map/turned/pallas_call | solution.py:374
  38.0 6.5 %pair_fields.1 = (f32[768,128]{1,0:T(8,128)S(1)}, f32[768,128]{1,0:T(8,128)S(1)}) custom-call(s32[48]{0:T(128)S(1)} %get-tuple-element.33.source_ref, s32[48]{0:T(128)S(1)} %get-tuple-element.32.term_ref, s32[48]{0:T(128)S(1)} %get-tuple-element.31.valid_ref, f32[8,256,128]{2,1,0:T(8,128)S(1)} %all-to-all-done.all_ref, ...), custom_call_target="tpu_custom_call" | custom-call | flops 3000000000 | bytes 6291456 | tf_op jit(solution)/shard_map/pair_fields/pallas_call | solution.py:396
  44.5 4.1 %collective-permute-start.3 = (f32[768,128]{1,0:T(8,128)S(1)}, f32[768,128]{1,0:T(8,128)S(1)}, u32[]{:S(2)}, u32[]{:S(2)}) collective-permute-start(f32[768,128]{1,0:T(8,128)S(1)} %get-tuple-element.27), channel_id=1, source_target_pairs={{0,1},{1,0},{2,3},{3,2},{4,5},{5,4},{6,7},{7,6},{8,9},{9,8},{10,11... | collective-permute-start | bytes 1179656 | tf_op jit(solution)/shard_map/ppermute | solution.py:474
  48.6 1.3 %collective-permute-done.3.theirs_ref = f32[768,128]{1,0:T(8,128)S(1)} collective-permute-done((f32[768,128]{1,0:T(8,128)S(1)}, f32[768,128]{1,0:T(8,128)S(1)}, u32[]{:S(2)}, u32[]{:S(2)}) %collective-permute-start.3) | collective-permute-done | bytes 393248 | tf_op jit(solution)/shard_map/ppermute | solution.py:474
  50.0 0.8 %merge.1 = f32[896,128]{1,0:T(8,128)} custom-call(f32[768,128]{1,0:T(8,128)S(1)} %get-tuple-element.26.mine_ref, f32[768,128]{1,0:T(8,128)S(1)} %collective-permute-done.3.theirs_ref, f32[4,32,128]{2,1,0:T(8,128)S(1)} %bitcast_add_fusion.1.own_ref), custom_call_target="tpu_custom_call" | custom-call | tf_op jit(solution)/shard_map/merge/pallas_call | solution.py:435
  50.8 12.9 %all-to-all-start.1 = ((f32[32,1,3584]{2,1,0:T(1,128)}), f32[32,1,3584]{2,1,0:T(1,128)S(1)}, u32[]{:S(2)}, u32[]{:S(2)}) async-start(f32[32,1,3584]{2,1,0:T(1,128)} %bitcast.30), calls=%async_computation.1 | async-start | bytes 917504 | tf_op jit(solution)/shard_map/all_to_all | solution.py:503
  63.7 7.8 %pair_action.1 = f32[256,128]{1,0:T(8,128)} custom-call(s32[48]{0:T(128)S(1)} %get-tuple-element.33.source_ref, s32[48]{0:T(128)S(1)} %get-tuple-element.32.term_ref, s32[48]{0:T(128)S(1)} %get-tuple-element.31.valid_ref, f32[32,8]{1,0:T(8,128)S(1)} %copy.26.cv_ref, f32[8,256,128]{2,1,0:T(8,128)S(1)} %all-to-all-done.all_ref, f32[1024,128]{1,0:T(8,128)S(1)} %bitcast.57, ...), custom_call_target="tpu_custom_call" | custom-call | flops 3000000000 | bytes 4194304 | tf_op jit(solution)/shard_map/pair_action/pallas_call | solution.py:415
  71.5 7.7 %all-to-all-done.1 = f32[32,1,3584]{2,1,0:T(1,128)S(1)} async-done(((f32[32,1,3584]{2,1,0:T(1,128)}), f32[32,1,3584]{2,1,0:T(1,128)S(1)}, u32[]{:S(2)}, u32[]{:S(2)}) %all-to-all-start.1) | async-done | bytes 458784 | tf_op jit(solution)/shard_map/all_to_all | solution.py:503
  79.2 0.6 total.1
  (28 shorter events, 0.2 us)
Async XLA Ops:
  0.6 9.7 %copy-start.7 = (f32[1,32,8]{1,2,0:T(8,128)S(1)}, f32[1,32,8]{1,2,0:T(8,128)}, u32[]{:S(2)}) copy-start(f32[1,32,8]{1,2,0:T(8,128)} %param.11) | copy-start | bytes 3076
  0.6 0.9 %copy-start = (f32[1,8,4096]{2,1,0:T(8,128)S(1)}, f32[1,8,4096]{2,1,0:T(8,128)}, u32[]{:S(2)}) copy-start(f32[1,8,4096]{2,1,0:T(8,128)} %param.8) | copy-start | bytes 393220
  1.6 8.9 %copy-start.1 = (f32[1,32,4096]{2,1,0:T(8,128)S(1)}, f32[1,32,4096]{2,1,0:T(8,128)}, u32[]{:S(2)}) copy-start(f32[1,32,4096]{2,1,0:T(8,128)} %param.10) | copy-start | bytes 1572868
  1.6 8.9 %copy-start.2 = (f32[1,32,4096]{2,1,0:T(8,128)S(1)}, f32[1,32,4096]{2,1,0:T(8,128)}, u32[]{:S(2)}) copy-start(f32[1,32,4096]{2,1,0:T(8,128)} %param.9) | copy-start | bytes 1572868
  2.7 35.3 %all-to-all-start = ((f32[8,256,128]{2,1,0:T(8,128)}), f32[8,256,128]{2,1,0:T(8,128)S(1)}, u32[]{:S(2)}, u32[]{:S(2)}) async-start(f32[8,256,128]{2,1,0:T(8,128)} %get-tuple-element.17), calls=%async_computation | async-start | bytes 2097152 | tf_op jit(solution)/shard_map/all_to_all | solution.py:491
  10.4 11.4 %copy-start.9 = (s32[128,3]{0,1:T(4,128)S(1)}, s32[128,3]{0,1:T(4,128)}, u32[]{:S(2)}) copy-start(s32[128,3]{0,1:T(4,128)} %param.15) | copy-start | bytes 4612
  10.4 14.7 %copy-start.8 = (f32[32,8]{0,1:T(8,128)S(1)}, f32[32,8]{0,1:T(8,128)}, u32[]{:S(2)}) copy-start(f32[32,8]{0,1:T(8,128)} %param.14) | copy-start | bytes 3076
  10.4 22.1 %copy-start.3 = (f32[32,4096]{1,0:T(8,128)S(1)}, f32[32,4096]{1,0:T(8,128)}, u32[]{:S(2)}) copy-start(f32[32,4096]{1,0:T(8,128)} %param.13) | copy-start | bytes 1572868
  16.5 0.7 copy-start.5
  17.2 5.8 %collective-permute-start = (f32[512,128]{1,0:T(8,128)S(1)}, f32[512,128]{1,0:T(8,128)S(1)}, u32[]{:S(2)}, u32[]{:S(2)}) collective-permute-start(f32[512,128]{1,0:T(8,128)S(1)} %get-tuple-element.21), channel_id=1, source_target_pairs={{0,1},{1,0},{2,3},{3,2},{4,5},{5,4},{6,7},{7,6},{8,9},{9,8},{10,11... | collective-permute-start | bytes 786440 | tf_op jit(solution)/shard_map/ppermute | solution.py:474
  23.0 6.6 %collective-permute-start.1 = (f32[2,4,32,128]{3,2,1,0:T(8,128)S(1)}, f32[2,4,32,128]{3,2,1,0:T(8,128)S(1)}, u32[]{:S(2)}, u32[]{:S(2)}) collective-permute-start(f32[2,4,32,128]{3,2,1,0:T(8,128)S(1)} %dynamic-slice_bitcast_fusion), channel_id=1, source_target_pairs={{0,2},{2,0},{4,6},{6,4},{1,3},{3,1},{5,7},{7,5},{8,10},{10,8},{12,... | collective-permute-start | bytes 393224 | tf_op jit(solution)/shard_map/ppermute | solution.py:484
  29.7 8.3 %collective-permute-start.2 = (f32[4,32,128]{2,1,0:T(8,128)S(1)}, f32[4,32,128]{2,1,0:T(8,128)S(1)}, u32[]{:S(2)}, u32[]{:S(2)}) collective-permute-start(f32[4,32,128]{2,1,0:T(8,128)S(1)} %dynamic-slice_bitcast_fusion.1), channel_id=1, source_target_pairs={{0,4},{2,6},{4,0},{6,2},{1,5},{3,7},{5,1},{7,3},{8,12},{10,14},{12... | collective-permute-start | bytes 196616 | tf_op jit(solution)/shard_map/ppermute | solution.py:484
  44.5 19.2 %copy-start.4 = (f32[32,4096]{1,0:T(8,128)S(1)}, f32[32,4096]{1,0:T(8,128)}, u32[]{:S(2)}) copy-start(f32[32,4096]{1,0:T(8,128)} %param.12) | copy-start | bytes 1572868
  44.5 19.2 %copy-start.6 = (f32[64,512]{1,0:T(8,128)S(1)}, f32[64,512]{1,0:T(8,128)}, u32[]{:S(2)}) copy-start(f32[64,512]{1,0:T(8,128)} %copy-done.5) | copy-start | bytes 393220
  44.5 5.4 %collective-permute-start.3 = (f32[768,128]{1,0:T(8,128)S(1)}, f32[768,128]{1,0:T(8,128)S(1)}, u32[]{:S(2)}, u32[]{:S(2)}) collective-permute-start(f32[768,128]{1,0:T(8,128)S(1)} %get-tuple-element.27), channel_id=1, source_target_pairs={{0,1},{1,0},{2,3},{3,2},{4,5},{5,4},{6,7},{7,6},{8,9},{9,8},{10,11... | collective-permute-start | bytes 1179656 | tf_op jit(solution)/shard_map/ppermute | solution.py:474
  50.8 28.4 %all-to-all-start.1 = ((f32[32,1,3584]{2,1,0:T(1,128)}), f32[32,1,3584]{2,1,0:T(1,128)S(1)}, u32[]{:S(2)}, u32[]{:S(2)}) async-start(f32[32,1,3584]{2,1,0:T(1,128)} %bitcast.30), calls=%async_computation.1 | async-start | bytes 917504 | tf_op jit(solution)/shard_map/all_to_all | solution.py:503

commit v5 on v4

--- a/solution.py
+++ b/solution.py
@@ -19,6 +19,9 @@
 ALL_TILES = PAIR_TILES + LAST_TILES
 UNROLL = 4
 CHUNKS = TERMS // 4
+HELD_TERMS = 8
+SENT_TERMS = TERMS - HELD_TERMS
+SENT_CHUNKS = SENT_TERMS // UNROLL
 F32 = jnp.float32
 BF16 = jnp.bfloat16
 NT = (((1,), (1,)), ((), ()))
@@ -163,7 +166,8 @@
     act_ref[...] = act_on(left_ref, wh_ref, wl_ref)
 
 
-def turned_kernel(cv_ref, ap_ref, c3_ref, zh_hbm, zl_hbm, ops_ref, zh_ref, zl_ref, sems):
+def turned_kernel(cv_ref, ap_ref, c3_ref, zh0_ref, zl0_ref, zh_hbm, zl_hbm,
+                  ops_ref, zh_ref, zl_ref, sems):
     def chunk_copies(j):
         rows = pl.ds(pl.multiple_of(j * UNROLL * N, UNROLL * N), UNROLL * N)
         return [
@@ -174,11 +178,13 @@
     left_p = split_lanes(ap_ref[...])
     spread(c3_ref, ops_ref)
 
-    def coupling_terms(j, carry):
+    def coupling_term(k, high_ref, low_ref, index):
+        product = dot(left_p, tile_nn(ops_ref[k]))
+        put_term(product, [cv_ref[k, g] for g in range(G)], index, high_ref, low_ref)
+
+    def sent_terms(j, carry):
         for u in range(UNROLL):
-            k = j * UNROLL + u
-            product = dot(left_p, tile_nn(ops_ref[k]))
-            put_term(product, [cv_ref[k, g] for g in range(G)], k, zh_ref, zl_ref)
+            coupling_term(HELD_TERMS + j * UNROLL + u, zh_ref, zl_ref, j * UNROLL + u)
 
         @pl.when(j > 0)
         def _():
@@ -187,17 +193,22 @@
 
         return carry
 
-    lax.fori_loop(0, CHUNKS, coupling_terms, 0)
-    for j in range(CHUNKS - 1):
+    def held_terms(j, carry):
+        for u in range(UNROLL):
+            coupling_term(j * UNROLL + u, zh0_ref, zl0_ref, j * UNROLL + u)
+        return carry
+
+    lax.fori_loop(0, SENT_CHUNKS, sent_terms, 0)
+    lax.fori_loop(0, 1, held_terms, 0)
+    for copy in chunk_copies(SENT_CHUNKS - 1):
+        copy.start()
+    lax.fori_loop(1, HELD_TERMS // UNROLL, held_terms, 0)
+    for j in range(SENT_CHUNKS):
         for copy in chunk_copies(j):
             copy.wait()
-    for copy in chunk_copies(CHUNKS - 1):
-        copy.start()
-    for copy in chunk_copies(CHUNKS - 1):
-        copy.wait()
-
-
-def field_kernel(source_ref, term_ref, valid_ref, all_ref, zh_hbm, zl_hbm,
+
+
+def field_kernel(source_ref, term_ref, valid_ref, all_ref, zh0_ref, zl0_ref, zh_hbm, zl_hbm,
                  mine_ref, other_ref, gh_ref, gl_ref, zh_ref, zl_ref, f_ref, sems):
     def chunk_copies(j):
         rows = pl.ds(pl.multiple_of(j * UNROLL * N, UNROLL * N), UNROLL * N)
@@ -206,7 +217,7 @@
             pltpu.make_async_copy(zl_hbm.at[rows, :], zl_ref.at[rows, :], sems.at[1, j]),
         ]
 
-    for j in range(CHUNKS):
+    for j in range(SENT_CHUNKS):
         for copy in chunk_copies(j):
             copy.start()
     for q in range(STATES):
@@ -215,12 +226,8 @@
             lanes = slice(pair * LANES, (pair + 1) * LANES)
             gh_ref[q * N : (q + 1) * N, lanes] = high
             gl_ref[q * N : (q + 1) * N, lanes] = low
-    def block(j, carry):
-        for copy in chunk_copies(2 * j) + chunk_copies(2 * j + 1):
-            copy.wait()
-        rows = pl.ds(pl.multiple_of(j * 2 * UNROLL * N, 2 * UNROLL * N), 2 * UNROLL * N)
-        zh = zh_ref[rows, :]
-        left = jnp.concatenate([zh, zl_ref[rows, :], zh], axis=1)
+    def block(zh, zl, rows):
+        left = jnp.concatenate([zh, zl, zh], axis=1)
         for half in range(2):
             here = slice(half * 4 * N, (half + 1) * 4 * N)
             gh = gh_ref[here, :]
@@ -228,9 +235,18 @@
             product = dot_nt(left, right)
             f_ref[2 * half, rows, :] = product[:, :LANES]
             f_ref[2 * half + 1, rows, :] = product[:, LANES:]
-        return carry
-
-    lax.fori_loop(0, CHUNKS // 2, block, 0)
+
+    def sent_block(j, carry):
+        for copy in chunk_copies(2 * j) + chunk_copies(2 * j + 1):
+            copy.wait()
+        size = 2 * UNROLL * N
+        rows = pl.ds(pl.multiple_of(j * size, size), size)
+        to_rows = pl.ds(pl.multiple_of((j + 1) * size, size), size)
+        block(zh_ref[rows, :], zl_ref[rows, :], to_rows)
+        return carry
+
+    block(zh0_ref[...], zl0_ref[...], slice(0, HELD_TERMS * N))
+    lax.fori_loop(0, SENT_CHUNKS // 2, sent_block, 0)
     left_lanes = is_left(N)
 
     def pick(slot):
@@ -333,7 +349,7 @@
 
 
 OWN_GRANT = 52
-FIELD_GRANT = 52
+FIELD_GRANT = 51
 
 
 def arrange(core, raw):
@@ -370,19 +386,21 @@
 
 
 def turned(cv, a2p, c3):
-    big = pltpu.VMEM((TERMS * N, G * N), BF16)
+    big = pltpu.VMEM((SENT_TERMS * N, G * N), BF16)
     return pl.pallas_call(
         turned_kernel,
         out_shape=(
-            shape(TERMS * N, G * N, dtype=BF16),
-            shape(TERMS * N, G * N, dtype=BF16),
+            shape(HELD_TERMS * N, G * N, dtype=BF16),
+            shape(HELD_TERMS * N, G * N, dtype=BF16),
+            shape(SENT_TERMS * N, G * N, dtype=BF16),
+            shape(SENT_TERMS * N, G * N, dtype=BF16),
         ),
         in_specs=[SMEM] + [VMEM] * 2,
-        out_specs=[HBM] * 2,
+        out_specs=[VMEM] * 2 + [HBM] * 2,
         scratch_shapes=[
             pltpu.VMEM((TERMS, N, LANES), F32),
             big, big,
-            pltpu.SemaphoreType.DMA((2, CHUNKS)),
+            pltpu.SemaphoreType.DMA((2, SENT_CHUNKS)),
         ],
         compiler_params=params(OWN_GRANT),
         cost_estimate=cost(1_000_000_000, 6 << 20),
@@ -390,25 +408,25 @@
     )(cv, a2p, c3)
 
 
-def pair_fields(source, term, valid, everyone, zh, zl):
-    big = pltpu.VMEM((TERMS * N, G * N), BF16)
+def pair_fields(source, term, valid, everyone, z):
+    big = pltpu.VMEM((SENT_TERMS * N, G * N), BF16)
     rows = N // 2 * PAIR_TILES
     return pl.pallas_call(
         field_kernel,
         out_shape=(shape(rows, LANES), shape(rows, LANES)),
-        in_specs=[SMEM] * 3 + [VMEM] + [HBM] * 2,
+        in_specs=[SMEM] * 3 + [VMEM] * 3 + [HBM] * 2,
         out_specs=[VMEM] * 2,
         scratch_shapes=[
             pltpu.VMEM((STATES * N, G * N), BF16),
             pltpu.VMEM((STATES * N, G * N), BF16),
             big, big,
             pltpu.VMEM((STATES // 2, TERMS * N, LANES), F32),
-            pltpu.SemaphoreType.DMA((2, CHUNKS)),
+            pltpu.SemaphoreType.DMA((2, SENT_CHUNKS)),
         ],
         compiler_params=params(FIELD_GRANT),
         cost_estimate=cost(3_000_000_000, 6 << 20),
         name="pair_fields",
-    )(source, term, valid, everyone, zh, zl)
+    )(source, term, valid, everyone, *z)
 
 
 def pair_action(source, term, valid, cv, everyone, c3, c2, act):
@@ -494,11 +512,11 @@
     act, own_mine, own_other = own_part(
         diag_v1[0], plain, mine_first, tile_rows(diag_h3[0]), tile_rows(diag_h2[0])
     )
-    zh, zl = turned(coup_v1, mine_first, c3)
+    z = turned(coup_v1, mine_first, c3)
     everyone, own_columns = lax.optimization_barrier(
         (everyone, reduce_own(own_mine, own_other))
     )
-    pair_mine, pair_other = pair_fields(*listed, everyone, zh, zl)
+    pair_mine, pair_other = pair_fields(*listed, everyone, z)
     sums = merge(pair_mine, other_core(pair_other), own_columns)
     parts = lax.all_to_all(
         sums.reshape(N // 2, 1, ALL_TILES * LANES), ("z", "x"), 0, 0, tiled=True

time: 80.2 us -> 80.1 us (level)
  waiting for transfers between devices: 14.1 us -> 15.4 us
  Pallas kernels: 28.3 us -> 27.1 us
    all_to_all x1, waiting for transfers between devices: 0.01 us -> 1.3 us  [per_device(): everyone = lax.all_to_all(to_all, 'state', 0, 0, tiled=True)]
    pallas_call x1, Pallas kernels: 5.4 us -> 4.28 us  [turned(): pl.pallas_call(turned_kernel, out_shape=(shape(HELD_TERMS * N, G * N, dty...]
    unnamed x22 -> x18, local copies, waits for them, and re-layouts: 1.74 us -> 1.09 us
  transfers between devices with their start and end apart: 6 -> 6, of which waited for: 4 -> 5; matrix products, arithmetic and copies ran while one was open for 1% -> 1% of each run, Pallas kernels for 24% -> 23%
where the time goes in v5:
time: 80.1 us; the launch traced here: 79.7 us
  starting transfers between devices  34.5 us (43%)
  Pallas kernels  27.1 us (34%)
  waiting for transfers between devices  15.4 us (19%)
  local copies, waits for them, and re-layouts  1.23 us (2%)
  between operations  0.9 us (1%)
    all_to_all x1, starting transfers between devices, per_device(): lax.all_to_all(sums.reshape(N // 2, 1, ALL_TILES * LANES), ('z', 'x'), 0,...  12.9 us
    ppermute x2, starting transfers between devices, other_core(): return lax.ppermute(value, 'core', [(0, 1), (1, 0)])  9.24 us
    pallas_call x1, Pallas kernels, pair_action(): pl.pallas_call(pair_kernel, out_shape=shape(PAIRS * N, LANES), in_specs=[...  7.76 us
    all_to_all x1, waiting for transfers between devices, per_device(): lax.all_to_all(sums.reshape(N // 2, 1, ALL_TILES * LANES), ('z', 'x'), 0,...  7.72 us
    all_to_all x1, starting transfers between devices, per_device(): everyone = lax.all_to_all(to_all, 'state', 0, 0, tiled=True)  7.64 us
    pallas_call x1, Pallas kernels, pair_fields(): pl.pallas_call(field_kernel, out_shape=(shape(rows, LANES), shape(rows, L...  6.38 us
    pallas_call x1, Pallas kernels, own_part(): pl.pallas_call(own_kernel, out_shape=(shape(N, G * N), shape(N // 2 * OWN...  6.05 us
    ppermute x2, starting transfers between devices, reduce_own(): lax.ppermute(send, 'x', [(i, i ^ bit) for i in range(X_CHIPS)])  4.77 us
  transfers between devices with their start and end apart: 6, of which 5 were waited for; matrix products, arithmetic and copies ran while one was open for 1% of the time, Pallas kernels for 23%

profile of v5, /device:TPU:1, one launch (start us, length us, event | category | flops | bytes accessed | tf_op | source)
XLA Modules:
  0.0 79.7 jit_solution(17784166176251915397)
XLA Ops:
  0.7 0.9 %copy-done = f32[1,8,4096]{2,1,0:T(8,128)S(1)} copy-done((f32[1,8,4096]{2,1,0:T(8,128)S(1)}, f32[1,8,4096]{2,1,0:T(8,128)}, u32[]{:S(2)}) %copy-start) | copy-done | bytes 131096
  1.6 1.2 %arrange.1 = (f32[8,256,128]{2,1,0:T(8,128)}, f32[256,128]{1,0:T(8,128)S(1)}, f32[256,128]{1,0:T(8,128)S(1)}) custom-call(s32[1]{0:T(128)} %bitcast.3.core_ref, f32[256,128]{1,0:T(8,128)S(1)} %bitcast.52), custom_call_target="tpu_custom_call" | custom-call | tf_op jit(solution)/shard_map/arrange/pallas_call | solution.py:356
  2.7 7.6 %all-to-all-start = ((f32[8,256,128]{2,1,0:T(8,128)}), f32[8,256,128]{2,1,0:T(8,128)S(1)}, u32[]{:S(2)}, u32[]{:S(2)}) async-start(f32[8,256,128]{2,1,0:T(8,128)} %get-tuple-element.19), calls=%async_computation | async-start | bytes 2097152 | tf_op jit(solution)/shard_map/all_to_all | solution.py:509
  10.4 0.1 copy.25
  10.5 6.0 %own_part.1 = (f32[64,512]{1,0:T(8,128)S(1)}, f32[512,128]{1,0:T(8,128)S(1)}, f32[512,128]{1,0:T(8,128)S(1)}) custom-call(f32[32,8]{1,0:T(8,128)S(1)} %bitcast.53, f32[256,128]{1,0:T(8,128)S(1)} %get-tuple-element.20.a_ref, f32[256,128]{1,0:T(8,128)S(1)} %get-tuple-element.21.ap_ref, f32[1024,128]{1,0:T(8,128)S(1)} %bitcast.54, f32[1024,128]{1,0:T(8,128)S(1)} %bitcast.55), custom_call_target="tpu_custom_call" | custom-call | flops 2000000000 | bytes 4194304 | tf_op jit(solution)/shard_map/own_part/pallas_call | solution.py:368
  16.5 4.8 %collective-permute-start = (f32[512,128]{1,0:T(8,128)S(1)}, f32[512,128]{1,0:T(8,128)S(1)}, u32[]{:S(2)}, u32[]{:S(2)}) collective-permute-start(f32[512,128]{1,0:T(8,128)S(1)} %get-tuple-element.23), channel_id=1, source_target_pairs={{0,1},{1,0},{2,3},{3,2},{4,5},{5,4},{6,7},{7,6},{8,9},{9,8},{10,11... | collective-permute-start | bytes 786440 | tf_op jit(solution)/shard_map/ppermute | solution.py:492
  21.4 0.1 copy.24
  21.5 0.2 reduce-window.8
  21.7 0.8 %collective-permute-done = f32[512,128]{1,0:T(8,128)S(1)} collective-permute-done((f32[512,128]{1,0:T(8,128)S(1)}, f32[512,128]{1,0:T(8,128)S(1)}, u32[]{:S(2)}, u32[]{:S(2)}) %collective-permute-start) | collective-permute-done | bytes 262176 | tf_op jit(solution)/shard_map/ppermute | solution.py:492
  22.5 1.9 %collective-permute-start.1 = (f32[2,4,32,128]{3,2,1,0:T(8,128)S(1)}, f32[2,4,32,128]{3,2,1,0:T(8,128)S(1)}, u32[]{:S(2)}, u32[]{:S(2)}) collective-permute-start(f32[2,4,32,128]{3,2,1,0:T(8,128)S(1)} %dynamic-slice_bitcast_fusion), channel_id=1, source_target_pairs={{0,2},{2,0},{4,6},{6,4},{1,3},{3,1},{5,7},{7,5},{8,10},{10,8},{12,... | collective-permute-start | bytes 393224 | tf_op jit(solution)/shard_map/ppermute | solution.py:502
  24.5 0.1 add_reduce_fusion
  24.7 0.1 convert_reduce_fusion
  24.9 4.3 %collective-permute-done.1 = f32[2,4,32,128]{3,2,1,0:T(8,128)S(1)} collective-permute-done((f32[2,4,32,128]{3,2,1,0:T(8,128)S(1)}, f32[2,4,32,128]{3,2,1,0:T(8,128)S(1)}, u32[]{:S(2)}, u32[]{:S(2)}) %collective-permute-start.1) | collective-permute-done | bytes 131104 | tf_op jit(solution)/shard_map/ppermute | solution.py:502
  29.2 2.8 %collective-permute-start.2 = (f32[4,32,128]{2,1,0:T(8,128)S(1)}, f32[4,32,128]{2,1,0:T(8,128)S(1)}, u32[]{:S(2)}, u32[]{:S(2)}) collective-permute-start(f32[4,32,128]{2,1,0:T(8,128)S(1)} %dynamic-slice_bitcast_fusion.1), channel_id=1, source_target_pairs={{0,4},{2,6},{4,0},{6,2},{1,5},{3,7},{5,1},{7,3},{8,12},{10,14},{12... | collective-permute-start | bytes 196616 | tf_op jit(solution)/shard_map/ppermute | solution.py:502
  32.0 4.3 %turned.1 = (bf16[512,512]{1,0:T(8,128)(2,1)S(1)}, bf16[512,512]{1,0:T(8,128)(2,1)S(1)}, bf16[1536,512]{1,0:T(8,128)(2,1)}, bf16[1536,512]{1,0:T(8,128)(2,1)}) custom-call(f32[32,8]{1,0:T(8,128)S(1)} %copy.26.cv_ref, f32[256,128]{1,0:T(8,128)S(1)} %get-tuple-element.21.ap_ref, f32[1024,128]{1,0:T(8,128)S(1)} %bitcast.56), custom_call_target="tpu_custom_call" | custom-call | flops 1000000000 | bytes 6291456 | tf_op jit(solution)/shard_map/turned/pallas_call | solution.py:390
  36.3 1.3 %all-to-all-done.all_ref = f32[8,256,128]{2,1,0:T(8,128)S(1)} async-done(((f32[8,256,128]{2,1,0:T(8,128)}), f32[8,256,128]{2,1,0:T(8,128)S(1)}, u32[]{:S(2)}, u32[]{:S(2)}) %all-to-all-start) | async-done | bytes 1048608 | tf_op jit(solution)/shard_map/all_to_all | solution.py:509
  37.6 6.4 %pair_fields.1 = (f32[768,128]{1,0:T(8,128)S(1)}, f32[768,128]{1,0:T(8,128)S(1)}) custom-call(s32[48]{0:T(128)S(1)} %get-tuple-element.37.source_ref, s32[48]{0:T(128)S(1)} %get-tuple-element.36.term_ref, s32[48]{0:T(128)S(1)} %get-tuple-element.35.valid_ref, f32[8,256,128]{2,1,0:T(8,128)S(1)} %all-to-all-done.all_ref, ...), custom_call_target="tpu_custom_call" | custom-call | flops 3000000000 | bytes 6291456 | tf_op jit(solution)/shard_map/pair_fields/pallas_call | solution.py:414
  44.0 4.4 %collective-permute-start.3 = (f32[768,128]{1,0:T(8,128)S(1)}, f32[768,128]{1,0:T(8,128)S(1)}, u32[]{:S(2)}, u32[]{:S(2)}) collective-permute-start(f32[768,128]{1,0:T(8,128)S(1)} %get-tuple-element.31), channel_id=1, source_target_pairs={{0,1},{1,0},{2,3},{3,2},{4,5},{5,4},{6,7},{7,6},{8,9},{9,8},{10,11... | collective-permute-start | bytes 1179656 | tf_op jit(solution)/shard_map/ppermute | solution.py:492
  48.5 1.3 %collective-permute-done.3.theirs_ref = f32[768,128]{1,0:T(8,128)S(1)} collective-permute-done((f32[768,128]{1,0:T(8,128)S(1)}, f32[768,128]{1,0:T(8,128)S(1)}, u32[]{:S(2)}, u32[]{:S(2)}) %collective-permute-start.3) | collective-permute-done | bytes 393248 | tf_op jit(solution)/shard_map/ppermute | solution.py:492
  49.8 0.8 %merge.1 = f32[896,128]{1,0:T(8,128)} custom-call(f32[768,128]{1,0:T(8,128)S(1)} %get-tuple-element.30.mine_ref, f32[768,128]{1,0:T(8,128)S(1)} %collective-permute-done.3.theirs_ref, f32[4,32,128]{2,1,0:T(8,128)S(1)} %bitcast_add_fusion.1.own_ref), custom_call_target="tpu_custom_call" | custom-call | tf_op jit(solution)/shard_map/merge/pallas_call | solution.py:453
  50.6 12.9 %all-to-all-start.1 = ((f32[32,1,3584]{2,1,0:T(1,128)}), f32[32,1,3584]{2,1,0:T(1,128)S(1)}, u32[]{:S(2)}, u32[]{:S(2)}) async-start(f32[32,1,3584]{2,1,0:T(1,128)} %bitcast.30), calls=%async_computation.1 | async-start | bytes 917504 | tf_op jit(solution)/shard_map/all_to_all | solution.py:521
  63.5 7.8 %pair_action.1 = f32[256,128]{1,0:T(8,128)} custom-call(s32[48]{0:T(128)S(1)} %get-tuple-element.37.source_ref, s32[48]{0:T(128)S(1)} %get-tuple-element.36.term_ref, s32[48]{0:T(128)S(1)} %get-tuple-element.35.valid_ref, f32[32,8]{1,0:T(8,128)S(1)} %copy.26.cv_ref, f32[8,256,128]{2,1,0:T(8,128)S(1)} %all-to-all-done.all_ref, f32[1024,128]{1,0:T(8,128)S(1)} %bitcast.57, ...), custom_call_target="tpu_custom_call" | custom-call | flops 3000000000 | bytes 4194304 | tf_op jit(solution)/shard_map/pair_action/pallas_call | solution.py:433
  71.3 7.7 %all-to-all-done.1 = f32[32,1,3584]{2,1,0:T(1,128)S(1)} async-done(((f32[32,1,3584]{2,1,0:T(1,128)}), f32[32,1,3584]{2,1,0:T(1,128)S(1)}, u32[]{:S(2)}, u32[]{:S(2)}) %all-to-all-start.1) | async-done | bytes 458784 | tf_op jit(solution)/shard_map/all_to_all | solution.py:521
  79.0 0.6 total.1
  (24 shorter events, 0.2 us)
Async XLA Ops:
  0.6 9.7 %copy-start.5 = (f32[1,32,8]{1,2,0:T(8,128)S(1)}, f32[1,32,8]{1,2,0:T(8,128)}, u32[]{:S(2)}) copy-start(f32[1,32,8]{1,2,0:T(8,128)} %param.11) | copy-start | bytes 3076
  0.6 0.9 %copy-start = (f32[1,8,4096]{2,1,0:T(8,128)S(1)}, f32[1,8,4096]{2,1,0:T(8,128)}, u32[]{:S(2)}) copy-start(f32[1,8,4096]{2,1,0:T(8,128)} %param.8) | copy-start | bytes 393220
  1.6 8.9 %copy-start.1 = (f32[1,32,4096]{2,1,0:T(8,128)S(1)}, f32[1,32,4096]{2,1,0:T(8,128)}, u32[]{:S(2)}) copy-start(f32[1,32,4096]{2,1,0:T(8,128)} %param.10) | copy-start | bytes 1572868
  1.6 8.9 %copy-start.2 = (f32[1,32,4096]{2,1,0:T(8,128)S(1)}, f32[1,32,4096]{2,1,0:T(8,128)}, u32[]{:S(2)}) copy-start(f32[1,32,4096]{2,1,0:T(8,128)} %param.9) | copy-start | bytes 1572868
  2.7 34.9 %all-to-all-start = ((f32[8,256,128]{2,1,0:T(8,128)}), f32[8,256,128]{2,1,0:T(8,128)S(1)}, u32[]{:S(2)}, u32[]{:S(2)}) async-start(f32[8,256,128]{2,1,0:T(8,128)} %get-tuple-element.19), calls=%async_computation | async-start | bytes 2097152 | tf_op jit(solution)/shard_map/all_to_all | solution.py:509
  10.4 10.9 %copy-start.7 = (s32[128,3]{0,1:T(4,128)S(1)}, s32[128,3]{0,1:T(4,128)}, u32[]{:S(2)}) copy-start(s32[128,3]{0,1:T(4,128)} %param.15) | copy-start | bytes 4612
  10.5 14.2 %copy-start.6 = (f32[32,8]{0,1:T(8,128)S(1)}, f32[32,8]{0,1:T(8,128)}, u32[]{:S(2)}) copy-start(f32[32,8]{0,1:T(8,128)} %param.14) | copy-start | bytes 3076
  16.5 15.5 %copy-start.3 = (f32[32,4096]{1,0:T(8,128)S(1)}, f32[32,4096]{1,0:T(8,128)}, u32[]{:S(2)}) copy-start(f32[32,4096]{1,0:T(8,128)} %param.13) | copy-start | bytes 1572868
  16.5 6.0 %collective-permute-start = (f32[512,128]{1,0:T(8,128)S(1)}, f32[512,128]{1,0:T(8,128)S(1)}, u32[]{:S(2)}, u32[]{:S(2)}) collective-permute-start(f32[512,128]{1,0:T(8,128)S(1)} %get-tuple-element.23), channel_id=1, source_target_pairs={{0,1},{1,0},{2,3},{3,2},{4,5},{5,4},{6,7},{7,6},{8,9},{9,8},{10,11... | collective-permute-start | bytes 786440 | tf_op jit(solution)/shard_map/ppermute | solution.py:492
  22.5 6.6 %collective-permute-start.1 = (f32[2,4,32,128]{3,2,1,0:T(8,128)S(1)}, f32[2,4,32,128]{3,2,1,0:T(8,128)S(1)}, u32[]{:S(2)}, u32[]{:S(2)}) collective-permute-start(f32[2,4,32,128]{3,2,1,0:T(8,128)S(1)} %dynamic-slice_bitcast_fusion), channel_id=1, source_target_pairs={{0,2},{2,0},{4,6},{6,4},{1,3},{3,1},{5,7},{7,5},{8,10},{10,8},{12,... | collective-permute-start | bytes 393224 | tf_op jit(solution)/shard_map/ppermute | solution.py:502
  29.2 7.2 %collective-permute-start.2 = (f32[4,32,128]{2,1,0:T(8,128)S(1)}, f32[4,32,128]{2,1,0:T(8,128)S(1)}, u32[]{:S(2)}, u32[]{:S(2)}) collective-permute-start(f32[4,32,128]{2,1,0:T(8,128)S(1)} %dynamic-slice_bitcast_fusion.1), channel_id=1, source_target_pairs={{0,4},{2,6},{4,0},{6,2},{1,5},{3,7},{5,1},{7,3},{8,12},{10,14},{12... | collective-permute-start | bytes 196616 | tf_op jit(solution)/shard_map/ppermute | solution.py:502
  44.0 19.5 %copy-start.4 = (f32[32,4096]{1,0:T(8,128)S(1)}, f32[32,4096]{1,0:T(8,128)}, u32[]{:S(2)}) copy-start(f32[32,4096]{1,0:T(8,128)} %param.12) | copy-start | bytes 1572868
  44.0 5.8 %collective-permute-start.3 = (f32[768,128]{1,0:T(8,128)S(1)}, f32[768,128]{1,0:T(8,128)S(1)}, u32[]{:S(2)}, u32[]{:S(2)}) collective-permute-start(f32[768,128]{1,0:T(8,128)S(1)} %get-tuple-element.31), channel_id=1, source_target_pairs={{0,1},{1,0},{2,3},{3,2},{4,5},{5,4},{6,7},{7,6},{8,9},{9,8},{10,11... | collective-permute-start | bytes 1179656 | tf_op jit(solution)/shard_map/ppermute | solution.py:492
  50.6 28.4 %all-to-all-start.1 = ((f32[32,1,3584]{2,1,0:T(1,128)}), f32[32,1,3584]{2,1,0:T(1,128)S(1)}, u32[]{:S(2)}, u32[]{:S(2)}) async-start(f32[32,1,3584]{2,1,0:T(1,128)} %bitcast.30), calls=%async_computation.1 | async-start | bytes 917504 | tf_op jit(solution)/shard_map/all_to_all | solution.py:521

commit v6 on v5

--- a/solution.py
+++ b/solution.py
@@ -209,69 +209,48 @@
 
 
 def field_kernel(source_ref, term_ref, valid_ref, all_ref, zh0_ref, zl0_ref, zh_hbm, zl_hbm,
-                 mine_ref, other_ref, gh_ref, gl_ref, zh_ref, zl_ref, f_ref, sems):
-    def chunk_copies(j):
-        rows = pl.ds(pl.multiple_of(j * UNROLL * N, UNROLL * N), UNROLL * N)
-        return [
-            pltpu.make_async_copy(zh_hbm.at[rows, :], zh_ref.at[rows, :], sems.at[0, j]),
-            pltpu.make_async_copy(zl_hbm.at[rows, :], zl_ref.at[rows, :], sems.at[1, j]),
+                 mine_ref, other_ref, both_ref, zh_ref, zl_ref, sems):
+    held = HELD_TERMS * N
+    copies = []
+    for j in range(SENT_CHUNKS):
+        rows = pl.ds(j * UNROLL * N, UNROLL * N)
+        to_rows = pl.ds(held + j * UNROLL * N, UNROLL * N)
+        copies += [
+            pltpu.make_async_copy(zh_hbm.at[rows, :], zh_ref.at[to_rows, :], sems.at[0, j]),
+            pltpu.make_async_copy(zl_hbm.at[rows, :], zl_ref.at[to_rows, :], sems.at[1, j]),
         ]
-
-    for j in range(SENT_CHUNKS):
-        for copy in chunk_copies(j):
-            copy.start()
+    for copy in copies:
+        copy.start()
+    zh_ref[:held, :] = zh0_ref[...]
+    zl_ref[:held, :] = zl0_ref[...]
     for q in range(STATES):
         for pair in range(PAIRS):
             high, low = split(all_ref[q, pair * N : (pair + 1) * N, :])
             lanes = slice(pair * LANES, (pair + 1) * LANES)
-            gh_ref[q * N : (q + 1) * N, lanes] = high
-            gl_ref[q * N : (q + 1) * N, lanes] = low
-    def block(zh, zl, rows):
-        left = jnp.concatenate([zh, zl, zh], axis=1)
-        for half in range(2):
-            here = slice(half * 4 * N, (half + 1) * 4 * N)
-            gh = gh_ref[here, :]
-            right = jnp.concatenate([gh, gh, gl_ref[here, :]], axis=1)
-            product = dot_nt(left, right)
-            f_ref[2 * half, rows, :] = product[:, :LANES]
-            f_ref[2 * half + 1, rows, :] = product[:, LANES:]
-
-    def sent_block(j, carry):
-        for copy in chunk_copies(2 * j) + chunk_copies(2 * j + 1):
-            copy.wait()
-        size = 2 * UNROLL * N
-        rows = pl.ds(pl.multiple_of(j * size, size), size)
-        to_rows = pl.ds(pl.multiple_of((j + 1) * size, size), size)
-        block(zh_ref[rows, :], zl_ref[rows, :], to_rows)
+            both_ref[q, :N, lanes] = high
+            both_ref[q, N:, lanes] = low
+    for copy in copies:
+        copy.wait()
+    left_lanes = is_left(N)
+
+    def slot_field(slot):
+        rows = pl.ds(pl.multiple_of(term_ref[slot] * N, N), N)
+        z = jnp.concatenate([zh_ref[rows, :], zl_ref[rows, :]], axis=0)
+        product = dot_nt(z, both_ref[source_ref[slot]])
+        half = product[:N] + product[N:]
+        field = half + pltpu.roll(half, N, 1)
+        return jnp.where(valid_ref[slot] == 1, field, 0.0)
+
+    def slot_pairs(j, carry):
+        for u in range(4):
+            i = 4 * j + u
+            field = jnp.where(left_lanes, slot_field(2 * i), slot_field(2 * i + 1))
+            where_to = pl.ds(i, N // 2, stride=PAIR_TILES)
+            mine_ref[where_to, :] = field[: N // 2]
+            other_ref[where_to, :] = field[N // 2 :]
         return carry
 
-    block(zh0_ref[...], zl0_ref[...], slice(0, HELD_TERMS * N))
-    lax.fori_loop(0, SENT_CHUNKS // 2, sent_block, 0)
-    left_lanes = is_left(N)
-
-    def pick(slot):
-        source = source_ref[slot]
-        rows = pl.ds(pl.multiple_of(term_ref[slot] * N, N), N)
-        return f_ref[source // 2, rows, :], lax.rem(source, 2)
-
-    def slot_pair(i):
-        first, odd_first = pick(2 * i)
-        second, odd_second = pick(2 * i + 1)
-        first = jnp.where(odd_first == 1, pltpu.roll(first, N, 1), first)
-        second = jnp.where(odd_second == 0, pltpu.roll(second, N, 1), second)
-        first = jnp.where(valid_ref[2 * i] == 1, first, 0.0)
-        second = jnp.where(valid_ref[2 * i + 1] == 1, second, 0.0)
-        field = jnp.where(left_lanes, first, second)
-        where_to = pl.ds(i, N // 2, stride=PAIR_TILES)
-        mine_ref[where_to, :] = field[: N // 2]
-        other_ref[where_to, :] = field[N // 2 :]
-
-    def slot_pairs(i, carry):
-        for u in range(PAIR_TILES // 2):
-            slot_pair(PAIR_TILES // 2 * i + u)
-        return carry
-
-    lax.fori_loop(0, 2, slot_pairs, 0)
+    lax.fori_loop(0, PAIR_TILES // 4, slot_pairs, 0)
 
 
 def pair_kernel(source_ref, term_ref, valid_ref, cv_ref, all_ref, c3_ref, c2_ref, act_ref,
@@ -409,7 +388,6 @@
 
 
 def pair_fields(source, term, valid, everyone, z):
-    big = pltpu.VMEM((SENT_TERMS * N, G * N), BF16)
     rows = N // 2 * PAIR_TILES
     return pl.pallas_call(
         field_kernel,
@@ -417,10 +395,9 @@
         in_specs=[SMEM] * 3 + [VMEM] * 3 + [HBM] * 2,
         out_specs=[VMEM] * 2,
         scratch_shapes=[
-            pltpu.VMEM((STATES * N, G * N), BF16),
-            pltpu.VMEM((STATES * N, G * N), BF16),
-            big, big,
-            pltpu.VMEM((STATES // 2, TERMS * N, LANES), F32),
+            pltpu.VMEM((STATES, LANES, G * N), BF16),
+            pltpu.VMEM((TERMS * N, G * N), BF16),
+            pltpu.VMEM((TERMS * N, G * N), BF16),
             pltpu.SemaphoreType.DMA((2, SENT_CHUNKS)),
         ],
         compiler_params=params(FIELD_GRANT),

time: 80.1 us -> 79.2 us (0.989)
  Pallas kernels: 27.1 us -> 26.2 us
    pallas_call x1, Pallas kernels: 6.38 us -> 5.51 us  [pair_fields(): pl.pallas_call(field_kernel, out_shape=(shape(rows, LANES), shape(rows, L...]
where the time goes in v6:
time: 79.2 us; the launch traced here: 78.8 us
  starting transfers between devices  34.5 us (44%)
  Pallas kernels  26.2 us (33%)
  waiting for transfers between devices  15.4 us (19%)
  local copies, waits for them, and re-layouts  1.23 us (2%)
  between operations  0.9 us (1%)
    all_to_all x1, starting transfers between devices, per_device(): lax.all_to_all(sums.reshape(N // 2, 1, ALL_TILES * LANES), ('z', 'x'), 0,...  12.9 us
    ppermute x2, starting transfers between devices, other_core(): return lax.ppermute(value, 'core', [(0, 1), (1, 0)])  9.24 us
    pallas_call x1, Pallas kernels, pair_action(): pl.pallas_call(pair_kernel, out_shape=shape(PAIRS * N, LANES), in_specs=[...  7.76 us
    all_to_all x1, waiting for transfers between devices, per_device(): lax.all_to_all(sums.reshape(N // 2, 1, ALL_TILES * LANES), ('z', 'x'), 0,...  7.72 us
    all_to_all x1, starting transfers between devices, per_device(): everyone = lax.all_to_all(to_all, 'state', 0, 0, tiled=True)  7.64 us
    pallas_call x1, Pallas kernels, own_part(): pl.pallas_call(own_kernel, out_shape=(shape(N, G * N), shape(N // 2 * OWN...  6.05 us
    pallas_call x1, Pallas kernels, pair_fields(): pl.pallas_call(field_kernel, out_shape=(shape(rows, LANES), shape(rows, L...  5.51 us
    ppermute x2, starting transfers between devices, reduce_own(): lax.ppermute(send, 'x', [(i, i ^ bit) for i in range(X_CHIPS)])  4.77 us
  transfers between devices with their start and end apart: 6, of which 5 were waited for; matrix products, arithmetic and copies ran while one was open for 1% of the time, Pallas kernels for 23%

profile of v6, /device:TPU:1, one launch (start us, length us, event | category | flops | bytes accessed | tf_op | source)
XLA Modules:
  0.0 78.8 jit_solution(14886807398896183486)
XLA Ops:
  0.7 0.9 %copy-done = f32[1,8,4096]{2,1,0:T(8,128)S(1)} copy-done((f32[1,8,4096]{2,1,0:T(8,128)S(1)}, f32[1,8,4096]{2,1,0:T(8,128)}, u32[]{:S(2)}) %copy-start) | copy-done | bytes 131096
  1.6 1.2 %arrange.1 = (f32[8,256,128]{2,1,0:T(8,128)}, f32[256,128]{1,0:T(8,128)S(1)}, f32[256,128]{1,0:T(8,128)S(1)}) custom-call(s32[1]{0:T(128)} %bitcast.3.core_ref, f32[256,128]{1,0:T(8,128)S(1)} %bitcast.52), custom_call_target="tpu_custom_call" | custom-call | tf_op jit(solution)/shard_map/arrange/pallas_call | solution.py:335
  2.7 7.6 %all-to-all-start = ((f32[8,256,128]{2,1,0:T(8,128)}), f32[8,256,128]{2,1,0:T(8,128)S(1)}, u32[]{:S(2)}, u32[]{:S(2)}) async-start(f32[8,256,128]{2,1,0:T(8,128)} %get-tuple-element.19), calls=%async_computation | async-start | bytes 2097152 | tf_op jit(solution)/shard_map/all_to_all | solution.py:486
  10.4 0.1 copy.25
  10.5 6.0 %own_part.1 = (f32[64,512]{1,0:T(8,128)S(1)}, f32[512,128]{1,0:T(8,128)S(1)}, f32[512,128]{1,0:T(8,128)S(1)}) custom-call(f32[32,8]{1,0:T(8,128)S(1)} %bitcast.53, f32[256,128]{1,0:T(8,128)S(1)} %get-tuple-element.20.a_ref, f32[256,128]{1,0:T(8,128)S(1)} %get-tuple-element.21.ap_ref, f32[1024,128]{1,0:T(8,128)S(1)} %bitcast.54, f32[1024,128]{1,0:T(8,128)S(1)} %bitcast.55), custom_call_target="tpu_custom_call" | custom-call | flops 2000000000 | bytes 4194304 | tf_op jit(solution)/shard_map/own_part/pallas_call | solution.py:347
  16.5 4.8 %collective-permute-start = (f32[512,128]{1,0:T(8,128)S(1)}, f32[512,128]{1,0:T(8,128)S(1)}, u32[]{:S(2)}, u32[]{:S(2)}) collective-permute-start(f32[512,128]{1,0:T(8,128)S(1)} %get-tuple-element.23), channel_id=1, source_target_pairs={{0,1},{1,0},{2,3},{3,2},{4,5},{5,4},{6,7},{7,6},{8,9},{9,8},{10,11... | collective-permute-start | bytes 786440 | tf_op jit(solution)/shard_map/ppermute | solution.py:469
  21.4 0.1 copy.24
  21.5 0.2 reduce-window.8
  21.7 0.8 %collective-permute-done = f32[512,128]{1,0:T(8,128)S(1)} collective-permute-done((f32[512,128]{1,0:T(8,128)S(1)}, f32[512,128]{1,0:T(8,128)S(1)}, u32[]{:S(2)}, u32[]{:S(2)}) %collective-permute-start) | collective-permute-done | bytes 262176 | tf_op jit(solution)/shard_map/ppermute | solution.py:469
  22.5 1.9 %collective-permute-start.1 = (f32[2,4,32,128]{3,2,1,0:T(8,128)S(1)}, f32[2,4,32,128]{3,2,1,0:T(8,128)S(1)}, u32[]{:S(2)}, u32[]{:S(2)}) collective-permute-start(f32[2,4,32,128]{3,2,1,0:T(8,128)S(1)} %dynamic-slice_bitcast_fusion), channel_id=1, source_target_pairs={{0,2},{2,0},{4,6},{6,4},{1,3},{3,1},{5,7},{7,5},{8,10},{10,8},{12,... | collective-permute-start | bytes 393224 | tf_op jit(solution)/shard_map/ppermute | solution.py:479
  24.5 0.1 add_reduce_fusion
  24.7 0.1 convert_reduce_fusion
  24.9 4.3 %collective-permute-done.1 = f32[2,4,32,128]{3,2,1,0:T(8,128)S(1)} collective-permute-done((f32[2,4,32,128]{3,2,1,0:T(8,128)S(1)}, f32[2,4,32,128]{3,2,1,0:T(8,128)S(1)}, u32[]{:S(2)}, u32[]{:S(2)}) %collective-permute-start.1) | collective-permute-done | bytes 131104 | tf_op jit(solution)/shard_map/ppermute | solution.py:479
  29.2 2.8 %collective-permute-start.2 = (f32[4,32,128]{2,1,0:T(8,128)S(1)}, f32[4,32,128]{2,1,0:T(8,128)S(1)}, u32[]{:S(2)}, u32[]{:S(2)}) collective-permute-start(f32[4,32,128]{2,1,0:T(8,128)S(1)} %dynamic-slice_bitcast_fusion.1), channel_id=1, source_target_pairs={{0,4},{2,6},{4,0},{6,2},{1,5},{3,7},{5,1},{7,3},{8,12},{10,14},{12... | collective-permute-start | bytes 196616 | tf_op jit(solution)/shard_map/ppermute | solution.py:479
  32.0 4.3 %turned.1 = (bf16[512,512]{1,0:T(8,128)(2,1)S(1)}, bf16[512,512]{1,0:T(8,128)(2,1)S(1)}, bf16[1536,512]{1,0:T(8,128)(2,1)}, bf16[1536,512]{1,0:T(8,128)(2,1)}) custom-call(f32[32,8]{1,0:T(8,128)S(1)} %copy.26.cv_ref, f32[256,128]{1,0:T(8,128)S(1)} %get-tuple-element.21.ap_ref, f32[1024,128]{1,0:T(8,128)S(1)} %bitcast.56), custom_call_target="tpu_custom_call" | custom-call | flops 1000000000 | bytes 6291456 | tf_op jit(solution)/shard_map/turned/pallas_call | solution.py:369
  36.3 1.3 %all-to-all-done.all_ref = f32[8,256,128]{2,1,0:T(8,128)S(1)} async-done(((f32[8,256,128]{2,1,0:T(8,128)}), f32[8,256,128]{2,1,0:T(8,128)S(1)}, u32[]{:S(2)}, u32[]{:S(2)}) %all-to-all-start) | async-done | bytes 1048608 | tf_op jit(solution)/shard_map/all_to_all | solution.py:486
  37.6 5.5 %pair_fields.1 = (f32[768,128]{1,0:T(8,128)S(1)}, f32[768,128]{1,0:T(8,128)S(1)}) custom-call(s32[48]{0:T(128)S(1)} %get-tuple-element.37.source_ref, s32[48]{0:T(128)S(1)} %get-tuple-element.36.term_ref, s32[48]{0:T(128)S(1)} %get-tuple-element.35.valid_ref, f32[8,256,128]{2,1,0:T(8,128)S(1)} %all-to-all-done.all_ref, ...), custom_call_target="tpu_custom_call" | custom-call | flops 3000000000 | bytes 6291456 | tf_op jit(solution)/shard_map/pair_fields/pallas_call | solution.py:392
  43.2 4.4 %collective-permute-start.3 = (f32[768,128]{1,0:T(8,128)S(1)}, f32[768,128]{1,0:T(8,128)S(1)}, u32[]{:S(2)}, u32[]{:S(2)}) collective-permute-start(f32[768,128]{1,0:T(8,128)S(1)} %get-tuple-element.31), channel_id=1, source_target_pairs={{0,1},{1,0},{2,3},{3,2},{4,5},{5,4},{6,7},{7,6},{8,9},{9,8},{10,11... | collective-permute-start | bytes 1179656 | tf_op jit(solution)/shard_map/ppermute | solution.py:469
  47.6 1.3 %collective-permute-done.3.theirs_ref = f32[768,128]{1,0:T(8,128)S(1)} collective-permute-done((f32[768,128]{1,0:T(8,128)S(1)}, f32[768,128]{1,0:T(8,128)S(1)}, u32[]{:S(2)}, u32[]{:S(2)}) %collective-permute-start.3) | collective-permute-done | bytes 393248 | tf_op jit(solution)/shard_map/ppermute | solution.py:469
  49.0 0.8 %merge.1 = f32[896,128]{1,0:T(8,128)} custom-call(f32[768,128]{1,0:T(8,128)S(1)} %get-tuple-element.30.mine_ref, f32[768,128]{1,0:T(8,128)S(1)} %collective-permute-done.3.theirs_ref, f32[4,32,128]{2,1,0:T(8,128)S(1)} %bitcast_add_fusion.1.own_ref), custom_call_target="tpu_custom_call" | custom-call | tf_op jit(solution)/shard_map/merge/pallas_call | solution.py:430
  49.8 12.9 %all-to-all-start.1 = ((f32[32,1,3584]{2,1,0:T(1,128)}), f32[32,1,3584]{2,1,0:T(1,128)S(1)}, u32[]{:S(2)}, u32[]{:S(2)}) async-start(f32[32,1,3584]{2,1,0:T(1,128)} %bitcast.30), calls=%async_computation.1 | async-start | bytes 917504 | tf_op jit(solution)/shard_map/all_to_all | solution.py:498
  62.7 7.8 %pair_action.1 = f32[256,128]{1,0:T(8,128)} custom-call(s32[48]{0:T(128)S(1)} %get-tuple-element.37.source_ref, s32[48]{0:T(128)S(1)} %get-tuple-element.36.term_ref, s32[48]{0:T(128)S(1)} %get-tuple-element.35.valid_ref, f32[32,8]{1,0:T(8,128)S(1)} %copy.26.cv_ref, f32[8,256,128]{2,1,0:T(8,128)S(1)} %all-to-all-done.all_ref, f32[1024,128]{1,0:T(8,128)S(1)} %bitcast.57, ...), custom_call_target="tpu_custom_call" | custom-call | flops 3000000000 | bytes 4194304 | tf_op jit(solution)/shard_map/pair_action/pallas_call | solution.py:410
  70.4 7.7 %all-to-all-done.1 = f32[32,1,3584]{2,1,0:T(1,128)S(1)} async-done(((f32[32,1,3584]{2,1,0:T(1,128)}), f32[32,1,3584]{2,1,0:T(1,128)S(1)}, u32[]{:S(2)}, u32[]{:S(2)}) %all-to-all-start.1) | async-done | bytes 458784 | tf_op jit(solution)/shard_map/all_to_all | solution.py:498
  78.2 0.6 total.1
  (24 shorter events, 0.2 us)
Async XLA Ops:
  0.6 9.7 %copy-start.5 = (f32[1,32,8]{1,2,0:T(8,128)S(1)}, f32[1,32,8]{1,2,0:T(8,128)}, u32[]{:S(2)}) copy-start(f32[1,32,8]{1,2,0:T(8,128)} %param.11) | copy-start | bytes 3076
  0.6 0.9 %copy-start = (f32[1,8,4096]{2,1,0:T(8,128)S(1)}, f32[1,8,4096]{2,1,0:T(8,128)}, u32[]{:S(2)}) copy-start(f32[1,8,4096]{2,1,0:T(8,128)} %param.8) | copy-start | bytes 393220
  1.6 8.9 %copy-start.1 = (f32[1,32,4096]{2,1,0:T(8,128)S(1)}, f32[1,32,4096]{2,1,0:T(8,128)}, u32[]{:S(2)}) copy-start(f32[1,32,4096]{2,1,0:T(8,128)} %param.10) | copy-start | bytes 1572868
  1.6 8.9 %copy-start.2 = (f32[1,32,4096]{2,1,0:T(8,128)S(1)}, f32[1,32,4096]{2,1,0:T(8,128)}, u32[]{:S(2)}) copy-start(f32[1,32,4096]{2,1,0:T(8,128)} %param.9) | copy-start | bytes 1572868
  2.7 34.9 %all-to-all-start = ((f32[8,256,128]{2,1,0:T(8,128)}), f32[8,256,128]{2,1,0:T(8,128)S(1)}, u32[]{:S(2)}, u32[]{:S(2)}) async-start(f32[8,256,128]{2,1,0:T(8,128)} %get-tuple-element.19), calls=%async_computation | async-start | bytes 2097152 | tf_op jit(solution)/shard_map/all_to_all | solution.py:486
  10.4 10.9 %copy-start.7 = (s32[128,3]{0,1:T(4,128)S(1)}, s32[128,3]{0,1:T(4,128)}, u32[]{:S(2)}) copy-start(s32[128,3]{0,1:T(4,128)} %param.15) | copy-start | bytes 4612
  10.5 14.2 %copy-start.6 = (f32[32,8]{0,1:T(8,128)S(1)}, f32[32,8]{0,1:T(8,128)}, u32[]{:S(2)}) copy-start(f32[32,8]{0,1:T(8,128)} %param.14) | copy-start | bytes 3076
  16.5 15.5 %copy-start.3 = (f32[32,4096]{1,0:T(8,128)S(1)}, f32[32,4096]{1,0:T(8,128)}, u32[]{:S(2)}) copy-start(f32[32,4096]{1,0:T(8,128)} %param.13) | copy-start | bytes 1572868
  16.5 6.0 %collective-permute-start = (f32[512,128]{1,0:T(8,128)S(1)}, f32[512,128]{1,0:T(8,128)S(1)}, u32[]{:S(2)}, u32[]{:S(2)}) collective-permute-start(f32[512,128]{1,0:T(8,128)S(1)} %get-tuple-element.23), channel_id=1, source_target_pairs={{0,1},{1,0},{2,3},{3,2},{4,5},{5,4},{6,7},{7,6},{8,9},{9,8},{10,11... | collective-permute-start | bytes 786440 | tf_op jit(solution)/shard_map/ppermute | solution.py:469
  22.5 6.6 %collective-permute-start.1 = (f32[2,4,32,128]{3,2,1,0:T(8,128)S(1)}, f32[2,4,32,128]{3,2,1,0:T(8,128)S(1)}, u32[]{:S(2)}, u32[]{:S(2)}) collective-permute-start(f32[2,4,32,128]{3,2,1,0:T(8,128)S(1)} %dynamic-slice_bitcast_fusion), channel_id=1, source_target_pairs={{0,2},{2,0},{4,6},{6,4},{1,3},{3,1},{5,7},{7,5},{8,10},{10,8},{12,... | collective-permute-start | bytes 393224 | tf_op jit(solution)/shard_map/ppermute | solution.py:479
  29.2 7.2 %collective-permute-start.2 = (f32[4,32,128]{2,1,0:T(8,128)S(1)}, f32[4,32,128]{2,1,0:T(8,128)S(1)}, u32[]{:S(2)}, u32[]{:S(2)}) collective-permute-start(f32[4,32,128]{2,1,0:T(8,128)S(1)} %dynamic-slice_bitcast_fusion.1), channel_id=1, source_target_pairs={{0,4},{2,6},{4,0},{6,2},{1,5},{3,7},{5,1},{7,3},{8,12},{10,14},{12... | collective-permute-start | bytes 196616 | tf_op jit(solution)/shard_map/ppermute | solution.py:479
  43.2 19.5 %copy-start.4 = (f32[32,4096]{1,0:T(8,128)S(1)}, f32[32,4096]{1,0:T(8,128)}, u32[]{:S(2)}) copy-start(f32[32,4096]{1,0:T(8,128)} %param.12) | copy-start | bytes 1572868
  43.2 5.8 %collective-permute-start.3 = (f32[768,128]{1,0:T(8,128)S(1)}, f32[768,128]{1,0:T(8,128)S(1)}, u32[]{:S(2)}, u32[]{:S(2)}) collective-permute-start(f32[768,128]{1,0:T(8,128)S(1)} %get-tuple-element.31), channel_id=1, source_target_pairs={{0,1},{1,0},{2,3},{3,2},{4,5},{5,4},{6,7},{7,6},{8,9},{9,8},{10,11... | collective-permute-start | bytes 1179656 | tf_op jit(solution)/shard_map/ppermute | solution.py:469
  49.8 28.4 %all-to-all-start.1 = ((f32[32,1,3584]{2,1,0:T(1,128)}), f32[32,1,3584]{2,1,0:T(1,128)S(1)}, u32[]{:S(2)}, u32[]{:S(2)}) async-start(f32[32,1,3584]{2,1,0:T(1,128)} %bitcast.30), calls=%async_computation.1 | async-start | bytes 917504 | tf_op jit(solution)/shard_map/all_to_all | solution.py:498
